TPU v7x, 256 devices: a whole 4x4x8 slice. The times are simulated.
256 devices in a mesh: section: 16 (over z, x_hi), fsdp: 16 (over x_lo, y, core).
Axes of the slice: x: 4 (x_hi: 2, x_lo: 2; x = x_hi * 2 + x_lo), y: 4, z: 8, core: 2. Of those that a mesh axis runs over, the one named last changes fastest.
Arguments:
- x_fwd: bfloat16 [16, 384, 4096], P('section', None, 'fsdp'), may hold values from -6 to 6
- x_saved: bfloat16 [16, 384, 4096], P('section', None, 'fsdp'), may hold values from -6 to 6
- cotangent: bfloat16 [16, 384, 4096], P('section', None, 'fsdp'), may hold values from -6 to 6
- qkv_weight: bfloat16 [16, 4096, 3, 4096], P('section', None, None, 'fsdp')
- gain: float32 [16, 4096], P('section', 'fsdp'), may hold values from 0.1 to 1.9
- block_lists: int32 [8, 3, 2], replicated, may hold values from 0 to 2, as said below
- plan: int32 [16, 2], P('section'), may hold values from 0 to 7
Outputs:
- y_next: bfloat16 [16, 384, 4096], P('section', None, 'fsdp')
- dx_prev: bfloat16 [16, 384, 4096], P('section', None, 'fsdp')
- w_grad: bfloat16 [16, 4096, 3, 4096], P('section', None, None, 'fsdp')
- gain_grad: float32 [16, 4096], P('section', 'fsdp')
Inputs may be any that keep to these rules, and one draw needn't show every extreme that they name: block_lists[z, b, 0] = b; the 2 entries of a row are distinct.
All inputs are finite; a program needn't handle non-finite values.
Results may differ from a plain program's by a relative error of at most 0.024.
Values may be sent and summed in bfloat16 or wider, within the bound.
No kernel may reach another device: no remote copies, remote signals or barrier semaphores. Data moves between devices by JAX's collectives and lax.ppermute only.
A program may use at most 128 MiB of HBM per device.

v0:
```python
import math

import jax
import jax.numpy as jnp
from jax import lax
from jax.sharding import PartitionSpec as P

HD = 128
BLK = 128


EPS = 1e-05


def shifted(block, axis, distance):
    devices = range(lax.axis_size(axis))
    route = [((i - distance) % len(devices), i) for i in devices]
    return lax.ppermute(block, axis, route)


def attend(query, key_in, value, block_ids):
    tokens, feat_width = query.shape
    head_count = feat_width // HD
    block_count = tokens // BLK
    band_size = block_ids.shape[1]
    q_blocks = query.reshape(block_count, BLK, head_count, HD)
    k_rows = key_in.reshape(block_count, BLK, head_count, HD)[block_ids].reshape(
        block_count, band_size * BLK, head_count, HD
    )
    v_rows = value.reshape(block_count, BLK, head_count, HD)[block_ids].reshape(
        block_count, band_size * BLK, head_count, HD
    )
    scores = jnp.einsum("qthd,qshd->qhts", q_blocks, k_rows, preferred_element_type=jnp.float32) * (
        1.0 / math.sqrt(HD)
    )
    row_max = jnp.max(scores, axis=3, keepdims=True)
    expd = jnp.exp(scores - row_max)
    probs = expd / jnp.sum(expd, axis=3, keepdims=True)
    probs_low = probs.astype(jnp.bfloat16)
    output = jnp.einsum(
        "qhts,qshd->qthd", probs_low, v_rows, preferred_element_type=jnp.float32
    ).reshape(tokens, feat_width)
    return (output, (probs, probs_low, q_blocks, k_rows, v_rows))


def attend_back(upstream, block_ids, saved):
    probs, probs_low, q_blocks, k_rows, v_rows = saved
    block_count, block_len, head_count, head_size = q_blocks.shape
    band_size = block_ids.shape[1]
    tokens = block_count * block_len
    c_blocks = upstream.reshape(block_count, block_len, head_count, head_size)
    grad_vrows = jnp.einsum(
        "qhts,qthd->qshd", probs_low, c_blocks, preferred_element_type=jnp.float32
    )
    grad_p = jnp.einsum("qthd,qshd->qhts", c_blocks, v_rows, preferred_element_type=jnp.float32)
    grad_s = (
        probs * (grad_p - jnp.sum(probs * grad_p, axis=3, keepdims=True)) * (1.0 / math.sqrt(HD))
    )
    grad_s_low = grad_s.astype(jnp.bfloat16)
    grad_q = jnp.einsum("qhts,qshd->qthd", grad_s_low, k_rows, preferred_element_type=jnp.float32)
    grad_krows = jnp.einsum(
        "qhts,qthd->qshd", grad_s_low, q_blocks, preferred_element_type=jnp.float32
    )
    onehot = (
        block_ids[:, :, None] == jnp.arange(block_count, dtype=jnp.int32)[None, None, :]
    ).astype(jnp.float32)
    band_shape = (block_count, band_size, block_len, head_count, head_size)
    grad_k = jnp.einsum("qbk,qbthd->kthd", onehot, grad_krows.reshape(band_shape))
    grad_v = jnp.einsum("qbk,qbthd->kthd", onehot, grad_vrows.reshape(band_shape))
    return (grad_q.reshape(tokens, -1), grad_k.reshape(tokens, -1), grad_v.reshape(tokens, -1))


def on_device(x_fwd, x_saved, cotangent, qkv_weight, gain, block_lists, plan):
    forward_in = x_fwd[0]
    saved_in = x_saved[0]
    upstream = cotangent[0]
    weight = qkv_weight[0]
    gain_row = gain[0]
    full_width = weight.shape[0]
    local = weight.shape[2]
    tokens = forward_in.shape[0]
    w_flat = weight.reshape(full_width, 3 * local)
    lists_fwd = block_lists[plan[0, 0]]
    lists_bwd = block_lists[plan[0, 1]]
    wide_fwd = forward_in.astype(jnp.float32)
    wide_bwd = saved_in.astype(jnp.float32)
    scaled_fwd = (wide_fwd * gain_row[None, :]).astype(jnp.bfloat16)
    scaled_bwd = (wide_bwd * gain_row[None, :]).astype(jnp.bfloat16)
    sq_fwd, sq_bwd = lax.psum(
        (jnp.sum(wide_fwd * wide_fwd, axis=1), jnp.sum(wide_bwd * wide_bwd, axis=1)), "fsdp"
    )
    scale_fwd = lax.rsqrt(sq_fwd / full_width + EPS)
    scale_bwd = lax.rsqrt(sq_bwd / full_width + EPS)
    product_fwd = jnp.dot(
        lax.all_gather(scaled_fwd, "fsdp", axis=1, tiled=True),
        w_flat,
        preferred_element_type=jnp.float32,
    )
    whole_bwd = lax.all_gather(scaled_bwd, "fsdp", axis=1, tiled=True)
    product_bwd = jnp.dot(whole_bwd, w_flat, preferred_element_type=jnp.float32)
    proj_fwd = (scale_fwd[:, None] * product_fwd).astype(jnp.bfloat16)
    attn_fwd = attend(
        proj_fwd[:, :local], proj_fwd[:, local : 2 * local], proj_fwd[:, 2 * local :], lists_fwd
    )[0]
    result = (wide_fwd + attn_fwd).astype(jnp.bfloat16)
    sent_on = shifted(result[None], "section", 1)
    proj_bwd = (scale_bwd[:, None] * product_bwd).astype(jnp.bfloat16)
    saved = attend(
        proj_bwd[:, :local], proj_bwd[:, local : 2 * local], proj_bwd[:, 2 * local :], lists_bwd
    )[1]
    grad_q, grad_k, grad_v = attend_back(upstream, lists_bwd, saved)
    stacked = jnp.stack([grad_q, grad_k, grad_v], axis=1).reshape(tokens, 3 * local)
    grads = (scale_bwd[:, None] * stacked).astype(jnp.bfloat16)
    grad_w = lax.dot_general(
        whole_bwd, grads, (((0,), (0,)), ((), ())), preferred_element_type=jnp.float32
    )
    grad_w = grad_w.astype(jnp.bfloat16).reshape(1, full_width, 3, local)
    partial_in = lax.dot_general(
        grads, w_flat, (((1,), (1,)), ((), ())), preferred_element_type=jnp.float32
    )
    summed_in = lax.psum(partial_in.astype(jnp.bfloat16), "fsdp").astype(jnp.float32)
    own_in = lax.dynamic_slice_in_dim(summed_in, lax.axis_index("fsdp") * local, local, 1)
    row_total = jnp.sum(whole_bwd.astype(jnp.float32) * summed_in, axis=1)
    grad_x = upstream.astype(jnp.float32) + gain_row[None, :] * own_in
    grad_x = grad_x - (scale_bwd * scale_bwd * row_total / full_width)[:, None] * wide_bwd
    sent_back = shifted(grad_x.astype(jnp.bfloat16)[None], "section", -1)
    grad_gain = jnp.sum(wide_bwd * own_in, axis=0)[None]
    return (sent_on, sent_back, grad_w, grad_gain)


def solution(mesh):
    in_specs = (
        P("section", None, "fsdp"),
        P("section", None, "fsdp"),
        P("section", None, "fsdp"),
        P("section", None, None, "fsdp"),
        P("section", "fsdp"),
        P(),
        P("section", None),
    )
    out_specs = (
        P("section", None, "fsdp"),
        P("section", None, "fsdp"),
        P("section", None, None, "fsdp"),
        P("section", "fsdp"),
    )
    return jax.shard_map(
        on_device, mesh=mesh, in_specs=in_specs, out_specs=out_specs, check_vma=False
    )
```

profile of v0, /device:TPU:8, one launch (start us, length us, event | category | flops | bytes accessed | tf_op | source)
XLA Modules:
  0.0 271.1 jit_solution(14417627607529717031)
XLA Ops:
  7.2 1.9 fusion.21
  9.1 0.7 all-gather.3.cloned.1.call-update
  9.9 1.3 fusion.70
  13.7 8.7 %copy.55 = bf16[1,4096,3,256]{1,3,2,0:T(8,128)(2,1)} copy(bf16[1,4096,3,256]{3,1,2,0:T(8,128)(2,1)} %param.10) | data formatting | bytes 12582912 | tf_op args[3]
  23.6 0.1 constant_dynamic-slice_fusion
  23.7 0.1 copy.66
  23.8 0.1 copy.56
  23.9 0.1 copy.67
  24.0 0.1 reshape.185
  24.1 26.6 %all-reduce = (f32[384]{0:T(512)S(1)}, f32[384]{0:T(512)S(1)}) all-reduce(f32[384]{0:T(512)S(1)} %get-tuple-element.28, f32[384]{0:T(512)S(1)} %get-tuple-element.32), channel_id=1, replica_groups=mesh['section'=16,'fsdp'=16] {'fsdp'}, use_global_device_ids=true, to_apply=%region_1.0 | all-reduce | flops 768 | bytes 6144 | tf_op jit(solution)/shard_map/psum | solution.py:89
  50.7 6.3 %all-gather.5.cloned.1.call-done = bf16[384,4096]{1,0:T(8,128)(2,1)} async-done(((bf16[384,256]{1,0:T(8,128)(2,1)}), bf16[384,4096]{1,0:T(8,128)(2,1)}) %all-gather.5.cloned.1.call-update) | async-done | bytes 3145744 | tf_op jit(solution)/shard_map/all_gather | solution.py:99
  57.0 6.4 %fusion.6 = bf16[384,768]{1,0:T(8,128)(2,1)S(1)} fusion(bf16[384,4096]{1,0:T(8,128)(2,1)} %all-gather.5.cloned.1.call-done, bf16[4096,768]{0,1:T(8,128)(2,1)} %bitcast.81, f32[384]{0:T(512)S(1)} %add_rsqrt_fusion), kind=kOutput, calls=%fused_computation.15 | convolution fusion | flops 2416508928 | bytes 10028544 | tf_op jit(solution)/shard_map/dot_general | solution.py:100
  63.4 0.1 reshape.158
  63.5 0.6 gather_fusion.3
  64.2 0.1 reshape.155
  64.3 0.6 gather_fusion.2
  65.0 0.1 reshape.157
  65.0 0.2 copy.80
  65.2 0.3 convolution_bitcast_fusion.1
  65.5 1.3 fusion.76
  66.8 5.9 %convolution_bitcast_fusion.4 = f32[3,128,2,128]{1,3,2,0:T(8,128)S(1)} fusion(f32[3,2,128,256]{3,2,1,0:T(8,128)S(1)} %convolution_bitcast_fusion.1, bf16[3,256,2,128]{3,1,0,2:T(8,128)(2,1)S(1)} %bitcast.91, f32[3,2,128,256]{3,2,1,0:T(8,128)} %get-tuple-element.37, f32[3,2,128]{2,1,0:T(2,128)S(1)} %get-tuple-element.36), kind=kOutput, calls=%fused_computation.28 | convolution fusion | flops 51708928 | bytes 2362368 | tf_op jit(solution)/shard_map/qhts,qshd->qthd/dot_general | solution.py:60
  72.7 0.2 copy.78
  72.9 0.3 stack_reshape.9
  73.2 5.4 %convolution_bitcast_fusion = bf16[3,256,2,128]{1,3,2,0:T(8,128)(2,1)S(1)} fusion(bf16[3,128,2,128]{1,3,2,0:T(8,128)(2,1)S(1)} %copy.80, f32[3,2,128,256]{3,2,1,0:T(8,128)S(1)} %convolution_bitcast_fusion.1, f32[3,2,128,256]{3,2,1,0:T(8,128)} %get-tuple-element.37, f32[3,2,128]{2,1,0:T(2,128)S(1)} %get-tuple-element.36), kind=kOutput, calls=%fused_computation.21 | convolution fusion | flops 51708928 | bytes 2165760 | tf_op jit(solution)/shard_map/qhts,qthd->qshd/dot_general | solution.py:61
  78.6 0.1 reshape.160
  78.7 0.7 copy.81
  79.4 0.5 convolution_bitcast_fusion.3
  79.9 0.2 copy.82
  80.1 0.3 stack_reshape.10
  80.5 1.7 fusion.32
  82.2 0.6 convolution_bitcast_fusion.2
  82.8 0.2 copy.86
  83.0 0.3 stack_reshape.11
  83.4 0.1 multiply_convert_fusion.1
  83.6 0.3 copy.87
  83.9 7.2 %convolution_convert_fusion.1 = bf16[384,4096]{1,0:T(8,128)(2,1)} fusion(bf16[384,768]{0,1:T(8,128)(2,1)S(1)} %bitcast.86, bf16[4096,768]{0,1:T(8,128)(2,1)} %bitcast.82), kind=kOutput, calls=%fused_computation.9 | convolution fusion | flops 2417491968 | bytes 10027008 | tf_op jit(solution)/shard_map/dot_general | solution.py:118
  91.1 0.1 copy.57
  91.2 0.1 reshape.169
  91.3 0.4 copy.88
  91.7 11.3 %all-gather.3.cloned.1.call-done = bf16[384,4096]{1,0:T(8,128)(2,1)} async-done(((bf16[384,256]{1,0:T(8,128)(2,1)}), bf16[384,4096]{1,0:T(8,128)(2,1)}) %all-gather.3.cloned.1.call-update) | async-done | bytes 3145744 | tf_op jit(solution)/shard_map/all_gather | solution.py:95
  103.0 6.4 %fusion.5 = bf16[384,768]{1,0:T(8,128)(2,1)S(1)} fusion(bf16[384,4096]{1,0:T(8,128)(2,1)} %all-gather.3.cloned.1.call-done, bf16[4096,768]{0,1:T(8,128)(2,1)} %bitcast.83, f32[384]{0:T(512)S(1)} %add_rsqrt_fusion.1), kind=kOutput, calls=%fused_computation.14 | convolution fusion | flops 2416508928 | bytes 10028544 | tf_op jit(solution)/shard_map/dot_general | solution.py:94
  109.5 0.1 reshape.149
  109.6 0.6 gather_fusion
  110.2 0.8 copy.59
  111.1 0.6 gather_fusion.1
  111.7 0.1 reshape.151
  111.8 0.5 fusion.71
  112.3 0.3 convolution_multiply_fusion.3
  112.6 0.2 copy-done.5
  112.7 1.6 convolution_bitcast_fusion.5
  114.4 0.2 copy.65
  114.6 0.3 reshape.154
  115.0 3.4 %collective-permute-start = (bf16[1,384,256]{2,1,0:T(8,128)(2,1)S(1)}, bf16[1,384,256]{2,1,0:T(8,128)(2,1)S(1)}, u32[]{:S(2)}, u32[]{:S(2)}) collective-permute-start(bf16[1,384,256]{2,1,0:T(8,128)(2,1)S(1)} %fusion.23), channel_id=1, source_target_pairs={{240,0},{0,16},{16,32},{32,48},{48,64},{64,80},{80,96},{96,112},{1... | collective-permute-start | bytes 589832 | tf_op jit(solution)/shard_map/ppermute | solution.py:18
  118.4 0.4 copy.89
  118.7 119.3 %all-reduce.3.cloned.1.call-done = bf16[384,4096]{1,0:T(8,128)(2,1)} async-done(((bf16[384,4096]{1,0:T(8,128)(2,1)}), bf16[384,4096]{1,0:T(8,128)(2,1)}) %all-reduce.3.cloned.1.call-update) | async-done | bytes 3145744 | tf_op jit(solution)/shard_map/psum | solution.py:121
  238.0 3.9 %multiply_reduce_fusion = f32[384]{0:T(512)S(1)} fusion(bf16[384,4096]{1,0:T(8,128)(2,1)} %all-gather.5.cloned.1.call-done, bf16[384,4096]{1,0:T(8,128)(2,1)} %all-reduce.3.cloned.1.call-done), kind=kLoop, calls=%fused_computation.8 | loop fusion | flops 6291072 | bytes 6292992 | tf_op jit(solution)/shard_map/reduce_sum | solution.py:123
  241.9 0.8 convert_element_type.94
  242.7 0.1 copy-done.3
  242.8 0.7 fusion.28
  243.5 5.5 %collective-permute-start.1 = (bf16[1,384,256]{2,1,0:T(8,128)(2,1)S(1)}, bf16[1,384,256]{2,1,0:T(8,128)(2,1)S(1)}, u32[]{:S(2)}, u32[]{:S(2)}) collective-permute-start(bf16[1,384,256]{2,1,0:T(8,128)(2,1)S(1)} %get-tuple-element.19), channel_id=1, source_target_pairs={{16,0},{32,16},{48,32},{64,48},{80,64},{96,80},{112,96},{128,112},... | collective-permute-start | bytes 589832 | tf_op jit(solution)/shard_map/ppermute | solution.py:18
  249.0 5.6 %convolution_convert_fusion = bf16[4096,768]{0,1:T(8,128)(2,1)} fusion(bf16[384,4096]{1,0:T(8,128)(2,1)S(1)} %copy-done.1, f32[384,768]{1,0:T(8,128)S(1)} %copy.89, f32[384]{0:T(512)S(1)} %add_rsqrt_fusion), kind=kOutput, calls=%fused_computation.7 | convolution fusion | flops 2419654656 | bytes 10618368 | tf_op jit(solution)/shard_map/dot_general | solution.py:114
  254.6 8.6 %copy.90 = bf16[1,4096,3,256]{3,1,2,0:T(8,128)(2,1)} copy(bf16[1,4096,3,256]{1,3,2,0:T(8,128)(2,1)} %bitcast.84) | data formatting | bytes 12582912
  263.2 0.7 copy.141
  263.9 0.7 copy.142
  (42 shorter events, 0.7 us)
Async XLA Ops:
  7.2 49.8 %all-gather.5.cloned.1.call-start = ((), (), s32[]{:S(2)}) async-start(), calls=%async_computation.1 | async-start | bytes 3342336 | tf_op jit(solution)/shard_map/all_gather | solution.py:99
  9.1 93.9 %all-gather.3.cloned.1.call-start = ((), (), s32[]{:S(2)}) async-start(), calls=%async_computation | async-start | bytes 3342336 | tf_op jit(solution)/shard_map/all_gather | solution.py:95
  9.8 228.2 %all-reduce.3.cloned.1.call-start = ((), (), s32[]{:S(2)}) async-start(), calls=%async_computation.2 | async-start | bytes 6291456 | tf_op jit(solution)/shard_map/psum | solution.py:121
  13.6 9.9 %copy-start.6 = (s32[8,3,2]{0,2,1:T(2,128)S(1)}, s32[8,3,2]{0,2,1:T(2,128)}, u32[]{:S(2)}) copy-start(s32[8,3,2]{0,2,1:T(2,128)} %param.12) | copy-start | bytes 580
  13.7 10.4 %copy-start.2 = (bf16[1,384,256]{2,1,0:T(8,128)(2,1)S(1)}, bf16[1,384,256]{2,1,0:T(8,128)(2,1)}, u32[]{:S(2)}) copy-start(bf16[1,384,256]{2,1,0:T(8,128)(2,1)} %param.9) | copy-start | bytes 589828
  111.7 1.0 copy-start.5
  112.3 2.6 copy-start.4
  115.0 148.2 %collective-permute-start = (bf16[1,384,256]{2,1,0:T(8,128)(2,1)S(1)}, bf16[1,384,256]{2,1,0:T(8,128)(2,1)S(1)}, u32[]{:S(2)}, u32[]{:S(2)}) collective-permute-start(bf16[1,384,256]{2,1,0:T(8,128)(2,1)S(1)} %fusion.23), channel_id=1, source_target_pairs={{240,0},{0,16},{16,32},{32,48},{48,64},{64,80},{80,96},{96,112},{1... | collective-permute-start | bytes 589832 | tf_op jit(solution)/shard_map/ppermute | solution.py:18
  238.0 3.9 %copy-start = (bf16[384,4096]{1,0:T(8,128)(2,1)S(1)}, bf16[384,4096]{1,0:T(8,128)(2,1)}, u32[]{:S(2)}) copy-start(bf16[384,4096]{1,0:T(8,128)(2,1)} %all-reduce.3.cloned.1.call-done) | copy-start | bytes 9437188
  241.9 0.9 copy-start.3
  241.9 0.9 copy-start.7
  241.9 7.1 %copy-start.1 = (bf16[384,4096]{1,0:T(8,128)(2,1)S(1)}, bf16[384,4096]{1,0:T(8,128)(2,1)}, u32[]{:S(2)}) copy-start(bf16[384,4096]{1,0:T(8,128)(2,1)} %all-gather.5.cloned.1.call-done) | copy-start | bytes 9437188
  243.5 19.6 %collective-permute-start.1 = (bf16[1,384,256]{2,1,0:T(8,128)(2,1)S(1)}, bf16[1,384,256]{2,1,0:T(8,128)(2,1)S(1)}, u32[]{:S(2)}, u32[]{:S(2)}) collective-permute-start(bf16[1,384,256]{2,1,0:T(8,128)(2,1)S(1)} %get-tuple-element.19), channel_id=1, source_target_pairs={{16,0},{32,16},{48,32},{64,48},{80,64},{96,80},{112,96},{128,112},... | collective-permute-start | bytes 589832 | tf_op jit(solution)/shard_map/ppermute | solution.py:18
Sparse Core Ops, SparseCore 0:
  10.3 46.6 all-gather.4
  59.3 43.6 all-gather.2
  105.7 132.2 all-reduce.2
where the time goes:
time: 276 us; the launch traced here: 271 us
  waiting for transfers between devices  138 us (50%)
  matrix products  43.6 us (16%)
  local copies, waits for them, and re-layouts  29 us (11%)
  blocking collectives  26.6 us (10%)
  between operations  17.8 us (6%)
  starting transfers between devices  8.97 us (3%)
  other arithmetic  7.41 us (3%)
    psum x1, waiting for transfers between devices, on_device(): lax.psum(partial_in.astype(jnp.bfloat16), 'fsdp').astype(jnp.float32)  119 us
    psum x1, blocking collectives, on_device(): lax.psum((jnp.sum(wide_fwd * wide_fwd, axis=1), jnp.sum(wide_bwd * wide_b...  26.6 us
    unnamed x22, local copies, waits for them, and re-layouts  19 us
    all_gather x1, waiting for transfers between devices, on_device(): lax.all_gather(scaled_fwd, 'fsdp', axis=1, tiled=True)  11.3 us
    ppermute x2, starting transfers between devices, shifted(): return lax.ppermute(block, axis, route)  8.85 us
    dot_general x1, matrix products, on_device(): lax.dot_general(grads, w_flat, (((1,), (1,)), ((), ())), preferred_elemen...  7.2 us
    dot_general x1, matrix products, on_device(): jnp.dot(lax.all_gather(scaled_fwd, 'fsdp', axis=1, tiled=True), w_flat, p...  6.38 us
    dot_general x1, matrix products, on_device(): product_bwd = jnp.dot(whole_bwd, w_flat, preferred_element_type=jnp.float32)  6.38 us
  transfers between devices with their start and end apart: 5, of which 3 were waited for; matrix products, arithmetic and copies ran while one was open for 28% of the time, Pallas kernels for 0%

commit v1 on v0

v1 whole, which is shorter than its diff:
```python
import math

import jax
import jax.numpy as jnp
from jax import lax
from jax.experimental import pallas as pl
from jax.experimental.pallas import tpu as pltpu
from jax.sharding import PartitionSpec as P

HD = 128
BLK = 128
EPS = 1e-05
STAT = 16
CHIPS = 8
F32 = jnp.float32
BF16 = jnp.bfloat16
VMEM_BYTES = 40 << 20


def pieces(row):
    high = row.astype(BF16).astype(F32)
    rest = row - high
    mid = rest.astype(BF16).astype(F32)
    return high, mid, rest - mid


def stat_rows(row, width):
    span = row.shape[1]
    index = lax.broadcasted_iota(jnp.int32, (STAT, width), 0)
    out = jnp.zeros((STAT, width), F32)
    for i, part in enumerate(pieces(row)):
        for j, start in enumerate(range(0, span, width)):
            held = part[:, start : start + width]
            if held.shape[1] < width:
                held = jnp.concatenate(
                    [held, jnp.zeros((1, width - held.shape[1]), F32)], axis=1
                )
            out = jnp.where(index == 3 * j + i, jnp.broadcast_to(held, (STAT, width)), out)
    return out.astype(BF16)


def stat_row(rows, span):
    width = rows.shape[1]
    parts = []
    for j, start in enumerate(range(0, span, width)):
        part = rows[3 * j : 3 * j + 1] + rows[3 * j + 1 : 3 * j + 2] + rows[3 * j + 2 : 3 * j + 3]
        parts.append(part[:, : min(width, span - start)])
    return parts[0] if len(parts) == 1 else jnp.concatenate(parts, axis=1)


def as_column(row):
    return jnp.transpose(jnp.broadcast_to(row, (HD, row.shape[1])))


def row_sums(folded):
    return jnp.sum(jnp.transpose(folded), axis=0, keepdims=True)


def pack_kernel(x_ref, gain_ref, out_ref):
    tokens = x_ref.shape[0]
    wide = x_ref[...].astype(F32)
    out_ref[:tokens, :] = (wide * gain_ref[...]).astype(BF16)
    squares = wide * wide
    folded = squares[:, :HD]
    for start in range(HD, squares.shape[1], HD):
        folded = folded + squares[:, start : start + HD]
    out_ref[tokens:, :] = stat_rows(row_sums(folded), out_ref.shape[1])


def block_mask(ints_ref, which, b, tokens):
    z = ints_ref[48 + which]
    column = lax.shift_right_logical(
        lax.broadcasted_iota(jnp.int32, (BLK, tokens), 1), BLK.bit_length() - 1
    )
    first = ints_ref[z * 6 + b * 2]
    second = ints_ref[z * 6 + b * 2 + 1]
    return (column == first) | (column == second)


def probabilities(query, key_in, mask):
    scores = lax.dot_general(
        query, key_in, (((1,), (1,)), ((), ())), preferred_element_type=F32
    ) * (1.0 / math.sqrt(HD))
    scores = jnp.where(mask, scores, -1e30)
    expd = jnp.exp(scores - jnp.max(scores, axis=1, keepdims=True))
    return expd / jnp.sum(expd, axis=1, keepdims=True)


def accumulate(mine_ref, other_ref, w_refs, acc_ref, stat_ref, tokens):
    step = pl.program_id(0)
    pairs = mine_ref.shape[0]
    local = mine_ref.shape[2]
    x_all = jnp.concatenate(
        [ref[i, :tokens, :] for i in range(pairs) for ref in (mine_ref, other_ref)], axis=1
    )
    stats = sum(
        ref[i, tokens:, :].astype(F32) for i in range(pairs) for ref in (mine_ref, other_ref)
    )
    for j in range(3):
        w_all = jnp.concatenate([ref[j] for ref in w_refs], axis=0)
        part = jnp.dot(x_all, w_all, preferred_element_type=F32)
        cols = slice(j * local, (j + 1) * local)

        @pl.when(step == 0)
        def _():
            acc_ref[:, cols] = part

        @pl.when(step > 0)
        def _():
            acc_ref[:, cols] += part

    @pl.when(step == 0)
    def _():
        stat_ref[...] = stats

    @pl.when(step > 0)
    def _():
        stat_ref[...] += stats


def row_scale(stat_ref, tokens, width):
    return lax.rsqrt(as_column(stat_row(stat_ref[...], tokens)) / width + EPS)


def project(acc_ref, scale, proj_ref):
    for start in range(0, acc_ref.shape[1], HD):
        proj_ref[:, start : start + HD] = (scale * acc_ref[:, start : start + HD]).astype(BF16)


def forward_kernel(ints_ref, mine_ref, other_ref, *refs):
    w_refs, (x_ref, out_ref, acc_ref, stat_ref, proj_ref) = refs[:-5], refs[-5:]
    tokens, local = x_ref.shape
    accumulate(mine_ref, other_ref, w_refs, acc_ref, stat_ref, tokens)

    @pl.when(pl.program_id(0) == pl.num_programs(0) - 1)
    def _():
        scale = row_scale(stat_ref, tokens, 2 * CHIPS * local)
        project(acc_ref, scale, proj_ref)
        for h in range(local // HD):
            at = h * HD
            key_in = proj_ref[:, local + at : local + at + HD]
            value = proj_ref[:, 2 * local + at : 2 * local + at + HD]
            for b in range(tokens // BLK):
                rows = slice(b * BLK, (b + 1) * BLK)
                probs = probabilities(
                    proj_ref[rows, at : at + HD], key_in, block_mask(ints_ref, 0, b, tokens)
                )
                attn = jnp.dot(probs.astype(BF16), value, preferred_element_type=F32)
                out_ref[rows, at : at + HD] = (
                    x_ref[rows, at : at + HD].astype(F32) + attn
                ).astype(BF16)


def backward_kernel(ints_ref, mine_ref, other_ref, *refs):
    w_refs = refs[:-8]
    c_ref, out_ref, scale_ref, acc_ref, stat_ref, proj_ref, p_ref, s_ref = refs[-8:]
    tokens, local = c_ref.shape
    accumulate(mine_ref, other_ref, w_refs, acc_ref, stat_ref, tokens)

    @pl.when(pl.program_id(0) == pl.num_programs(0) - 1)
    def _():
        scale = row_scale(stat_ref, tokens, 2 * CHIPS * local)
        scale_ref[...] = scale
        project(acc_ref, scale, proj_ref)
        over_tokens = (((0,), (0,)), ((), ()))
        folded = jnp.zeros((tokens, HD), F32)
        for h in range(local // HD):
            at = h * HD
            query = proj_ref[:, at : at + HD]
            key_in = proj_ref[:, local + at : local + at + HD]
            value = proj_ref[:, 2 * local + at : 2 * local + at + HD]
            upstream = c_ref[:, at : at + HD]
            for b in range(tokens // BLK):
                rows = slice(b * BLK, (b + 1) * BLK)
                probs = probabilities(query[rows], key_in, block_mask(ints_ref, 1, b, tokens))
                grad_p = lax.dot_general(
                    upstream[rows], value, (((1,), (1,)), ((), ())), preferred_element_type=F32
                )
                inner = jnp.sum(probs * grad_p, axis=1, keepdims=True)
                p_ref[rows, :] = probs.astype(BF16)
                s_ref[rows, :] = (probs * (grad_p - inner) * (1.0 / math.sqrt(HD))).astype(BF16)
            grad_s = s_ref[...]
            parts = (
                jnp.dot(grad_s, key_in, preferred_element_type=F32),
                lax.dot_general(grad_s, query, over_tokens, preferred_element_type=F32),
                lax.dot_general(p_ref[...], upstream, over_tokens, preferred_element_type=F32),
            )
            for j, part in enumerate(parts):
                cols = slice(j * local + at, j * local + at + HD)
                grads = (scale * part).astype(BF16)
                out_ref[:tokens, cols] = grads
                folded = folded + grads.astype(F32) * acc_ref[:, cols]
        out_ref[tokens:, :] = stat_rows(row_sums(folded), out_ref.shape[1])


def weight_specs(pairs, local, part):
    def spec(i, side):
        return pl.BlockSpec((3, local, local), lambda d, ints: (0, ints[part + side * 8 + d * pairs + i], 0))

    return [spec(i, side) for i in range(pairs) for side in range(2)]


def attention_call(kernel, ints, mine, other, weight, extra, out_shapes, scratch, pairs, name):
    chips, rows, local = mine.shape
    whole = lambda shape: pl.BlockSpec(shape, lambda d, ints: (0,) * len(shape))
    blocks = pl.BlockSpec((pairs, rows, local), lambda d, ints: (d, 0, 0))
    tokens = extra.shape[0]
    specs = weight_specs(pairs, local, 50)
    return pl.pallas_call(
        kernel,
        out_shape=out_shapes,
        grid_spec=pltpu.PrefetchScalarGridSpec(
            num_scalar_prefetch=1,
            grid=(chips // pairs,),
            in_specs=[blocks, blocks, *specs, whole(extra.shape)],
            out_specs=jax.tree.map(lambda s: whole(s.shape), out_shapes),
            scratch_shapes=[
                pltpu.VMEM((tokens, 3 * local), F32),
                pltpu.VMEM((STAT, local), F32),
                pltpu.VMEM((tokens, 3 * local), BF16),
                *scratch,
            ],
        ),
        compiler_params=pltpu.CompilerParams(vmem_limit_bytes=VMEM_BYTES),
        name=name,
    )(ints, mine, other, *([weight] * len(specs)), extra)


def input_grad_kernel(ints_ref, mine_ref, other_ref, w_mine_ref, w_other_ref, *out_refs):
    tokens = mine_ref.shape[0] - STAT
    local = out_refs[0].shape[1]
    step = pl.program_id(0)
    grads = jnp.concatenate([mine_ref[:tokens, :], other_ref[:tokens, :]], axis=1)
    w_all = jnp.concatenate([ref[j] for ref in (w_mine_ref, w_other_ref) for j in range(3)], axis=1)
    part = lax.dot_general(
        grads, w_all, (((1,), (1,)), ((), ())), preferred_element_type=F32
    ).astype(BF16)
    totals = stat_row(mine_ref[tokens:, :].astype(F32) + other_ref[tokens:, :].astype(F32), tokens)
    stats = stat_rows(totals, local)
    for i, ref in enumerate(out_refs):

        @pl.when(step == i)
        def _():
            ref[:tokens, :] = part
            ref[tokens:, :] = stats


def input_grad(ints, mine, other, weight, w_other, first, count, name):
    rows = mine.shape[0]
    local = weight.shape[2]
    whole = lambda shape: pl.BlockSpec(shape, lambda d, ints: (0,) * len(shape))
    w_spec = pl.BlockSpec((3, local, local), lambda d, ints: (0, ints[50 + first + d], 0))
    return pl.pallas_call(
        input_grad_kernel,
        out_shape=[jax.ShapeDtypeStruct((rows, local), BF16)] * count,
        grid_spec=pltpu.PrefetchScalarGridSpec(
            num_scalar_prefetch=1,
            grid=(count,),
            in_specs=[whole(mine.shape), whole(other.shape), w_spec, w_spec],
            out_specs=[whole((rows, local))] * count,
        ),
        compiler_params=pltpu.CompilerParams(vmem_limit_bytes=VMEM_BYTES),
        name=name,
    )(ints, mine, other, weight, w_other)


def weight_grad_kernel(ints_ref, mine_ref, other_ref, g_ref, out_ref):
    tokens = g_ref.shape[0] - STAT
    local = mine_ref.shape[2]
    side = ints_ref[66]
    grads = g_ref[:tokens, :]
    for ref, at in ((mine_ref, side), (other_ref, 1 - side)):
        part = lax.dot_general(
            ref[0, :tokens, :], grads, (((0,), (0,)), ((), ())), preferred_element_type=F32
        )
        for j in range(3):
            out_ref[j, pl.ds(pl.multiple_of(at * local, local), local), :] = part[
                :, j * local : (j + 1) * local
            ].astype(BF16)


def weight_grad(ints, mine, other, grads):
    chips, rows, local = mine.shape
    blocks = pl.BlockSpec((1, rows, local), lambda d, ints: (d, 0, 0))
    return pl.pallas_call(
        weight_grad_kernel,
        out_shape=jax.ShapeDtypeStruct((3, 2 * chips * local, local), BF16),
        grid_spec=pltpu.PrefetchScalarGridSpec(
            num_scalar_prefetch=1,
            grid=(chips,),
            in_specs=[blocks, blocks, pl.BlockSpec(grads.shape, lambda d, ints: (0, 0))],
            out_specs=pl.BlockSpec((3, 2 * local, local), lambda d, ints: (0, ints[67 + d], 0)),
        ),
        compiler_params=pltpu.CompilerParams(vmem_limit_bytes=VMEM_BYTES),
        name="weight_grad",
    )(ints, mine, other, grads)


def finish_kernel(*refs):
    blocks, (x_ref, c_ref, gain_ref, scale_ref, dx_ref, gg_ref) = refs[:CHIPS], refs[CHIPS:]
    tokens, local = x_ref.shape
    own_in = blocks[0][:tokens, :].astype(F32)
    stats = blocks[0][tokens:, :].astype(F32)
    for ref in blocks[1:]:
        own_in = own_in + ref[:tokens, :].astype(F32)
        stats = stats + ref[tokens:, :].astype(F32)
    total = as_column(stat_row(stats, tokens))
    scale = scale_ref[...]
    factor = scale * scale * total / (2 * CHIPS * local)
    x_wide = x_ref[...].astype(F32)
    for start in range(0, local, HD):
        cols = slice(start, start + HD)
        grad_x = c_ref[:, cols].astype(F32) + gain_ref[:, cols] * own_in[:, cols]
        dx_ref[:, cols] = (grad_x - factor * x_wide[:, cols]).astype(BF16)
    gg_ref[...] = jnp.sum(x_wide * own_in, axis=0, keepdims=True)


def plain_call(kernel, out_shape, name, *args):
    return pl.pallas_call(
        kernel,
        out_shape=out_shape,
        compiler_params=pltpu.CompilerParams(vmem_limit_bytes=VMEM_BYTES),
        name=name,
    )(*args)


def to_chip(block, distance):
    route = [(i, ((i >> 1) ^ distance) << 1 | (i & 1)) for i in range(2 * CHIPS)]
    return lax.ppermute(block, "fsdp", route)


def to_core(block):
    return lax.ppermute(block, "fsdp", [(i, i ^ 1) for i in range(2 * CHIPS)])


def shifted(block, axis, distance):
    count = lax.axis_size(axis)
    return lax.ppermute(block, axis, [((i - distance) % count, i) for i in range(count)])


def gathered(block):
    return jnp.stack([block] + [to_chip(block, d) for d in range(1, CHIPS)])


def on_device(x_fwd, x_saved, cotangent, qkv_weight, gain, block_lists, plan):
    forward_in = x_fwd[0]
    saved_in = x_saved[0]
    upstream = cotangent[0]
    weight = jnp.transpose(qkv_weight[0], (1, 0, 2))
    tokens, local = forward_in.shape
    me = lax.axis_index("fsdp").astype(jnp.int32)
    chip, side = me // 2, me % 2
    apart = jnp.arange(CHIPS, dtype=jnp.int32) ^ chip
    ints = jnp.concatenate(
        [
            block_lists.reshape(-1),
            plan.reshape(-1),
            apart * 2 + side,
            apart * 2 + 1 - side,
            side[None],
            apart,
        ]
    )
    packed = jax.ShapeDtypeStruct((tokens + STAT, local), BF16)
    pay_bwd = plain_call(pack_kernel, packed, "pack_bwd", saved_in, gain)
    pay_fwd = plain_call(pack_kernel, packed, "pack_fwd", forward_in, gain)
    w_other = to_core(weight)

    mine_bwd = gathered(pay_bwd)
    mine_bwd, pay_fwd, w_other = lax.optimization_barrier((mine_bwd, pay_fwd, w_other))
    other_bwd = to_core(mine_bwd)
    grads, scale = attention_call(
        backward_kernel,
        ints,
        mine_bwd,
        other_bwd,
        weight,
        upstream,
        (
            jax.ShapeDtypeStruct((tokens + STAT, 3 * local), BF16),
            jax.ShapeDtypeStruct((tokens, HD), F32),
        ),
        [pltpu.VMEM((tokens, tokens), BF16), pltpu.VMEM((tokens, tokens), BF16)],
        2,
        "backward",
    )
    grads_other = to_core(grads)
    blocks = input_grad(ints, grads, grads_other, weight, w_other, 0, CHIPS, "input_grad")
    blocks = [blocks[0]] + [to_chip(blocks[d], d) for d in range(1, CHIPS)]

    mine_fwd = gathered(pay_fwd)
    other_fwd = to_core(mine_fwd)
    result = attention_call(
        forward_kernel,
        ints,
        mine_fwd,
        other_fwd,
        weight,
        forward_in,
        jax.ShapeDtypeStruct((tokens, local), BF16),
        [],
        2,
        "forward",
    )
    sent_on = shifted(result, "section", 1)
    grad_w = weight_grad(ints, mine_bwd, other_bwd, grads)
    grad_x, grad_gain = plain_call(
        finish_kernel,
        (
            jax.ShapeDtypeStruct((tokens, local), BF16),
            jax.ShapeDtypeStruct((1, local), F32),
        ),
        "finish",
        *blocks,
        saved_in,
        upstream,
        gain,
        scale,
    )
    sent_back = shifted(grad_x, "section", -1)
    return (sent_on[None], sent_back[None], jnp.transpose(grad_w, (1, 0, 2))[None], grad_gain)


def solution(mesh):
    in_specs = (
        P("section", None, "fsdp"),
        P("section", None, "fsdp"),
        P("section", None, "fsdp"),
        P("section", None, None, "fsdp"),
        P("section", "fsdp"),
        P(),
        P("section", None),
    )
    out_specs = (
        P("section", None, "fsdp"),
        P("section", None, "fsdp"),
        P("section", None, None, "fsdp"),
        P("section", "fsdp"),
    )
    return jax.shard_map(
        on_device, mesh=mesh, in_specs=in_specs, out_specs=out_specs, check_vma=False
    )
```

time: 276 us -> 156 us (0.57)
  waiting for transfers between devices: 138 us -> 51 us
  matrix products: 43.6 us -> 0 us
  starting transfers between devices: 8.97 us -> 51.5 us
  Pallas kernels: 0 us -> 36.2 us
  blocking collectives: 26.6 us -> 0 us
  between operations: 17.8 us -> 0.94 us
  local copies, waits for them, and re-layouts: 29 us -> 13.4 us
  other arithmetic: 7.41 us -> 0.01 us
    psum x1 -> x0, waiting for transfers between devices: 119 us -> none  [on_device(): lax.psum(partial_in.astype(jnp.bfloat16), 'fsdp').astype(jnp.float32)]
    ppermute x2 -> x27, waiting for transfers between devices: 0.01 us -> 51 us  [the longest x21 48.9 us: to_chip(): return lax.ppermute(block, 'fsdp', route)]
    ppermute x2 -> x27, starting transfers between devices: 8.85 us -> 51.5 us  [the longest x21 41.8 us: to_chip(): return lax.ppermute(block, 'fsdp', route)]
    dot_general x12 -> x0, matrix products: 41.8 us -> none  [the longest x1 7.2 us: on_device(): lax.dot_general(grads, w_flat, (((1,), (1,)), ((), ())), preferred_elemen...]
    pallas_call x0 -> x7, Pallas kernels: none -> 36.2 us  [the longest x2 20.3 us: attention_call(): pl.pallas_call(kernel, out_shape=out_shapes, grid_spec=pltpu.PrefetchScal...]
    psum x1 -> x0, blocking collectives: 26.6 us -> none  [on_device(): lax.psum((jnp.sum(wide_fwd * wide_fwd, axis=1), jnp.sum(wide_bwd * wide_b...]
    all_gather x2 -> x0, waiting for transfers between devices: 17.6 us -> none  [the longest x1 11.3 us: on_device(): lax.all_gather(scaled_fwd, 'fsdp', axis=1, tiled=True)]
    unnamed x22 -> x45, local copies, waits for them, and re-layouts: 19 us -> 12.5 us
  transfers between devices with their start and end apart: 5 -> 27, of which waited for: 3 -> 9; matrix products, arithmetic and copies ran while one was open for 28% -> 4% of each run, Pallas kernels for 0% -> 24%
where the time goes in v1:
time: 156 us; the launch traced here: 153 us
  starting transfers between devices  51.5 us (33%)
  waiting for transfers between devices  51 us (33%)
  Pallas kernels  36.2 us (23%)
  local copies, waits for them, and re-layouts  13.4 us (9%)
    ppermute x21, waiting for transfers between devices, to_chip(): return lax.ppermute(block, 'fsdp', route)  48.9 us
    ppermute x21, starting transfers between devices, to_chip(): return lax.ppermute(block, 'fsdp', route)  41.8 us
    pallas_call x2, Pallas kernels, attention_call(): pl.pallas_call(kernel, out_shape=out_shapes, grid_spec=pltpu.PrefetchScal...  20.3 us
    unnamed x45, local copies, waits for them, and re-layouts  12.5 us
    ppermute x2, starting transfers between devices, shifted(): lax.ppermute(block, axis, [((i - distance) % count, i) for i in range(cou...  9.06 us
    pallas_call x1, Pallas kernels, input_grad(): pl.pallas_call(input_grad_kernel, out_shape=[jax.ShapeDtypeStruct((rows,...  7.65 us
    pallas_call x1, Pallas kernels, weight_grad(): pl.pallas_call(weight_grad_kernel, out_shape=jax.ShapeDtypeStruct((3, 2 *...  7.12 us
  transfers between devices with their start and end apart: 27, of which 9 were waited for; matrix products, arithmetic and copies ran while one was open for 4% of the time, Pallas kernels for 24%

profile of v1, /device:TPU:8, one launch (start us, length us, event | category | flops | bytes accessed | tf_op | source)
XLA Modules:
  0.0 153.0 jit_solution(12987011964373337289)
XLA Ops:
  0.6 0.1 collective-permute-start.7
  0.7 0.0 copy-start.4
  0.7 0.9 copy-done.4
  1.7 0.7 copy-done.6
  2.3 0.1 pack_bwd.1
  2.5 2.6 %collective-permute-start.6 = (bf16[400,256]{1,0:T(8,128)(2,1)S(1)}, bf16[400,256]{1,0:T(8,128)(2,1)S(1)}, u32[]{:S(2)}, u32[]{:S(2)}) collective-permute-start(bf16[400,256]{1,0:T(8,128)(2,1)S(1)} %pack_bwd.1), channel_id=1, source_target_pairs={{0,14},{1,15},{2,12},{3,13},{4,10},{5,11},{6,8},{7,9},{8,6},{9,7},... | collective-permute-start | bytes 614408 | tf_op jit(solution)/shard_map/ppermute | solution.py:329
  5.1 2.6 %collective-permute-start.5 = (bf16[400,256]{1,0:T(8,128)(2,1)S(1)}, bf16[400,256]{1,0:T(8,128)(2,1)S(1)}, u32[]{:S(2)}, u32[]{:S(2)}) collective-permute-start(bf16[400,256]{1,0:T(8,128)(2,1)S(1)} %pack_bwd.1), channel_id=1, source_target_pairs={{0,12},{1,13},{2,14},{3,15},{4,8},{5,9},{6,10},{7,11},{8,4},{9,5},... | collective-permute-start | bytes 614408 | tf_op jit(solution)/shard_map/ppermute | solution.py:329
  7.7 0.8 collective-permute-start.4
  8.5 0.5 collective-permute-start
  9.0 0.9 copy-done.1
  9.9 0.7 copy-done.7
  10.6 0.1 pack_fwd.1
  10.7 13.2 %collective-permute-done = bf16[400,256]{1,0:T(8,128)(2,1)S(1)} collective-permute-done((bf16[400,256]{1,0:T(8,128)(2,1)S(1)}, bf16[400,256]{1,0:T(8,128)(2,1)S(1)}, u32[]{:S(2)}, u32[]{:S(2)}) %collective-permute-start) | collective-permute-done | bytes 204832 | tf_op jit(solution)/shard_map/ppermute | solution.py:329
  23.9 1.7 %collective-permute-start.1 = (bf16[400,256]{1,0:T(8,128)(2,1)S(1)}, bf16[400,256]{1,0:T(8,128)(2,1)S(1)}, u32[]{:S(2)}, u32[]{:S(2)}) collective-permute-start(bf16[400,256]{1,0:T(8,128)(2,1)S(1)} %pack_bwd.1), channel_id=1, source_target_pairs={{0,4},{1,5},{2,6},{3,7},{4,0},{5,1},{6,2},{7,3},{8,12},{9,13},{10,... | collective-permute-start | bytes 614408 | tf_op jit(solution)/shard_map/ppermute | solution.py:329
  25.6 5.6 %collective-permute-done.1 = bf16[400,256]{1,0:T(8,128)(2,1)S(1)} collective-permute-done((bf16[400,256]{1,0:T(8,128)(2,1)S(1)}, bf16[400,256]{1,0:T(8,128)(2,1)S(1)}, u32[]{:S(2)}, u32[]{:S(2)}) %collective-permute-start.1) | collective-permute-done | bytes 204832 | tf_op jit(solution)/shard_map/ppermute | solution.py:329
  31.2 1.6 %collective-permute-start.2 = (bf16[400,256]{1,0:T(8,128)(2,1)S(1)}, bf16[400,256]{1,0:T(8,128)(2,1)S(1)}, u32[]{:S(2)}, u32[]{:S(2)}) collective-permute-start(bf16[400,256]{1,0:T(8,128)(2,1)S(1)} %pack_bwd.1), channel_id=1, source_target_pairs={{0,6},{1,7},{2,4},{3,5},{4,2},{5,3},{6,0},{7,1},{8,14},{9,15},{10,... | collective-permute-start | bytes 614408 | tf_op jit(solution)/shard_map/ppermute | solution.py:329
  32.8 4.1 %collective-permute-done.2 = bf16[400,256]{1,0:T(8,128)(2,1)S(1)} collective-permute-done((bf16[400,256]{1,0:T(8,128)(2,1)S(1)}, bf16[400,256]{1,0:T(8,128)(2,1)S(1)}, u32[]{:S(2)}, u32[]{:S(2)}) %collective-permute-start.2) | collective-permute-done | bytes 204832 | tf_op jit(solution)/shard_map/ppermute | solution.py:329
  36.9 1.3 collective-permute-start.3
  38.2 5.1 %collective-permute-done.3 = bf16[400,256]{1,0:T(8,128)(2,1)S(1)} collective-permute-done((bf16[400,256]{1,0:T(8,128)(2,1)S(1)}, bf16[400,256]{1,0:T(8,128)(2,1)S(1)}, u32[]{:S(2)}, u32[]{:S(2)}) %collective-permute-start.3) | collective-permute-done | bytes 204832 | tf_op jit(solution)/shard_map/ppermute | solution.py:329
  43.4 0.0 copy-start.10
  43.5 0.0 copy-start.9
  43.5 2.8 %collective-permute-start.14 = (bf16[400,256]{1,0:T(8,128)(2,1)S(1)}, bf16[400,256]{1,0:T(8,128)(2,1)S(1)}, u32[]{:S(2)}, u32[]{:S(2)}) collective-permute-start(bf16[400,256]{1,0:T(8,128)(2,1)S(1)} %pack_fwd.1), channel_id=1, source_target_pairs={{0,14},{1,15},{2,12},{3,13},{4,10},{5,11},{6,8},{7,9},{8,6},{9,7},... | collective-permute-start | bytes 614408 | tf_op jit(solution)/shard_map/ppermute | solution.py:329
  46.3 2.2 %collective-permute-start.13 = (bf16[400,256]{1,0:T(8,128)(2,1)S(1)}, bf16[400,256]{1,0:T(8,128)(2,1)S(1)}, u32[]{:S(2)}, u32[]{:S(2)}) collective-permute-start(bf16[400,256]{1,0:T(8,128)(2,1)S(1)} %pack_fwd.1), channel_id=1, source_target_pairs={{0,12},{1,13},{2,14},{3,15},{4,8},{5,9},{6,10},{7,11},{8,4},{9,5},... | collective-permute-start | bytes 614408 | tf_op jit(solution)/shard_map/ppermute | solution.py:329
  48.5 1.0 collective-permute-start.12
  49.5 1.0 collective-permute-start.11
  50.5 1.5 collective-permute-start.8
  52.0 0.7 bitcast_dynamic-update-slice_fusion.7
  52.7 6.9 %collective-permute-done.8 = bf16[400,256]{1,0:T(8,128)(2,1)S(1)} collective-permute-done((bf16[400,256]{1,0:T(8,128)(2,1)S(1)}, bf16[400,256]{1,0:T(8,128)(2,1)S(1)}, u32[]{:S(2)}, u32[]{:S(2)}) %collective-permute-start.8) | collective-permute-done | bytes 204832 | tf_op jit(solution)/shard_map/ppermute | solution.py:329
  59.6 4.8 %collective-permute-start.9 = (bf16[400,256]{1,0:T(8,128)(2,1)S(1)}, bf16[400,256]{1,0:T(8,128)(2,1)S(1)}, u32[]{:S(2)}, u32[]{:S(2)}) collective-permute-start(bf16[400,256]{1,0:T(8,128)(2,1)S(1)} %pack_fwd.1), channel_id=1, source_target_pairs={{0,4},{1,5},{2,6},{3,7},{4,0},{5,1},{6,2},{7,3},{8,12},{9,13},{10,... | collective-permute-start | bytes 614408 | tf_op jit(solution)/shard_map/ppermute | solution.py:329
  64.4 0.7 bitcast_dynamic-update-slice_fusion.6
  65.0 3.1 %collective-permute-done.9 = bf16[400,256]{1,0:T(8,128)(2,1)S(1)} collective-permute-done((bf16[400,256]{1,0:T(8,128)(2,1)S(1)}, bf16[400,256]{1,0:T(8,128)(2,1)S(1)}, u32[]{:S(2)}, u32[]{:S(2)}) %collective-permute-start.9) | collective-permute-done | bytes 204832 | tf_op jit(solution)/shard_map/ppermute | solution.py:329
  68.2 1.9 %collective-permute-start.10 = (bf16[400,256]{1,0:T(8,128)(2,1)S(1)}, bf16[400,256]{1,0:T(8,128)(2,1)S(1)}, u32[]{:S(2)}, u32[]{:S(2)}) collective-permute-start(bf16[400,256]{1,0:T(8,128)(2,1)S(1)} %pack_fwd.1), channel_id=1, source_target_pairs={{0,6},{1,7},{2,4},{3,5},{4,2},{5,3},{6,0},{7,1},{8,14},{9,15},{10,... | collective-permute-start | bytes 614408 | tf_op jit(solution)/shard_map/ppermute | solution.py:329
  70.1 0.7 bitcast_dynamic-update-slice_fusion.5
  70.8 3.1 %collective-permute-done.10 = bf16[400,256]{1,0:T(8,128)(2,1)S(1)} collective-permute-done((bf16[400,256]{1,0:T(8,128)(2,1)S(1)}, bf16[400,256]{1,0:T(8,128)(2,1)S(1)}, u32[]{:S(2)}, u32[]{:S(2)}) %collective-permute-start.10) | collective-permute-done | bytes 204832 | tf_op jit(solution)/shard_map/ppermute | solution.py:329
  74.0 0.7 bitcast_dynamic-update-slice_fusion.4
  74.7 0.7 bitcast_dynamic-update-slice_fusion.3
  75.4 0.7 bitcast_dynamic-update-slice_fusion.2
  76.1 0.7 bitcast_dynamic-update-slice_fusion.1
  76.8 0.7 bitcast_dynamic-update-slice_fusion.mine_ref
  77.5 0.5 collective-permute-start.15
  78.0 0.1 copy.12
  78.1 0.1 reshape.14
  78.2 0.1 concatenate.3.ints_ref
  78.3 2.8 %copy-done = bf16[1,4096,3,256]{3,1,2,0:T(8,128)(2,1)S(1)} copy-done((bf16[1,4096,3,256]{3,1,2,0:T(8,128)(2,1)S(1)}, bf16[1,4096,3,256]{3,1,2,0:T(8,128)(2,1)}, u32[]{:S(2)}) %copy-start) | copy-done | bytes 6291480
  81.1 9.5 %backward.1 = (bf16[400,768]{1,0:T(8,128)(2,1)S(1)}, f32[384,128]{1,0:T(8,128)S(1)}) custom-call(s32[75]{0:T(128)S(1)} %concatenate.3.ints_ref, bf16[8,400,256]{2,1,0:T(8,128)(2,1)S(1)} %bitcast_dynamic-update-slice_fusion.8.mine_ref, bf16[8,400,256]{2,1,0:T(8,128)(2,1)S(1)} %collective-permute-done.17.other_ref, bf16[3,4096,256]{2,1,0:T(8,128)(2,1)S(1)} %bitcast.46, ...), custom_call_target="tpu_custom_call" | custom-call | tf_op jit(solution)/shard_map/backward/pallas_call | solution.py:209
  90.6 0.0 slice-start
  90.7 0.1 collective-permute-start.18
  90.8 2.0 %collective-permute-done.18.other_ref = bf16[400,768]{1,0:T(8,128)(2,1)S(1)} collective-permute-done((bf16[400,768]{1,0:T(8,128)(2,1)S(1)}, bf16[400,768]{1,0:T(8,128)(2,1)S(1)}, u32[]{:S(2)}, u32[]{:S(2)}) %collective-permute-start.18) | collective-permute-done | bytes 614432 | tf_op jit(solution)/shard_map/ppermute | solution.py:333
  92.8 7.6 %input_grad.1 = (bf16[400,256]{1,0:T(8,128)(2,1)S(1)}, bf16[400,256]{1,0:T(8,128)(2,1)S(1)}, bf16[400,256]{1,0:T(8,128)(2,1)S(1)}, bf16[400,256]{1,0:T(8,128)(2,...) custom-call(s32[75]{0:T(128)S(1)} %concatenate.3.ints_ref, ...), custom_call_target="tpu_custom_call" | custom-call | tf_op jit(solution)/shard_map/input_grad/pallas_call | solution.py:253
  100.5 2.8 %collective-permute-start.19 = (bf16[400,256]{1,0:T(8,128)(2,1)S(1)}, bf16[400,256]{1,0:T(8,128)(2,1)S(1)}, u32[]{:S(2)}, u32[]{:S(2)}) collective-permute-start(bf16[400,256]{1,0:T(8,128)(2,1)S(1)} %get-tuple-element.24), channel_id=1, source_target_pairs={{0,2},{1,3},{2,0},{3,1},{4,6},{5,7},{6,4},{7,5},{8,10},{9,11},{10,... | collective-permute-start | bytes 614408 | tf_op jit(solution)/shard_map/ppermute | solution.py:329
  103.2 2.1 %collective-permute-start.20 = (bf16[400,256]{1,0:T(8,128)(2,1)S(1)}, bf16[400,256]{1,0:T(8,128)(2,1)S(1)}, u32[]{:S(2)}, u32[]{:S(2)}) collective-permute-start(bf16[400,256]{1,0:T(8,128)(2,1)S(1)} %get-tuple-element.25), channel_id=1, source_target_pairs={{0,4},{1,5},{2,6},{3,7},{4,0},{5,1},{6,2},{7,3},{8,12},{9,13},{10,... | collective-permute-start | bytes 614408 | tf_op jit(solution)/shard_map/ppermute | solution.py:329
  105.4 0.5 collective-permute-start.21
  105.8 0.8 collective-permute-start.22
  106.7 2.7 %collective-permute-start.23 = (bf16[400,256]{1,0:T(8,128)(2,1)S(1)}, bf16[400,256]{1,0:T(8,128)(2,1)S(1)}, u32[]{:S(2)}, u32[]{:S(2)}) collective-permute-start(bf16[400,256]{1,0:T(8,128)(2,1)S(1)} %get-tuple-element.28), channel_id=1, source_target_pairs={{0,10},{1,11},{2,8},{3,9},{4,14},{5,15},{6,12},{7,13},{8,2},{9,3},... | collective-permute-start | bytes 614408 | tf_op jit(solution)/shard_map/ppermute | solution.py:329
  109.4 3.9 %collective-permute-start.24 = (bf16[400,256]{1,0:T(8,128)(2,1)S(1)}, bf16[400,256]{1,0:T(8,128)(2,1)S(1)}, u32[]{:S(2)}, u32[]{:S(2)}) collective-permute-start(bf16[400,256]{1,0:T(8,128)(2,1)S(1)} %get-tuple-element.29), channel_id=1, source_target_pairs={{0,12},{1,13},{2,14},{3,15},{4,8},{5,9},{6,10},{7,11},{8,4},{9,5},... | collective-permute-start | bytes 614408 | tf_op jit(solution)/shard_map/ppermute | solution.py:329
  113.3 7.7 %collective-permute-done.20.refs_2_ = bf16[400,256]{1,0:T(8,128)(2,1)S(1)} collective-permute-done((bf16[400,256]{1,0:T(8,128)(2,1)S(1)}, bf16[400,256]{1,0:T(8,128)(2,1)S(1)}, u32[]{:S(2)}, u32[]{:S(2)}) %collective-permute-start.20) | collective-permute-done | bytes 204832 | tf_op jit(solution)/shard_map/ppermute | solution.py:329
  121.1 2.7 %collective-permute-start.25 = (bf16[400,256]{1,0:T(8,128)(2,1)S(1)}, bf16[400,256]{1,0:T(8,128)(2,1)S(1)}, u32[]{:S(2)}, u32[]{:S(2)}) collective-permute-start(bf16[400,256]{1,0:T(8,128)(2,1)S(1)} %get-tuple-element.30), channel_id=1, source_target_pairs={{0,14},{1,15},{2,12},{3,13},{4,10},{5,11},{6,8},{7,9},{8,6},{9,7},... | collective-permute-start | bytes 614408 | tf_op jit(solution)/shard_map/ppermute | solution.py:329
  123.8 10.7 %forward.1 = bf16[384,256]{1,0:T(8,128)(2,1)S(1)} custom-call(s32[75]{0:T(128)S(1)} %concatenate.3.ints_ref, bf16[8,400,256]{2,1,0:T(8,128)(2,1)} %bitcast_dynamic-update-slice_fusion.mine_ref, bf16[8,400,256]{2,1,0:T(8,128)(2,1)} %collective-permute-done.15.other_ref, bf16[3,4096,256]{2,1,0:T(8,128)(2,1)S(1)} %bitcast.53, ...), custom_call_target="tpu_custom_call" | custom-call | tf_op jit(solution)/shard_map/forward/pallas_call | solution.py:209
  134.5 3.7 %collective-permute-start.16 = (bf16[384,256]{1,0:T(8,128)(2,1)S(1)}, bf16[384,256]{1,0:T(8,128)(2,1)S(1)}, u32[]{:S(2)}, u32[]{:S(2)}) collective-permute-start(bf16[384,256]{1,0:T(8,128)(2,1)S(1)} %forward.1), channel_id=1, source_target_pairs={{240,0},{0,16},{16,32},{32,48},{48,64},{64,80},{80,96},{96,112},{1... | collective-permute-start | bytes 589832 | tf_op jit(solution)/shard_map/ppermute | solution.py:338
  138.3 0.9 finish.1
  139.2 5.3 %collective-permute-start.26 = (bf16[384,256]{1,0:T(8,128)(2,1)S(1)}, bf16[384,256]{1,0:T(8,128)(2,1)S(1)}, u32[]{:S(2)}, u32[]{:S(2)}) collective-permute-start(bf16[384,256]{1,0:T(8,128)(2,1)S(1)} %get-tuple-element.32), channel_id=1, source_target_pairs={{16,0},{32,16},{48,32},{64,48},{80,64},{96,80},{112,96},{128,112},... | collective-permute-start | bytes 589832 | tf_op jit(solution)/shard_map/ppermute | solution.py:338
  144.6 7.1 %weight_grad.1 = bf16[3,4096,256]{2,1,0:T(8,128)(2,1)} custom-call(s32[75]{0:T(128)S(1)} %concatenate.3.ints_ref, bf16[8,400,256]{2,1,0:T(8,128)(2,1)S(1)} %bitcast_dynamic-update-slice_fusion.8.mine_ref, bf16[8,400,256]{2,1,0:T(8,128)(2,1)S(1)} %collective-permute-done.17.other_ref, bf16[400,768]{1,0:T(8,128)(2,1)S(1)} %get-tuple-element.21.mine_ref.g_ref), custom_call_target="tpu_custom_call" | custom-call | tf_op jit(solution)/shard_map/weight_grad/pallas_call | solution.py:285
  151.7 0.7 copy.29
  152.4 0.7 copy.30
  (49 shorter events, 0.2 us)
Async XLA Ops:
  0.6 42.8 %collective-permute-start.7 = (bf16[3,4096,256]{2,1,0:T(8,128)(2,1)}, bf16[3,4096,256]{2,1,0:T(8,128)(2,1)S(1)}, u32[]{:S(2)}, u32[]{:S(2)}) collective-permute-start(bf16[3,4096,256]{2,1,0:T(8,128)(2,1)} %bitcast.45), channel_id=1, source_target_pairs={{0,1},{1,0},{2,3},{3,2},{4,5},{5,4},{6,7},{7,6},{8,9},{9,8},{10,11... | collective-permute-start | bytes 18874376 | tf_op jit(solution)/shard_map/ppermute | solution.py:333
  0.7 0.9 copy-start.4
  1.7 0.7 copy-start.6
  2.5 40.9 %collective-permute-start.6 = (bf16[400,256]{1,0:T(8,128)(2,1)S(1)}, bf16[400,256]{1,0:T(8,128)(2,1)S(1)}, u32[]{:S(2)}, u32[]{:S(2)}) collective-permute-start(bf16[400,256]{1,0:T(8,128)(2,1)S(1)} %pack_bwd.1), channel_id=1, source_target_pairs={{0,14},{1,15},{2,12},{3,13},{4,10},{5,11},{6,8},{7,9},{8,6},{9,7},... | collective-permute-start | bytes 614408 | tf_op jit(solution)/shard_map/ppermute | solution.py:329
  5.1 38.3 %collective-permute-start.5 = (bf16[400,256]{1,0:T(8,128)(2,1)S(1)}, bf16[400,256]{1,0:T(8,128)(2,1)S(1)}, u32[]{:S(2)}, u32[]{:S(2)}) collective-permute-start(bf16[400,256]{1,0:T(8,128)(2,1)S(1)} %pack_bwd.1), channel_id=1, source_target_pairs={{0,12},{1,13},{2,14},{3,15},{4,8},{5,9},{6,10},{7,11},{8,4},{9,5},... | collective-permute-start | bytes 614408 | tf_op jit(solution)/shard_map/ppermute | solution.py:329
  7.7 35.6 %collective-permute-start.4 = (bf16[400,256]{1,0:T(8,128)(2,1)S(1)}, bf16[400,256]{1,0:T(8,128)(2,1)S(1)}, u32[]{:S(2)}, u32[]{:S(2)}) collective-permute-start(bf16[400,256]{1,0:T(8,128)(2,1)S(1)} %pack_bwd.1), channel_id=1, source_target_pairs={{0,10},{1,11},{2,8},{3,9},{4,14},{5,15},{6,12},{7,13},{8,2},{9,3},... | collective-permute-start | bytes 614408 | tf_op jit(solution)/shard_map/ppermute | solution.py:329
  8.5 15.4 %collective-permute-start = (bf16[400,256]{1,0:T(8,128)(2,1)S(1)}, bf16[400,256]{1,0:T(8,128)(2,1)S(1)}, u32[]{:S(2)}, u32[]{:S(2)}) collective-permute-start(bf16[400,256]{1,0:T(8,128)(2,1)S(1)} %pack_bwd.1), channel_id=1, source_target_pairs={{0,2},{1,3},{2,0},{3,1},{4,6},{5,7},{6,4},{7,5},{8,10},{9,11},{10,... | collective-permute-start | bytes 614408 | tf_op jit(solution)/shard_map/ppermute | solution.py:329
  9.0 0.9 copy-start.1
  9.9 0.7 copy-start.7
  23.9 7.3 %collective-permute-start.1 = (bf16[400,256]{1,0:T(8,128)(2,1)S(1)}, bf16[400,256]{1,0:T(8,128)(2,1)S(1)}, u32[]{:S(2)}, u32[]{:S(2)}) collective-permute-start(bf16[400,256]{1,0:T(8,128)(2,1)S(1)} %pack_bwd.1), channel_id=1, source_target_pairs={{0,4},{1,5},{2,6},{3,7},{4,0},{5,1},{6,2},{7,3},{8,12},{9,13},{10,... | collective-permute-start | bytes 614408 | tf_op jit(solution)/shard_map/ppermute | solution.py:329
  31.2 5.8 %collective-permute-start.2 = (bf16[400,256]{1,0:T(8,128)(2,1)S(1)}, bf16[400,256]{1,0:T(8,128)(2,1)S(1)}, u32[]{:S(2)}, u32[]{:S(2)}) collective-permute-start(bf16[400,256]{1,0:T(8,128)(2,1)S(1)} %pack_bwd.1), channel_id=1, source_target_pairs={{0,6},{1,7},{2,4},{3,5},{4,2},{5,3},{6,0},{7,1},{8,14},{9,15},{10,... | collective-permute-start | bytes 614408 | tf_op jit(solution)/shard_map/ppermute | solution.py:329
  36.9 6.4 %collective-permute-start.3 = (bf16[400,256]{1,0:T(8,128)(2,1)S(1)}, bf16[400,256]{1,0:T(8,128)(2,1)S(1)}, u32[]{:S(2)}, u32[]{:S(2)}) collective-permute-start(bf16[400,256]{1,0:T(8,128)(2,1)S(1)} %pack_bwd.1), channel_id=1, source_target_pairs={{0,8},{1,9},{2,10},{3,11},{4,12},{5,13},{6,14},{7,15},{8,0},{9,1},... | collective-permute-start | bytes 614408 | tf_op jit(solution)/shard_map/ppermute | solution.py:329
  43.4 34.5 %copy-start.10 = (s32[8,3,2]{0,2,1:T(2,128)S(1)}, s32[8,3,2]{0,2,1:T(2,128)}, u32[]{:S(2)}) copy-start(s32[8,3,2]{0,2,1:T(2,128)} %param.12) | copy-start | bytes 580
  43.4 34.8 %copy-start.11 = (s32[1,2]{1,0:T(1,128)S(1)}, s32[1,2]{1,0:T(1,128)}, u32[]{:S(2)}) copy-start(s32[1,2]{1,0:T(1,128)} %param.13) | copy-start | bytes 28
  43.5 34.9 %copy-start.3 = (bf16[1,384,256]{2,1,0:T(8,128)(2,1)S(1)}, bf16[1,384,256]{2,1,0:T(8,128)(2,1)}, u32[]{:S(2)}) copy-start(bf16[1,384,256]{2,1,0:T(8,128)(2,1)} %param.9) | copy-start | bytes 589828
  43.5 33.3 %copy-start.9 = (bf16[3,4096,256]{2,1,0:T(8,128)(2,1)}, bf16[3,4096,256]{2,1,0:T(8,128)(2,1)S(1)}, u32[]{:S(2)}) copy-start(bf16[3,4096,256]{2,1,0:T(8,128)(2,1)S(1)} %collective-permute-done.7.w_other_ref) | copy-start | bytes 18874372
  43.5 33.3 %collective-permute-start.14 = (bf16[400,256]{1,0:T(8,128)(2,1)S(1)}, bf16[400,256]{1,0:T(8,128)(2,1)S(1)}, u32[]{:S(2)}, u32[]{:S(2)}) collective-permute-start(bf16[400,256]{1,0:T(8,128)(2,1)S(1)} %pack_fwd.1), channel_id=1, source_target_pairs={{0,14},{1,15},{2,12},{3,13},{4,10},{5,11},{6,8},{7,9},{8,6},{9,7},... | collective-permute-start | bytes 614408 | tf_op jit(solution)/shard_map/ppermute | solution.py:329
  46.3 29.8 %collective-permute-start.13 = (bf16[400,256]{1,0:T(8,128)(2,1)S(1)}, bf16[400,256]{1,0:T(8,128)(2,1)S(1)}, u32[]{:S(2)}, u32[]{:S(2)}) collective-permute-start(bf16[400,256]{1,0:T(8,128)(2,1)S(1)} %pack_fwd.1), channel_id=1, source_target_pairs={{0,12},{1,13},{2,14},{3,15},{4,8},{5,9},{6,10},{7,11},{8,4},{9,5},... | collective-permute-start | bytes 614408 | tf_op jit(solution)/shard_map/ppermute | solution.py:329
  48.5 26.9 %collective-permute-start.12 = (bf16[400,256]{1,0:T(8,128)(2,1)S(1)}, bf16[400,256]{1,0:T(8,128)(2,1)S(1)}, u32[]{:S(2)}, u32[]{:S(2)}) collective-permute-start(bf16[400,256]{1,0:T(8,128)(2,1)S(1)} %pack_fwd.1), channel_id=1, source_target_pairs={{0,10},{1,11},{2,8},{3,9},{4,14},{5,15},{6,12},{7,13},{8,2},{9,3},... | collective-permute-start | bytes 614408 | tf_op jit(solution)/shard_map/ppermute | solution.py:329
  49.5 25.2 %collective-permute-start.11 = (bf16[400,256]{1,0:T(8,128)(2,1)S(1)}, bf16[400,256]{1,0:T(8,128)(2,1)S(1)}, u32[]{:S(2)}, u32[]{:S(2)}) collective-permute-start(bf16[400,256]{1,0:T(8,128)(2,1)S(1)} %pack_fwd.1), channel_id=1, source_target_pairs={{0,8},{1,9},{2,10},{3,11},{4,12},{5,13},{6,14},{7,15},{8,0},{9,1},... | collective-permute-start | bytes 614408 | tf_op jit(solution)/shard_map/ppermute | solution.py:329
  50.5 9.1 %collective-permute-start.8 = (bf16[400,256]{1,0:T(8,128)(2,1)S(1)}, bf16[400,256]{1,0:T(8,128)(2,1)S(1)}, u32[]{:S(2)}, u32[]{:S(2)}) collective-permute-start(bf16[400,256]{1,0:T(8,128)(2,1)S(1)} %pack_fwd.1), channel_id=1, source_target_pairs={{0,2},{1,3},{2,0},{3,1},{4,6},{5,7},{6,4},{7,5},{8,10},{9,11},{10,... | collective-permute-start | bytes 614408 | tf_op jit(solution)/shard_map/ppermute | solution.py:329
  59.6 8.6 %collective-permute-start.9 = (bf16[400,256]{1,0:T(8,128)(2,1)S(1)}, bf16[400,256]{1,0:T(8,128)(2,1)S(1)}, u32[]{:S(2)}, u32[]{:S(2)}) collective-permute-start(bf16[400,256]{1,0:T(8,128)(2,1)S(1)} %pack_fwd.1), channel_id=1, source_target_pairs={{0,4},{1,5},{2,6},{3,7},{4,0},{5,1},{6,2},{7,3},{8,12},{9,13},{10,... | collective-permute-start | bytes 614408 | tf_op jit(solution)/shard_map/ppermute | solution.py:329
  68.2 5.8 %collective-permute-start.10 = (bf16[400,256]{1,0:T(8,128)(2,1)S(1)}, bf16[400,256]{1,0:T(8,128)(2,1)S(1)}, u32[]{:S(2)}, u32[]{:S(2)}) collective-permute-start(bf16[400,256]{1,0:T(8,128)(2,1)S(1)} %pack_fwd.1), channel_id=1, source_target_pairs={{0,6},{1,7},{2,4},{3,5},{4,2},{5,3},{6,0},{7,1},{8,14},{9,15},{10,... | collective-permute-start | bytes 614408 | tf_op jit(solution)/shard_map/ppermute | solution.py:329
  74.0 4.4 %collective-permute-start.17 = (bf16[8,400,256]{2,1,0:T(8,128)(2,1)S(1)}, bf16[8,400,256]{2,1,0:T(8,128)(2,1)S(1)}, u32[]{:S(2)}, u32[]{:S(2)}) collective-permute-start(bf16[8,400,256]{2,1,0:T(8,128)(2,1)S(1)} %bitcast_dynamic-update-slice_fusion.8.mine_ref), channel_id=1, source_target_pairs={{0,1},{1,0},{2,3},{3,2},{4,5},{5,4},{6,7},{7,6},{8,9},{9,8},{10,11... | collective-permute-start | bytes 4915208 | tf_op jit(solution)/shard_map/ppermute | solution.py:333
  77.5 29.2 %collective-permute-start.15 = (bf16[8,400,256]{2,1,0:T(8,128)(2,1)}, bf16[8,400,256]{2,1,0:T(8,128)(2,1)}, u32[]{:S(2)}, u32[]{:S(2)}) collective-permute-start(bf16[8,400,256]{2,1,0:T(8,128)(2,1)} %bitcast_dynamic-update-slice_fusion.mine_ref), channel_id=1, source_target_pairs={{0,1},{1,0},{2,3},{3,2},{4,5},{5,4},{6,7},{7,6},{8,9},{9,8},{10,11... | collective-permute-start | bytes 4915208 | tf_op jit(solution)/shard_map/ppermute | solution.py:333
  78.3 2.8 %copy-start = (bf16[1,4096,3,256]{3,1,2,0:T(8,128)(2,1)S(1)}, bf16[1,4096,3,256]{3,1,2,0:T(8,128)(2,1)}, u32[]{:S(2)}) copy-start(bf16[1,4096,3,256]{3,1,2,0:T(8,128)(2,1)} %param.10) | copy-start | bytes 18874372
  90.6 33.1 %slice-start = ((s8[6291456]{0:T(1024)(128)(4,1)}), s8[4194304]{0:T(1024)(128)(4,1)S(1)}, s32[]{:S(2)}) async-start(s8[6291456]{0:T(1024)(128)(4,1)} %bitcast.51), calls=%async_computation | async-start | bytes 8388608
  90.7 33.1 %slice-start.1 = ((s8[6291456]{0:T(1024)(128)(4,1)}), s8[2097152]{0:T(1024)(128)(4,1)S(1)}, s32[]{:S(2)}) async-start(s8[6291456]{0:T(1024)(128)(4,1)} %bitcast.51), calls=%async_computation.1 | async-start | bytes 4194304
  90.7 33.1 %copy-start.2 = (bf16[1,384,256]{2,1,0:T(8,128)(2,1)S(1)}, bf16[1,384,256]{2,1,0:T(8,128)(2,1)}, u32[]{:S(2)}) copy-start(bf16[1,384,256]{2,1,0:T(8,128)(2,1)} %param.7) | copy-start | bytes 589828
  90.7 2.1 %collective-permute-start.18 = (bf16[400,768]{1,0:T(8,128)(2,1)S(1)}, bf16[400,768]{1,0:T(8,128)(2,1)S(1)}, u32[]{:S(2)}, u32[]{:S(2)}) collective-permute-start(bf16[400,768]{1,0:T(8,128)(2,1)S(1)} %get-tuple-element.21.mine_ref.g_ref), channel_id=1, source_target_pairs={{0,1},{1,0},{2,3},{3,2},{4,5},{5,4},{6,7},{7,6},{8,9},{9,8},{10,11... | collective-permute-start | bytes 1843208 | tf_op jit(solution)/shard_map/ppermute | solution.py:333
  100.5 8.9 %collective-permute-start.19 = (bf16[400,256]{1,0:T(8,128)(2,1)S(1)}, bf16[400,256]{1,0:T(8,128)(2,1)S(1)}, u32[]{:S(2)}, u32[]{:S(2)}) collective-permute-start(bf16[400,256]{1,0:T(8,128)(2,1)S(1)} %get-tuple-element.24), channel_id=1, source_target_pairs={{0,2},{1,3},{2,0},{3,1},{4,6},{5,7},{6,4},{7,5},{8,10},{9,11},{10,... | collective-permute-start | bytes 614408 | tf_op jit(solution)/shard_map/ppermute | solution.py:329
  103.2 17.8 %collective-permute-start.20 = (bf16[400,256]{1,0:T(8,128)(2,1)S(1)}, bf16[400,256]{1,0:T(8,128)(2,1)S(1)}, u32[]{:S(2)}, u32[]{:S(2)}) collective-permute-start(bf16[400,256]{1,0:T(8,128)(2,1)S(1)} %get-tuple-element.25), channel_id=1, source_target_pairs={{0,4},{1,5},{2,6},{3,7},{4,0},{5,1},{6,2},{7,3},{8,12},{9,13},{10,... | collective-permute-start | bytes 614408 | tf_op jit(solution)/shard_map/ppermute | solution.py:329
  105.4 29.2 %collective-permute-start.21 = (bf16[400,256]{1,0:T(8,128)(2,1)S(1)}, bf16[400,256]{1,0:T(8,128)(2,1)S(1)}, u32[]{:S(2)}, u32[]{:S(2)}) collective-permute-start(bf16[400,256]{1,0:T(8,128)(2,1)S(1)} %get-tuple-element.26), channel_id=1, source_target_pairs={{0,6},{1,7},{2,4},{3,5},{4,2},{5,3},{6,0},{7,1},{8,14},{9,15},{10,... | collective-permute-start | bytes 614408 | tf_op jit(solution)/shard_map/ppermute | solution.py:329
  105.8 32.4 %collective-permute-start.22 = (bf16[400,256]{1,0:T(8,128)(2,1)S(1)}, bf16[400,256]{1,0:T(8,128)(2,1)S(1)}, u32[]{:S(2)}, u32[]{:S(2)}) collective-permute-start(bf16[400,256]{1,0:T(8,128)(2,1)S(1)} %get-tuple-element.27), channel_id=1, source_target_pairs={{0,8},{1,9},{2,10},{3,11},{4,12},{5,13},{6,14},{7,15},{8,0},{9,1},... | collective-permute-start | bytes 614408 | tf_op jit(solution)/shard_map/ppermute | solution.py:329
  106.7 31.6 %collective-permute-start.23 = (bf16[400,256]{1,0:T(8,128)(2,1)S(1)}, bf16[400,256]{1,0:T(8,128)(2,1)S(1)}, u32[]{:S(2)}, u32[]{:S(2)}) collective-permute-start(bf16[400,256]{1,0:T(8,128)(2,1)S(1)} %get-tuple-element.28), channel_id=1, source_target_pairs={{0,10},{1,11},{2,8},{3,9},{4,14},{5,15},{6,12},{7,13},{8,2},{9,3},... | collective-permute-start | bytes 614408 | tf_op jit(solution)/shard_map/ppermute | solution.py:329
  109.4 28.9 %collective-permute-start.24 = (bf16[400,256]{1,0:T(8,128)(2,1)S(1)}, bf16[400,256]{1,0:T(8,128)(2,1)S(1)}, u32[]{:S(2)}, u32[]{:S(2)}) collective-permute-start(bf16[400,256]{1,0:T(8,128)(2,1)S(1)} %get-tuple-element.29), channel_id=1, source_target_pairs={{0,12},{1,13},{2,14},{3,15},{4,8},{5,9},{6,10},{7,11},{8,4},{9,5},... | collective-permute-start | bytes 614408 | tf_op jit(solution)/shard_map/ppermute | solution.py:329
  121.1 17.2 %copy-start.5 = (bf16[1,384,256]{2,1,0:T(8,128)(2,1)S(1)}, bf16[1,384,256]{2,1,0:T(8,128)(2,1)}, u32[]{:S(2)}) copy-start(bf16[1,384,256]{2,1,0:T(8,128)(2,1)} %param.8) | copy-start | bytes 589828
  121.1 17.2 %copy-start.8 = (f32[1,256]{1,0:T(1,128)S(1)}, f32[1,256]{1,0:T(1,128)}, u32[]{:S(2)}) copy-start(f32[1,256]{1,0:T(1,128)} %refs_10_.1) | copy-start | bytes 3076
  121.1 17.2 %collective-permute-start.25 = (bf16[400,256]{1,0:T(8,128)(2,1)S(1)}, bf16[400,256]{1,0:T(8,128)(2,1)S(1)}, u32[]{:S(2)}, u32[]{:S(2)}) collective-permute-start(bf16[400,256]{1,0:T(8,128)(2,1)S(1)} %get-tuple-element.30), channel_id=1, source_target_pairs={{0,14},{1,15},{2,12},{3,13},{4,10},{5,11},{6,8},{7,9},{8,6},{9,7},... | collective-permute-start | bytes 614408 | tf_op jit(solution)/shard_map/ppermute | solution.py:329
  134.5 17.2 %collective-permute-start.16 = (bf16[384,256]{1,0:T(8,128)(2,1)S(1)}, bf16[384,256]{1,0:T(8,128)(2,1)S(1)}, u32[]{:S(2)}, u32[]{:S(2)}) collective-permute-start(bf16[384,256]{1,0:T(8,128)(2,1)S(1)} %forward.1), channel_id=1, source_target_pairs={{240,0},{0,16},{16,32},{32,48},{48,64},{64,80},{80,96},{96,112},{1... | collective-permute-start | bytes 589832 | tf_op jit(solution)/shard_map/ppermute | solution.py:338
  139.2 12.4 %collective-permute-start.26 = (bf16[384,256]{1,0:T(8,128)(2,1)S(1)}, bf16[384,256]{1,0:T(8,128)(2,1)S(1)}, u32[]{:S(2)}, u32[]{:S(2)}) collective-permute-start(bf16[384,256]{1,0:T(8,128)(2,1)S(1)} %get-tuple-element.32), channel_id=1, source_target_pairs={{16,0},{32,16},{48,32},{64,48},{80,64},{96,80},{112,96},{128,112},... | collective-permute-start | bytes 589832 | tf_op jit(solution)/shard_map/ppermute | solution.py:338

commit v2 on v1

v2 whole, which is shorter than its diff:
```python
import functools
import math

import jax
import jax.numpy as jnp
from jax import lax
from jax.experimental import pallas as pl
from jax.experimental.pallas import tpu as pltpu
from jax.sharding import PartitionSpec as P

HD = 128
BLK = 128
EPS = 1e-05
STAT = 16
CHIPS = 8
F32 = jnp.float32
BF16 = jnp.bfloat16
VMEM_BYTES = 40 << 20


def pieces(row):
    high = row.astype(BF16).astype(F32)
    rest = row - high
    mid = rest.astype(BF16).astype(F32)
    return high, mid, rest - mid


def stat_rows(row, width):
    span = row.shape[1]
    index = lax.broadcasted_iota(jnp.int32, (STAT, width), 0)
    out = jnp.zeros((STAT, width), F32)
    for i, part in enumerate(pieces(row)):
        for j, start in enumerate(range(0, span, width)):
            held = part[:, start : start + width]
            if held.shape[1] < width:
                held = jnp.concatenate(
                    [held, jnp.zeros((1, width - held.shape[1]), F32)], axis=1
                )
            out = jnp.where(index == 3 * j + i, jnp.broadcast_to(held, (STAT, width)), out)
    return out.astype(BF16)


def stat_row(rows, span):
    width = rows.shape[1]
    parts = []
    for j, start in enumerate(range(0, span, width)):
        part = rows[3 * j : 3 * j + 1] + rows[3 * j + 1 : 3 * j + 2] + rows[3 * j + 2 : 3 * j + 3]
        parts.append(part[:, : min(width, span - start)])
    return parts[0] if len(parts) == 1 else jnp.concatenate(parts, axis=1)


def as_column(row):
    return jnp.transpose(jnp.broadcast_to(row, (HD, row.shape[1])))


def row_sums(folded):
    return jnp.sum(jnp.transpose(folded), axis=0, keepdims=True)


def pack_kernel(x_ref, gain_ref, out_ref):
    tokens = x_ref.shape[0]
    wide = x_ref[...].astype(F32)
    out_ref[:tokens, :] = (wide * gain_ref[...]).astype(BF16)
    squares = wide * wide
    folded = squares[:, :HD]
    for start in range(HD, squares.shape[1], HD):
        folded = folded + squares[:, start : start + HD]
    out_ref[tokens:, :] = stat_rows(row_sums(folded), out_ref.shape[1])


def listed(ints_ref, which, b, shape, dim):
    z = ints_ref[48 + which]
    block = lax.shift_right_logical(
        lax.broadcasted_iota(jnp.int32, shape, dim), BLK.bit_length() - 1
    )
    return (block == ints_ref[z * 6 + b * 2]) | (block == ints_ref[z * 6 + b * 2 + 1])


def contract(left, right, left_dim, right_dim):
    return lax.dot_general(
        left, right, (((left_dim,), (right_dim,)), ((), ())), preferred_element_type=F32
    )


def softmax(scores, mask, axis):
    scores = jnp.where(mask, scores * (1.0 / math.sqrt(HD)), -1e30)
    expd = jnp.exp(scores - jnp.max(scores, axis=axis, keepdims=True))
    return expd * (1.0 / jnp.sum(expd, axis=axis, keepdims=True))


def partial_product(ints_ref, at, mine_ref, other_ref, w_ref, tokens):
    count, _, local = mine_ref.shape
    both = [(ref, i) for i in range(count) for ref in (mine_ref, other_ref)]
    x_all = jnp.concatenate([ref[i, :tokens, :] for ref, i in both], axis=1)
    places = [ints_ref[50 + side * 8 + at + i] for i in range(count) for side in range(2)]
    parts = []
    for j in range(3):
        w_all = jnp.concatenate(
            [w_ref[j, pl.ds(pl.multiple_of(p * local, local), local), :] for p in places], axis=0
        )
        parts.append(jnp.dot(x_all, w_all, preferred_element_type=F32))
    stats = sum(ref[i, tokens:, :].astype(F32) for ref, i in both)
    return parts, stats


def first_kernel(ints_ref, mine_ref, other_ref, w_ref, acc_ref, stat_ref):
    tokens = acc_ref.shape[0]
    local = mine_ref.shape[2]
    parts, stats = partial_product(ints_ref, 0, mine_ref, other_ref, w_ref, tokens)
    for j, part in enumerate(parts):
        acc_ref[:, j * local : (j + 1) * local] = part
    stat_ref[...] = stats


def finish_product(ints_ref, first_ref, stat_ref, mine_ref, other_ref, w_ref, acc_ref, proj_ref):
    tokens = first_ref.shape[0]
    local = mine_ref.shape[2]
    parts, stats = partial_product(ints_ref, 4, mine_ref, other_ref, w_ref, tokens)
    width = 2 * CHIPS * local
    scale = lax.rsqrt(as_column(stat_row(stat_ref[...] + stats, tokens)) / width + EPS)
    for j, part in enumerate(parts):
        for start in range(0, local, HD):
            cols = slice(j * local + start, j * local + start + HD)
            whole = first_ref[:, cols] + part[:, start : start + HD]
            if acc_ref is not None:
                acc_ref[:, cols] = whole
            proj_ref[:, cols] = (scale * whole).astype(BF16)
    return scale


def forward_kernel(
    ints_ref, first_ref, stat_ref, mine_ref, other_ref, w_ref, x_ref, out_ref, proj_ref
):
    tokens, local = x_ref.shape
    finish_product(ints_ref, first_ref, stat_ref, mine_ref, other_ref, w_ref, None, proj_ref)
    for b in range(tokens // BLK):
        rows = slice(b * BLK, (b + 1) * BLK)
        mask = listed(ints_ref, 0, b, (BLK, tokens), 1)
        for h in range(local // HD):
            at = h * HD
            key_in = proj_ref[:, local + at : local + at + HD]
            value = proj_ref[:, 2 * local + at : 2 * local + at + HD]
            scores = contract(proj_ref[rows, at : at + HD], key_in, 1, 1)
            probs = softmax(scores, mask, 1)
            attn = jnp.dot(probs.astype(BF16), value, preferred_element_type=F32)
            out_ref[rows, at : at + HD] = (x_ref[rows, at : at + HD].astype(F32) + attn).astype(
                BF16
            )


def backward_kernel(
    ints_ref,
    first_ref,
    stat_ref,
    mine_ref,
    other_ref,
    w_ref,
    c_ref,
    out_ref,
    scale_ref,
    acc_ref,
    proj_ref,
    p_ref,
    s_ref,
):
    tokens, local = c_ref.shape
    scale = finish_product(
        ints_ref, first_ref, stat_ref, mine_ref, other_ref, w_ref, acc_ref, proj_ref
    )
    scale_ref[...] = scale
    folded = jnp.zeros((tokens, HD), F32)
    masks = [listed(ints_ref, 1, b, (tokens, BLK), 0) for b in range(tokens // BLK)]
    for h in range(local // HD):
        at = h * HD
        query = proj_ref[:, at : at + HD]
        key_in = proj_ref[:, local + at : local + at + HD]
        value = proj_ref[:, 2 * local + at : 2 * local + at + HD]
        upstream = c_ref[:, at : at + HD]
        for b, mask in enumerate(masks):
            cols = slice(b * BLK, (b + 1) * BLK)
            probs = softmax(contract(key_in, query[cols], 1, 1), mask, 0)
            grad_p = contract(value, upstream[cols], 1, 1)
            inner = jnp.sum(probs * grad_p, axis=0, keepdims=True)
            p_ref[:, cols] = probs.astype(BF16)
            s_ref[:, cols] = (probs * (grad_p - inner) * (1.0 / math.sqrt(HD))).astype(BF16)
        grad_s = s_ref[...]
        parts = (
            contract(grad_s, key_in, 0, 0),
            jnp.dot(grad_s, query, preferred_element_type=F32),
            jnp.dot(p_ref[...], upstream, preferred_element_type=F32),
        )
        for j, part in enumerate(parts):
            cols = slice(j * local + at, j * local + at + HD)
            grads = (scale * part).astype(BF16)
            out_ref[:tokens, cols] = grads
            folded = folded + grads.astype(F32) * acc_ref[:, cols]
    out_ref[tokens:, :] = stat_rows(row_sums(folded), out_ref.shape[1])


def input_grad_kernel(places, ints_ref, mine_ref, other_ref, w_mine_ref, w_other_ref, *out_refs):
    tokens = mine_ref.shape[0] - STAT
    local = out_refs[0].shape[1]
    grads = jnp.concatenate([mine_ref[:tokens, :], other_ref[:tokens, :]], axis=1)
    totals = stat_row(mine_ref[tokens:, :].astype(F32) + other_ref[tokens:, :].astype(F32), tokens)
    stats = stat_rows(totals, local)
    for place, ref in zip(places, out_refs):
        rows = pl.ds(pl.multiple_of(ints_ref[50 + place] * local, local), local)
        w_all = jnp.concatenate(
            [w[j, rows, :] for w in (w_mine_ref, w_other_ref) for j in range(3)], axis=1
        )
        ref[:tokens, :] = contract(grads, w_all, 1, 1).astype(BF16)
        ref[tokens:, :] = stats


def weight_grad_kernel(ints_ref, mine_ref, other_ref, more_ref, rest_ref, g_ref, out_ref):
    tokens = g_ref.shape[0] - STAT
    local = mine_ref.shape[2]
    side = ints_ref[66]
    step = pl.program_id(0)
    grads = g_ref[:tokens, :]

    def add(ref, at, i):
        part = contract(ref[i, :tokens, :], grads, 0, 0)
        for j in range(3):
            out_ref[j, pl.ds(pl.multiple_of(at * local, local), local), :] = part[
                :, j * local : (j + 1) * local
            ].astype(BF16)

    half = mine_ref.shape[0]

    @pl.when(step < half)
    def _():
        add(mine_ref, side, step)
        add(other_ref, 1 - side, step)

    @pl.when(step >= half)
    def _():
        add(more_ref, side, step - half)
        add(rest_ref, 1 - side, step - half)


def weight_grad(ints, blocks, grads):
    chips, rows, local = 2 * blocks[0].shape[0], *blocks[0].shape[1:]
    whole = lambda a: pl.BlockSpec(a.shape, lambda d, ints: (0,) * a.ndim)
    return pl.pallas_call(
        weight_grad_kernel,
        out_shape=jax.ShapeDtypeStruct((3, 2 * chips * local, local), BF16),
        grid_spec=pltpu.PrefetchScalarGridSpec(
            num_scalar_prefetch=1,
            grid=(chips,),
            in_specs=[whole(a) for a in (*blocks, grads)],
            out_specs=pl.BlockSpec((3, 2 * local, local), lambda d, ints: (0, ints[67 + d], 0)),
        ),
        compiler_params=pltpu.CompilerParams(vmem_limit_bytes=VMEM_BYTES),
        cost_estimate=cost(7.0),
        name="weight_grad",
    )(ints, *blocks, grads)


def finish_kernel(*refs):
    blocks, (x_ref, c_ref, gain_ref, scale_ref, dx_ref, gg_ref) = refs[:CHIPS], refs[CHIPS:]
    tokens, local = x_ref.shape
    own_in = blocks[0][:tokens, :].astype(F32)
    stats = blocks[0][tokens:, :].astype(F32)
    for ref in blocks[1:]:
        own_in = own_in + ref[:tokens, :].astype(F32)
        stats = stats + ref[tokens:, :].astype(F32)
    total = as_column(stat_row(stats, tokens))
    scale = scale_ref[...]
    factor = scale * scale * total / (2 * CHIPS * local)
    x_wide = x_ref[...].astype(F32)
    for start in range(0, local, HD):
        cols = slice(start, start + HD)
        grad_x = c_ref[:, cols].astype(F32) + gain_ref[:, cols] * own_in[:, cols]
        dx_ref[:, cols] = (grad_x - factor * x_wide[:, cols]).astype(BF16)
    gg_ref[...] = jnp.sum(x_wide * own_in, axis=0, keepdims=True)


def cost(us):
    return pl.CostEstimate(flops=int(us * 1.1e9), transcendentals=0, bytes_accessed=0)


def plain_call(kernel, out_shape, name, us, *args, scratch=()):
    vmem = pl.BlockSpec(memory_space=pltpu.VMEM)
    specs = [
        pl.BlockSpec(memory_space=pltpu.SMEM) if a.dtype == jnp.int32 else vmem for a in args
    ]
    return pl.pallas_call(
        kernel,
        out_shape=out_shape,
        in_specs=specs,
        out_specs=jax.tree.map(lambda s: vmem, out_shape),
        scratch_shapes=list(scratch),
        compiler_params=pltpu.CompilerParams(vmem_limit_bytes=VMEM_BYTES),
        cost_estimate=cost(us),
        name=name,
    )(*args)


def to_chip(block, distance):
    route = [(i, ((i >> 1) ^ distance) << 1 | (i & 1)) for i in range(2 * CHIPS)]
    return lax.ppermute(block, "fsdp", route)


def to_core(block):
    return lax.ppermute(block, "fsdp", [(i, i ^ 1) for i in range(2 * CHIPS)])


def shifted(block, axis, distance):
    count = lax.axis_size(axis)
    return lax.ppermute(block, axis, [((i - distance) % count, i) for i in range(count)])


NEAR = (0, 4, 1, 3)
FAR = (2, 5, 7, 6)
SPLIT = 208
tie = lax.optimization_barrier


def near(block):
    return [block] + [to_chip(block, d) for d in NEAR[1:]]


def far(blocks):
    _, by_x, by_1, by_3 = blocks
    return to_chip(by_3, 1), to_chip(by_1, 4), to_chip(by_x, 3)


def last(blocks):
    at_2, _, at_7 = blocks
    return jnp.concatenate([to_chip(at_2[:SPLIT], 4), to_chip(at_7[SPLIT:], 1)])


def on_device(x_fwd, x_saved, cotangent, qkv_weight, gain, block_lists, plan):
    forward_in = x_fwd[0]
    saved_in = x_saved[0]
    upstream = cotangent[0]
    weight = jnp.transpose(qkv_weight[0], (1, 0, 2))
    tokens, local = forward_in.shape
    me = lax.axis_index("fsdp").astype(jnp.int32)
    chip, side = me // 2, me % 2
    apart = jnp.array(NEAR + FAR, dtype=jnp.int32) ^ chip
    ints = jnp.concatenate(
        [
            block_lists.reshape(-1),
            plan.reshape(-1),
            apart * 2 + side,
            apart * 2 + 1 - side,
            side[None],
            apart,
        ]
    )
    block = jax.ShapeDtypeStruct((tokens + STAT, local), BF16)
    wide = jax.ShapeDtypeStruct((tokens, 3 * local), F32)
    stat = jax.ShapeDtypeStruct((STAT, local), F32)
    narrow = jax.ShapeDtypeStruct((tokens, local), BF16)
    proj = pltpu.VMEM((tokens, 3 * local), BF16)

    pay_bwd = plain_call(pack_kernel, block, "pack_bwd", 1.0, saved_in, gain)
    pay_fwd = plain_call(pack_kernel, block, "pack_fwd", 1.0, forward_in, gain)
    w_other = to_core(weight)

    near_bwd = near(pay_bwd)
    mine_a = jnp.stack(near_bwd)
    other_a = to_core(mine_a)
    far_bwd = far(near_bwd)
    first, first_stat = plain_call(
        first_kernel, (wide, stat), "first_bwd", 2.5, ints, mine_a, other_a, weight
    )
    far_bwd, w_other, pay_fwd = tie((far_bwd, w_other, pay_fwd))
    mine_b = jnp.stack([*far_bwd, last(far_bwd)])
    near_fwd = near(pay_fwd)
    other_b = to_core(mine_b)
    grads, scale = plain_call(
        backward_kernel,
        (
            jax.ShapeDtypeStruct((tokens + STAT, 3 * local), BF16),
            jax.ShapeDtypeStruct((tokens, HD), F32),
        ),
        "backward",
        6.0,
        ints,
        first,
        first_stat,
        mine_b,
        other_b,
        weight,
        upstream,
        scratch=[
            pltpu.VMEM((tokens, 3 * local), F32),
            proj,
            pltpu.VMEM((tokens, tokens), BF16),
            pltpu.VMEM((tokens, tokens), BF16),
        ],
    )
    far_fwd = far(near_fwd)
    grads_other = to_core(grads)
    gone = []
    for name, places in (("input_grad_far", (7, 6, 5, 4)), ("input_grad_near", (1, 2, 3, 0))):
        parts = plain_call(
            functools.partial(input_grad_kernel, places),
            [block] * 4,
            name,
            2.0,
            ints,
            grads,
            grads_other,
            weight,
            w_other,
        )
        for place, part in zip(places, parts):
            gone.append(to_chip(part, (NEAR + FAR)[place]) if place else part)

    mine_fa = jnp.stack(near_fwd)
    mine_fb = jnp.stack([*far_fwd, last(far_fwd)])
    other_fa, other_fb = to_core(mine_fa), to_core(mine_fb)
    first_f, stat_f = plain_call(
        first_kernel, (wide, stat), "first_fwd", 2.5, ints, mine_fa, other_fa, weight
    )
    result = plain_call(
        forward_kernel,
        narrow,
        "forward",
        4.0,
        ints,
        first_f,
        stat_f,
        mine_fb,
        other_fb,
        weight,
        forward_in,
        scratch=[proj],
    )
    sent_on = shifted(result, "section", 1)
    grad_w = weight_grad(ints, (mine_a, other_a, mine_b, other_b), grads)
    grad_x, grad_gain = plain_call(
        finish_kernel,
        (narrow, jax.ShapeDtypeStruct((1, local), F32)),
        "finish",
        1.0,
        *gone,
        saved_in,
        upstream,
        gain,
        scale,
    )
    sent_back = shifted(grad_x, "section", -1)
    return (sent_on[None], sent_back[None], jnp.transpose(grad_w, (1, 0, 2))[None], grad_gain)


def solution(mesh):
    in_specs = (
        P("section", None, "fsdp"),
        P("section", None, "fsdp"),
        P("section", None, "fsdp"),
        P("section", None, None, "fsdp"),
        P("section", "fsdp"),
        P(),
        P("section", None),
    )
    out_specs = (
        P("section", None, "fsdp"),
        P("section", None, "fsdp"),
        P("section", None, None, "fsdp"),
        P("section", "fsdp"),
    )
    return jax.shard_map(
        on_device, mesh=mesh, in_specs=in_specs, out_specs=out_specs, check_vma=False
    )
```

time: 156 us -> 106 us (0.68); the launches traced: 153 us -> 106 us
  waiting for transfers between devices: 51 us -> 18.6 us
  Pallas kernels: 36.2 us -> 29.9 us
  local copies, waits for them, and re-layouts: 13.4 us -> 7.7 us
  starting transfers between devices: 51.5 us -> 46.8 us
  other arithmetic: 0.01 us -> 1.64 us
    ppermute x21 -> x23, waiting for transfers between devices: 48.9 us -> 18.6 us  [to_chip(): return lax.ppermute(block, 'fsdp', route)]
    ppermute x21 -> x23, starting transfers between devices: 41.8 us -> 35.2 us  [to_chip(): return lax.ppermute(block, 'fsdp', route)]
    pallas_call x6 -> x9, Pallas kernels: 29.1 us -> 22.6 us  [plain_call(): pl.pallas_call(kernel, out_shape=out_shape, in_specs=specs, out_specs=jax...]
    unnamed x45 -> x33, local copies, waits for them, and re-layouts: 12.5 us -> 7.48 us
    ppermute x2, starting transfers between devices: 9.06 us -> 11.1 us  [shifted(): lax.ppermute(block, axis, [((i - distance) % count, i) for i in range(cou...]
    ppermute x4 -> x6, waiting for transfers between devices: 2.03 us -> 0.02 us  [to_core(): return lax.ppermute(block, 'fsdp', [(i, i ^ 1) for i in range(2 * CHIPS)])]
    another operation x0 -> x6, other arithmetic: none -> 1.63 us  [the longest x1 1.28 us: on_device(): mine_fa = jnp.stack(near_fwd)]
  transfers between devices with their start and end apart: 27 -> 31, of which waited for: 9 -> 10; matrix products, arithmetic and copies ran while one was open for 4% -> 2% of each run, Pallas kernels for 24% -> 28%
where the time goes in v2:
time: 106 us
  starting transfers between devices  46.8 us (44%)
  Pallas kernels  29.9 us (28%)
  waiting for transfers between devices  18.6 us (18%)
  local copies, waits for them, and re-layouts  7.7 us (7%)
  other arithmetic  1.64 us (2%)
    ppermute x23, starting transfers between devices, to_chip(): return lax.ppermute(block, 'fsdp', route)  35.2 us
    pallas_call x9, Pallas kernels, plain_call(): pl.pallas_call(kernel, out_shape=out_shape, in_specs=specs, out_specs=jax...  22.6 us
    ppermute x23, waiting for transfers between devices, to_chip(): return lax.ppermute(block, 'fsdp', route)  18.6 us
    ppermute x2, starting transfers between devices, shifted(): lax.ppermute(block, axis, [((i - distance) % count, i) for i in range(cou...  11.1 us
    unnamed x33, local copies, waits for them, and re-layouts  7.48 us
    pallas_call x1, Pallas kernels, weight_grad(): pl.pallas_call(weight_grad_kernel, out_shape=jax.ShapeDtypeStruct((3, 2 *...  7.3 us
  transfers between devices with their start and end apart: 31, of which 10 were waited for; matrix products, arithmetic and copies ran while one was open for 2% of the time, Pallas kernels for 28%

profile of v2, /device:TPU:8, one launch (start us, length us, event | category | flops | bytes accessed | tf_op | source)
XLA Modules:
  0.0 105.6 jit_solution(5233579153846359025)
XLA Ops:
  0.7 0.1 collective-permute-start.6
  0.8 0.9 copy-done.3
  1.7 0.7 copy-done.6
  2.4 0.1 pack_bwd.1
  2.5 1.7 %collective-permute-start = (bf16[400,256]{1,0:T(8,128)(2,1)S(1)}, bf16[400,256]{1,0:T(8,128)(2,1)S(1)}, u32[]{:S(2)}, u32[]{:S(2)}) collective-permute-start(bf16[400,256]{1,0:T(8,128)(2,1)S(1)} %pack_bwd.1), channel_id=1, source_target_pairs={{0,6},{1,7},{2,4},{3,5},{4,2},{5,3},{6,0},{7,1},{8,14},{9,15},{10,... | collective-permute-start | bytes 614408 | tf_op jit(solution)/shard_map/ppermute | solution.py:302
  4.2 1.9 %collective-permute-start.2 = (bf16[400,256]{1,0:T(8,128)(2,1)S(1)}, bf16[400,256]{1,0:T(8,128)(2,1)S(1)}, u32[]{:S(2)}, u32[]{:S(2)}) collective-permute-start(bf16[400,256]{1,0:T(8,128)(2,1)S(1)} %pack_bwd.1), channel_id=1, source_target_pairs={{0,2},{1,3},{2,0},{3,1},{4,6},{5,7},{6,4},{7,5},{8,10},{9,11},{10,... | collective-permute-start | bytes 614408 | tf_op jit(solution)/shard_map/ppermute | solution.py:302
  6.1 1.5 %collective-permute-start.4 = (bf16[400,256]{1,0:T(8,128)(2,1)S(1)}, bf16[400,256]{1,0:T(8,128)(2,1)S(1)}, u32[]{:S(2)}, u32[]{:S(2)}) collective-permute-start(bf16[400,256]{1,0:T(8,128)(2,1)S(1)} %pack_bwd.1), channel_id=1, source_target_pairs={{0,8},{1,9},{2,10},{3,11},{4,12},{5,13},{6,14},{7,15},{8,0},{9,1},... | collective-permute-start | bytes 614408 | tf_op jit(solution)/shard_map/ppermute | solution.py:302
  7.6 2.5 %collective-permute-done = bf16[400,256]{1,0:T(8,128)(2,1)S(1)} collective-permute-done((bf16[400,256]{1,0:T(8,128)(2,1)S(1)}, bf16[400,256]{1,0:T(8,128)(2,1)S(1)}, u32[]{:S(2)}, u32[]{:S(2)}) %collective-permute-start) | collective-permute-done | bytes 204832 | tf_op jit(solution)/shard_map/ppermute | solution.py:302
  10.1 3.4 %collective-permute-start.1 = (bf16[400,256]{1,0:T(8,128)(2,1)S(1)}, bf16[400,256]{1,0:T(8,128)(2,1)S(1)}, u32[]{:S(2)}, u32[]{:S(2)}) collective-permute-start(bf16[400,256]{1,0:T(8,128)(2,1)S(1)} %collective-permute-done), channel_id=1, source_target_pairs={{0,2},{1,3},{2,0},{3,1},{4,6},{5,7},{6,4},{7,5},{8,10},{9,11},{10,... | collective-permute-start | bytes 614408 | tf_op jit(solution)/shard_map/ppermute | solution.py:302
  13.5 2.2 %collective-permute-start.5 = (bf16[400,256]{1,0:T(8,128)(2,1)S(1)}, bf16[400,256]{1,0:T(8,128)(2,1)S(1)}, u32[]{:S(2)}, u32[]{:S(2)}) collective-permute-start(bf16[400,256]{1,0:T(8,128)(2,1)S(1)} %collective-permute-done.4), channel_id=1, source_target_pairs={{0,6},{1,7},{2,4},{3,5},{4,2},{5,3},{6,0},{7,1},{8,14},{9,15},{10,... | collective-permute-start | bytes 614408 | tf_op jit(solution)/shard_map/ppermute | solution.py:302
  15.6 0.1 pad_maximum_fusion.2.mine_ref
  15.8 0.1 collective-permute-start.18
  15.9 0.9 copy-done.1
  16.8 0.7 copy-done.7
  17.5 0.1 pack_fwd.1
  17.6 0.8 collective-permute-done.1
  18.4 1.5 %collective-permute-done.3 = bf16[400,256]{1,0:T(8,128)(2,1)S(1)} collective-permute-done((bf16[400,256]{1,0:T(8,128)(2,1)S(1)}, bf16[400,256]{1,0:T(8,128)(2,1)S(1)}, u32[]{:S(2)}, u32[]{:S(2)}) %collective-permute-start.3) | collective-permute-done | bytes 204832 | tf_op jit(solution)/shard_map/ppermute | solution.py:302
  19.9 0.1 collective-permute-done.5
  20.1 1.7 %collective-permute-start.19 = (bf16[208,256]{1,0:T(8,128)(2,1)S(1)}, bf16[208,256]{1,0:T(8,128)(2,1)S(1)}, u32[]{:S(2)}, u32[]{:S(2)}) collective-permute-start(bf16[208,256]{1,0:T(8,128)(2,1)S(1)} %slice.14), channel_id=1, source_target_pairs={{0,8},{1,9},{2,10},{3,11},{4,12},{5,13},{6,14},{7,15},{8,0},{9,1},... | collective-permute-start | bytes 319496 | tf_op jit(solution)/shard_map/ppermute | solution.py:302
  21.8 1.6 %collective-permute-start.20 = (bf16[192,256]{1,0:T(8,128)(2,1)S(1)}, bf16[192,256]{1,0:T(8,128)(2,1)S(1)}, u32[]{:S(2)}, u32[]{:S(2)}) collective-permute-start(bf16[192,256]{1,0:T(8,128)(2,1)S(1)} %slice.15), channel_id=1, source_target_pairs={{0,2},{1,3},{2,0},{3,1},{4,6},{5,7},{6,4},{7,5},{8,10},{9,11},{10,... | collective-permute-start | bytes 294920 | tf_op jit(solution)/shard_map/ppermute | solution.py:302
  23.3 3.1 %collective-permute-done.20 = bf16[192,256]{1,0:T(8,128)(2,1)S(1)} collective-permute-done((bf16[192,256]{1,0:T(8,128)(2,1)S(1)}, bf16[192,256]{1,0:T(8,128)(2,1)S(1)}, u32[]{:S(2)}, u32[]{:S(2)}) %collective-permute-start.20) | collective-permute-done | bytes 98336 | tf_op jit(solution)/shard_map/ppermute | solution.py:302
  26.5 0.1 pad_maximum_fusion.3.mine_ref.more_ref
  26.6 0.1 collective-permute-start.21
  26.7 0.1 copy.13
  26.8 0.1 reshape.14
  26.9 0.8 collective-permute-start.9
  27.7 1.5 %collective-permute-start.7 = (bf16[400,256]{1,0:T(8,128)(2,1)S(1)}, bf16[400,256]{1,0:T(8,128)(2,1)}, u32[]{:S(2)}, u32[]{:S(2)}) collective-permute-start(bf16[400,256]{1,0:T(8,128)(2,1)S(1)} %pack_fwd.1), channel_id=1, source_target_pairs={{0,8},{1,9},{2,10},{3,11},{4,12},{5,13},{6,14},{7,15},{8,0},{9,1},... | collective-permute-start | bytes 614408 | tf_op jit(solution)/shard_map/ppermute | solution.py:302
  29.2 0.1 concatenate.9.ints_ref
  29.3 2.1 %collective-permute-start.8 = (bf16[400,256]{1,0:T(8,128)(2,1)S(1)}, bf16[400,256]{1,0:T(8,128)(2,1)S(1)}, u32[]{:S(2)}, u32[]{:S(2)}) collective-permute-start(bf16[400,256]{1,0:T(8,128)(2,1)S(1)} %pack_fwd.1), channel_id=1, source_target_pairs={{0,2},{1,3},{2,0},{3,1},{4,6},{5,7},{6,4},{7,5},{8,10},{9,11},{10,... | collective-permute-start | bytes 614408 | tf_op jit(solution)/shard_map/ppermute | solution.py:302
  31.4 3.6 %collective-permute-done.7 = bf16[400,256]{1,0:T(8,128)(2,1)} collective-permute-done((bf16[400,256]{1,0:T(8,128)(2,1)S(1)}, bf16[400,256]{1,0:T(8,128)(2,1)}, u32[]{:S(2)}, u32[]{:S(2)}) %collective-permute-start.7) | collective-permute-done | bytes 204832 | tf_op jit(solution)/shard_map/ppermute | solution.py:302
  35.0 1.4 %collective-permute-start.13 = (bf16[400,256]{1,0:T(8,128)(2,1)}, bf16[400,256]{1,0:T(8,128)(2,1)S(1)}, u32[]{:S(2)}, u32[]{:S(2)}) collective-permute-start(bf16[400,256]{1,0:T(8,128)(2,1)} %collective-permute-done.7), channel_id=1, source_target_pairs={{0,6},{1,7},{2,4},{3,5},{4,2},{5,3},{6,0},{7,1},{8,14},{9,15},{10,... | collective-permute-start | bytes 614408 | tf_op jit(solution)/shard_map/ppermute | solution.py:302
  36.4 2.7 %collective-permute-start.11 = (bf16[400,256]{1,0:T(8,128)(2,1)}, bf16[400,256]{1,0:T(8,128)(2,1)S(1)}, u32[]{:S(2)}, u32[]{:S(2)}) collective-permute-start(bf16[400,256]{1,0:T(8,128)(2,1)} %collective-permute-done.9), channel_id=1, source_target_pairs={{0,2},{1,3},{2,0},{3,1},{4,6},{5,7},{6,4},{7,5},{8,10},{9,11},{10,... | collective-permute-start | bytes 614408 | tf_op jit(solution)/shard_map/ppermute | solution.py:302
  39.1 2.8 %copy-done = bf16[1,4096,3,256]{3,1,2,0:T(8,128)(2,1)S(1)} copy-done((bf16[1,4096,3,256]{3,1,2,0:T(8,128)(2,1)S(1)}, bf16[1,4096,3,256]{3,1,2,0:T(8,128)(2,1)}, u32[]{:S(2)}) %copy-start) | copy-done | bytes 6291480
  41.8 1.9 %first_bwd.1 = (f32[384,768]{1,0:T(8,128)S(1)}, f32[16,256]{1,0:T(8,128)S(1)}) custom-call(s32[75]{0:T(128)S(1)} %concatenate.9.ints_ref, bf16[4,400,256]{2,1,0:T(8,128)(2,1)S(1)} %pad_maximum_fusion.2.mine_ref, bf16[4,400,256]{2,1,0:T(8,128)(2,1)S(1)} %collective-permute-done.18.other_ref, bf16[3,4096,256]{2,1,0:T(8,128)(2,1)S(1)} %bitcast.32), custom_call_target="tpu_custom_call" | custom-call | flops 2750000128 | tf_op jit(solution)/shard_map/first_bwd/pallas_call | solution.py:288
  43.8 0.0 slice-start
  43.8 1.3 %pad_maximum_fusion.mine_ref = bf16[4,400,256]{2,1,0:T(8,128)(2,1)S(1)} fusion(bf16[1,400,256]{2,1,0:T(8,128)(2,1)} %bitcast.9, bf16[1,400,256]{2,1,0:T(8,128)(2,1)S(1)} %bitcast.52, bf16[1,400,256]{2,1,0:T(8,128)(2,1)} %bitcast.7, bf16[1,400,256]{2,1,0:T(8,128)(2,1)S(1)} %bitcast.40), kind=kLoop, calls=%fused_computation | loop fusion | flops 1228800 | bytes 1638400 | tf_op jit(solution)/shard_map/stack | solution.py:414
  45.1 0.1 collective-permute-start.10
  45.2 1.0 collective-permute-start.12
  46.3 0.3 collective-permute-start.15
  46.6 1.2 %collective-permute-start.14 = (bf16[208,256]{1,0:T(8,128)(2,1)S(1)}, bf16[208,256]{1,0:T(8,128)(2,1)S(1)}, u32[]{:S(2)}, u32[]{:S(2)}) collective-permute-start(bf16[208,256]{1,0:T(8,128)(2,1)S(1)} %slice.16), channel_id=1, source_target_pairs={{0,8},{1,9},{2,10},{3,11},{4,12},{5,13},{6,14},{7,15},{8,0},{9,1},... | collective-permute-start | bytes 319496 | tf_op jit(solution)/shard_map/ppermute | solution.py:302
  47.7 4.6 %backward.1 = (bf16[400,768]{1,0:T(8,128)(2,1)S(1)}, f32[384,128]{1,0:T(8,128)S(1)}) custom-call(s32[75]{0:T(128)S(1)} %concatenate.9.ints_ref, f32[384,768]{1,0:T(8,128)S(1)} %get-tuple-element.28.first_ref, f32[16,256]{1,0:T(8,128)S(1)} %get-tuple-element.29.stat_ref, bf16[4,400,256]{2,1,0:T(8,128)(2,1)S(1)} %pad_maximum_fusion.3.mine_ref.more_ref, ...), custom_call_target="tpu_custom_call" | custom-call | flops 6600000000 | tf_op jit(solution)/shard_map/backward/pallas_call | solution.py:288
  52.3 0.1 collective-permute-start.22
  52.4 2.6 %collective-permute-done.14 = bf16[208,256]{1,0:T(8,128)(2,1)S(1)} collective-permute-done((bf16[208,256]{1,0:T(8,128)(2,1)S(1)}, bf16[208,256]{1,0:T(8,128)(2,1)S(1)}, u32[]{:S(2)}, u32[]{:S(2)}) %collective-permute-start.14) | collective-permute-done | bytes 106528 | tf_op jit(solution)/shard_map/ppermute | solution.py:302
  55.0 0.1 pad_maximum_fusion.1.mine_ref
  55.1 0.1 collective-permute-start.16
  55.3 1.9 %first_fwd.1 = (f32[384,768]{1,0:T(8,128)S(1)}, f32[16,256]{1,0:T(8,128)S(1)}) custom-call(s32[75]{0:T(128)S(1)} %concatenate.9.ints_ref, bf16[4,400,256]{2,1,0:T(8,128)(2,1)S(1)} %pad_maximum_fusion.mine_ref, bf16[4,400,256]{2,1,0:T(8,128)(2,1)S(1)} %collective-permute-done.10.other_ref, bf16[3,4096,256]{2,1,0:T(8,128)(2,1)S(1)} %bitcast.36), custom_call_target="tpu_custom_call" | custom-call | flops 2750000128 | tf_op jit(solution)/shard_map/first_fwd/pallas_call | solution.py:288
  57.2 4.2 %input_grad_far.1 = (bf16[400,256]{1,0:T(8,128)(2,1)S(1)}, bf16[400,256]{1,0:T(8,128)(2,1)S(1)}, bf16[400,256]{1,0:T(8,128)(2,1)S(1)}, bf16[400,256]{1,0:T(8,128)(2,1)S(1)}) custom-call(s32[75]{0:T(128)S(1)} %concatenate.9.ints_ref, bf16[400,768]{1,0:T(8,128)(2,1)S(1)} %get-tuple-element.33.mine_ref.g_ref, ...), custom_call_target="tpu_custom_call" | custom-call | flops 2200000000 | tf_op jit(solution)/shard_map/input_grad_far/pallas_call | solution.py:288
  61.4 1.1 %collective-permute-start.23 = (bf16[400,256]{1,0:T(8,128)(2,1)S(1)}, bf16[400,256]{1,0:T(8,128)(2,1)S(1)}, u32[]{:S(2)}, u32[]{:S(2)}) collective-permute-start(bf16[400,256]{1,0:T(8,128)(2,1)S(1)} %get-tuple-element.35), channel_id=1, source_target_pairs={{0,12},{1,13},{2,14},{3,15},{4,8},{5,9},{6,10},{7,11},{8,4},{9,5},... | collective-permute-start | bytes 614408 | tf_op jit(solution)/shard_map/ppermute | solution.py:302
  62.6 1.3 %collective-permute-start.24 = (bf16[400,256]{1,0:T(8,128)(2,1)S(1)}, bf16[400,256]{1,0:T(8,128)(2,1)S(1)}, u32[]{:S(2)}, u32[]{:S(2)}) collective-permute-start(bf16[400,256]{1,0:T(8,128)(2,1)S(1)} %get-tuple-element.36), channel_id=1, source_target_pairs={{0,14},{1,15},{2,12},{3,13},{4,10},{5,11},{6,8},{7,9},{8,6},{9,7},... | collective-permute-start | bytes 614408 | tf_op jit(solution)/shard_map/ppermute | solution.py:302
  63.9 3.6 %collective-permute-start.25 = (bf16[400,256]{1,0:T(8,128)(2,1)S(1)}, bf16[400,256]{1,0:T(8,128)(2,1)S(1)}, u32[]{:S(2)}, u32[]{:S(2)}) collective-permute-start(bf16[400,256]{1,0:T(8,128)(2,1)S(1)} %get-tuple-element.37), channel_id=1, source_target_pairs={{0,10},{1,11},{2,8},{3,9},{4,14},{5,15},{6,12},{7,13},{8,2},{9,3},... | collective-permute-start | bytes 614408 | tf_op jit(solution)/shard_map/ppermute | solution.py:302
  67.5 4.2 %input_grad_near.1 = (bf16[400,256]{1,0:T(8,128)(2,1)S(1)}, bf16[400,256]{1,0:T(8,128)(2,1)S(1)}, bf16[400,256]{1,0:T(8,128)(2,1)S(1)}, bf16[400,256]{1,0:T(8,128)(2,1)S(1)}) custom-call(s32[75]{0:T(128)S(1)} %concatenate.9.ints_ref, bf16[400,768]{1,0:T(8,128)(2,1)S(1)} %get-tuple-element.33.mine_ref.g_ref, ...), custom_call_target="tpu_custom_call" | custom-call | flops 2200000000 | tf_op jit(solution)/shard_map/input_grad_near/pallas_call | solution.py:288
  71.8 1.3 %collective-permute-start.27 = (bf16[400,256]{1,0:T(8,128)(2,1)S(1)}, bf16[400,256]{1,0:T(8,128)(2,1)S(1)}, u32[]{:S(2)}, u32[]{:S(2)}) collective-permute-start(bf16[400,256]{1,0:T(8,128)(2,1)S(1)} %get-tuple-element.39), channel_id=1, source_target_pairs={{0,8},{1,9},{2,10},{3,11},{4,12},{5,13},{6,14},{7,15},{8,0},{9,1},... | collective-permute-start | bytes 614408 | tf_op jit(solution)/shard_map/ppermute | solution.py:302
  73.1 0.6 collective-permute-done.23.refs_0_
  73.7 2.1 %collective-permute-start.28 = (bf16[400,256]{1,0:T(8,128)(2,1)S(1)}, bf16[400,256]{1,0:T(8,128)(2,1)S(1)}, u32[]{:S(2)}, u32[]{:S(2)}) collective-permute-start(bf16[400,256]{1,0:T(8,128)(2,1)S(1)} %get-tuple-element.40), channel_id=1, source_target_pairs={{0,2},{1,3},{2,0},{3,1},{4,6},{5,7},{6,4},{7,5},{8,10},{9,11},{10,... | collective-permute-start | bytes 614408 | tf_op jit(solution)/shard_map/ppermute | solution.py:302
  75.8 2.4 %collective-permute-done.24.refs_1_ = bf16[400,256]{1,0:T(8,128)(2,1)S(1)} collective-permute-done((bf16[400,256]{1,0:T(8,128)(2,1)S(1)}, bf16[400,256]{1,0:T(8,128)(2,1)S(1)}, u32[]{:S(2)}, u32[]{:S(2)}) %collective-permute-start.24) | collective-permute-done | bytes 204832 | tf_op jit(solution)/shard_map/ppermute | solution.py:302
  78.2 0.9 collective-permute-start.29
  79.1 4.5 %forward.1 = bf16[384,256]{1,0:T(8,128)(2,1)S(1)} custom-call(s32[75]{0:T(128)S(1)} %concatenate.9.ints_ref, f32[384,768]{1,0:T(8,128)S(1)} %get-tuple-element.26.first_ref, f32[16,256]{1,0:T(8,128)S(1)} %get-tuple-element.27.stat_ref, bf16[4,400,256]{2,1,0:T(8,128)(2,1)S(1)} %pad_maximum_fusion.1.mine_ref, ...), custom_call_target="tpu_custom_call" | custom-call | flops 4400000000 | tf_op jit(solution)/shard_map/forward/pallas_call | solution.py:288
  83.6 2.9 %collective-permute-start.17 = (bf16[384,256]{1,0:T(8,128)(2,1)S(1)}, bf16[384,256]{1,0:T(8,128)(2,1)S(1)}, u32[]{:S(2)}, u32[]{:S(2)}) collective-permute-start(bf16[384,256]{1,0:T(8,128)(2,1)S(1)} %forward.1), channel_id=1, source_target_pairs={{240,0},{0,16},{16,32},{32,48},{48,64},{64,80},{80,96},{96,112},{1... | collective-permute-start | bytes 589832 | tf_op jit(solution)/shard_map/ppermute | solution.py:311
  86.5 1.4 %collective-permute-done.28.refs_5_ = bf16[400,256]{1,0:T(8,128)(2,1)S(1)} collective-permute-done((bf16[400,256]{1,0:T(8,128)(2,1)S(1)}, bf16[400,256]{1,0:T(8,128)(2,1)S(1)}, u32[]{:S(2)}, u32[]{:S(2)}) %collective-permute-start.28) | collective-permute-done | bytes 204832 | tf_op jit(solution)/shard_map/ppermute | solution.py:302
  87.9 0.9 finish.1
  88.8 8.2 %collective-permute-start.30 = (bf16[384,256]{1,0:T(8,128)(2,1)S(1)}, bf16[384,256]{1,0:T(8,128)(2,1)S(1)}, u32[]{:S(2)}, u32[]{:S(2)}) collective-permute-start(bf16[384,256]{1,0:T(8,128)(2,1)S(1)} %get-tuple-element.44), channel_id=1, source_target_pairs={{16,0},{32,16},{48,32},{64,48},{80,64},{96,80},{112,96},{128,112},... | collective-permute-start | bytes 589832 | tf_op jit(solution)/shard_map/ppermute | solution.py:311
  97.0 7.3 %weight_grad.1 = bf16[3,4096,256]{2,1,0:T(8,128)(2,1)} custom-call(s32[75]{0:T(128)S(1)} %concatenate.9.ints_ref, bf16[4,400,256]{2,1,0:T(8,128)(2,1)S(1)} %pad_maximum_fusion.2.mine_ref, bf16[4,400,256]{2,1,0:T(8,128)(2,1)S(1)} %collective-permute-done.18.other_ref, bf16[4,400,256]{2,1,0:T(8,128)(2,1)S(1)} %pad_maximum_fusion.3.mine_ref.more_ref, ...), custom_call_target="tpu_custom_call" | custom-call | flops 7699999744 | tf_op jit(solution)/shard_map/weight_grad/pallas_call | solution.py:245
  104.3 0.7 copy.16
  105.0 0.7 copy.17
  (55 shorter events, 0.2 us)
Async XLA Ops:
  0.6 26.1 %copy-start.10 = (s32[8,3,2]{0,2,1:T(2,128)S(1)}, s32[8,3,2]{0,2,1:T(2,128)}, u32[]{:S(2)}) copy-start(s32[8,3,2]{0,2,1:T(2,128)} %param.13) | copy-start | bytes 580
  0.6 28.6 %copy-start.11 = (s32[1,2]{1,0:T(1,128)S(1)}, s32[1,2]{1,0:T(1,128)}, u32[]{:S(2)}) copy-start(s32[1,2]{1,0:T(1,128)} %param.14) | copy-start | bytes 28
  0.7 19.4 %collective-permute-start.6 = (bf16[3,4096,256]{2,1,0:T(8,128)(2,1)}, bf16[3,4096,256]{2,1,0:T(8,128)(2,1)S(1)}, u32[]{:S(2)}, u32[]{:S(2)}) collective-permute-start(bf16[3,4096,256]{2,1,0:T(8,128)(2,1)} %bitcast.31), channel_id=1, source_target_pairs={{0,1},{1,0},{2,3},{3,2},{4,5},{5,4},{6,7},{7,6},{8,9},{9,8},{10,11... | collective-permute-start | bytes 18874376 | tf_op jit(solution)/shard_map/ppermute | solution.py:306
  0.8 0.9 copy-start.3
  1.7 0.7 copy-start.6
  2.4 26.8 %copy-start.12 = (s32[8]{0:T(128)S(1)}, s32[8]{0:T(128)}, u32[]{:S(2)}) copy-start(s32[8]{0:T(128)} %constant.32.clone) | copy-start | bytes 100
  2.5 7.6 %collective-permute-start = (bf16[400,256]{1,0:T(8,128)(2,1)S(1)}, bf16[400,256]{1,0:T(8,128)(2,1)S(1)}, u32[]{:S(2)}, u32[]{:S(2)}) collective-permute-start(bf16[400,256]{1,0:T(8,128)(2,1)S(1)} %pack_bwd.1), channel_id=1, source_target_pairs={{0,6},{1,7},{2,4},{3,5},{4,2},{5,3},{6,0},{7,1},{8,14},{9,15},{10,... | collective-permute-start | bytes 614408 | tf_op jit(solution)/shard_map/ppermute | solution.py:302
  4.2 9.3 %collective-permute-start.2 = (bf16[400,256]{1,0:T(8,128)(2,1)S(1)}, bf16[400,256]{1,0:T(8,128)(2,1)S(1)}, u32[]{:S(2)}, u32[]{:S(2)}) collective-permute-start(bf16[400,256]{1,0:T(8,128)(2,1)S(1)} %pack_bwd.1), channel_id=1, source_target_pairs={{0,2},{1,3},{2,0},{3,1},{4,6},{5,7},{6,4},{7,5},{8,10},{9,11},{10,... | collective-permute-start | bytes 614408 | tf_op jit(solution)/shard_map/ppermute | solution.py:302
  6.1 7.4 %collective-permute-start.4 = (bf16[400,256]{1,0:T(8,128)(2,1)S(1)}, bf16[400,256]{1,0:T(8,128)(2,1)S(1)}, u32[]{:S(2)}, u32[]{:S(2)}) collective-permute-start(bf16[400,256]{1,0:T(8,128)(2,1)S(1)} %pack_bwd.1), channel_id=1, source_target_pairs={{0,8},{1,9},{2,10},{3,11},{4,12},{5,13},{6,14},{7,15},{8,0},{9,1},... | collective-permute-start | bytes 614408 | tf_op jit(solution)/shard_map/ppermute | solution.py:302
  10.1 8.3 %collective-permute-start.1 = (bf16[400,256]{1,0:T(8,128)(2,1)S(1)}, bf16[400,256]{1,0:T(8,128)(2,1)S(1)}, u32[]{:S(2)}, u32[]{:S(2)}) collective-permute-start(bf16[400,256]{1,0:T(8,128)(2,1)S(1)} %collective-permute-done), channel_id=1, source_target_pairs={{0,2},{1,3},{2,0},{3,1},{4,6},{5,7},{6,4},{7,5},{8,10},{9,11},{10,... | collective-permute-start | bytes 614408 | tf_op jit(solution)/shard_map/ppermute | solution.py:302
  13.5 6.4 %collective-permute-start.3 = (bf16[400,256]{1,0:T(8,128)(2,1)S(1)}, bf16[400,256]{1,0:T(8,128)(2,1)S(1)}, u32[]{:S(2)}, u32[]{:S(2)}) collective-permute-start(bf16[400,256]{1,0:T(8,128)(2,1)S(1)} %collective-permute-done.2), channel_id=1, source_target_pairs={{0,8},{1,9},{2,10},{3,11},{4,12},{5,13},{6,14},{7,15},{8,0},{9,1},... | collective-permute-start | bytes 614408 | tf_op jit(solution)/shard_map/ppermute | solution.py:302
  13.5 6.5 %collective-permute-start.5 = (bf16[400,256]{1,0:T(8,128)(2,1)S(1)}, bf16[400,256]{1,0:T(8,128)(2,1)S(1)}, u32[]{:S(2)}, u32[]{:S(2)}) collective-permute-start(bf16[400,256]{1,0:T(8,128)(2,1)S(1)} %collective-permute-done.4), channel_id=1, source_target_pairs={{0,6},{1,7},{2,4},{3,5},{4,2},{5,3},{6,0},{7,1},{8,14},{9,15},{10,... | collective-permute-start | bytes 614408 | tf_op jit(solution)/shard_map/ppermute | solution.py:302
  15.8 23.3 %collective-permute-start.18 = (bf16[4,400,256]{2,1,0:T(8,128)(2,1)S(1)}, bf16[4,400,256]{2,1,0:T(8,128)(2,1)S(1)}, u32[]{:S(2)}, u32[]{:S(2)}) collective-permute-start(bf16[4,400,256]{2,1,0:T(8,128)(2,1)S(1)} %pad_maximum_fusion.2.mine_ref), channel_id=1, source_target_pairs={{0,1},{1,0},{2,3},{3,2},{4,5},{5,4},{6,7},{7,6},{8,9},{9,8},{10,11... | collective-permute-start | bytes 2457608 | tf_op jit(solution)/shard_map/ppermute | solution.py:306
  15.9 0.9 copy-start.1
  16.8 0.7 copy-start.7
  20.0 6.4 %copy-start.9 = (bf16[3,4096,256]{2,1,0:T(8,128)(2,1)}, bf16[3,4096,256]{2,1,0:T(8,128)(2,1)S(1)}, u32[]{:S(2)}) copy-start(bf16[3,4096,256]{2,1,0:T(8,128)(2,1)S(1)} %collective-permute-done.6.w_other_ref) | copy-start | bytes 18874372
  20.1 6.4 %collective-permute-start.19 = (bf16[208,256]{1,0:T(8,128)(2,1)S(1)}, bf16[208,256]{1,0:T(8,128)(2,1)S(1)}, u32[]{:S(2)}, u32[]{:S(2)}) collective-permute-start(bf16[208,256]{1,0:T(8,128)(2,1)S(1)} %slice.14), channel_id=1, source_target_pairs={{0,8},{1,9},{2,10},{3,11},{4,12},{5,13},{6,14},{7,15},{8,0},{9,1},... | collective-permute-start | bytes 319496 | tf_op jit(solution)/shard_map/ppermute | solution.py:302
  21.8 4.7 %collective-permute-start.20 = (bf16[192,256]{1,0:T(8,128)(2,1)S(1)}, bf16[192,256]{1,0:T(8,128)(2,1)S(1)}, u32[]{:S(2)}, u32[]{:S(2)}) collective-permute-start(bf16[192,256]{1,0:T(8,128)(2,1)S(1)} %slice.15), channel_id=1, source_target_pairs={{0,2},{1,3},{2,0},{3,1},{4,6},{5,7},{6,4},{7,5},{8,10},{9,11},{10,... | collective-permute-start | bytes 294920 | tf_op jit(solution)/shard_map/ppermute | solution.py:302
  26.6 21.1 %collective-permute-start.21 = (bf16[4,400,256]{2,1,0:T(8,128)(2,1)S(1)}, bf16[4,400,256]{2,1,0:T(8,128)(2,1)S(1)}, u32[]{:S(2)}, u32[]{:S(2)}) collective-permute-start(bf16[4,400,256]{2,1,0:T(8,128)(2,1)S(1)} %pad_maximum_fusion.3.mine_ref.more_ref), channel_id=1, source_target_pairs={{0,1},{1,0},{2,3},{3,2},{4,5},{5,4},{6,7},{7,6},{8,9},{9,8},{10,11... | collective-permute-start | bytes 2457608 | tf_op jit(solution)/shard_map/ppermute | solution.py:306
  26.9 9.4 %collective-permute-start.9 = (bf16[400,256]{1,0:T(8,128)(2,1)S(1)}, bf16[400,256]{1,0:T(8,128)(2,1)}, u32[]{:S(2)}, u32[]{:S(2)}) collective-permute-start(bf16[400,256]{1,0:T(8,128)(2,1)S(1)} %pack_fwd.1), channel_id=1, source_target_pairs={{0,6},{1,7},{2,4},{3,5},{4,2},{5,3},{6,0},{7,1},{8,14},{9,15},{10,... | collective-permute-start | bytes 614408 | tf_op jit(solution)/shard_map/ppermute | solution.py:302
  27.7 7.3 %collective-permute-start.7 = (bf16[400,256]{1,0:T(8,128)(2,1)S(1)}, bf16[400,256]{1,0:T(8,128)(2,1)}, u32[]{:S(2)}, u32[]{:S(2)}) collective-permute-start(bf16[400,256]{1,0:T(8,128)(2,1)S(1)} %pack_fwd.1), channel_id=1, source_target_pairs={{0,8},{1,9},{2,10},{3,11},{4,12},{5,13},{6,14},{7,15},{8,0},{9,1},... | collective-permute-start | bytes 614408 | tf_op jit(solution)/shard_map/ppermute | solution.py:302
  29.3 14.5 %collective-permute-start.8 = (bf16[400,256]{1,0:T(8,128)(2,1)S(1)}, bf16[400,256]{1,0:T(8,128)(2,1)S(1)}, u32[]{:S(2)}, u32[]{:S(2)}) collective-permute-start(bf16[400,256]{1,0:T(8,128)(2,1)S(1)} %pack_fwd.1), channel_id=1, source_target_pairs={{0,2},{1,3},{2,0},{3,1},{4,6},{5,7},{6,4},{7,5},{8,10},{9,11},{10,... | collective-permute-start | bytes 614408 | tf_op jit(solution)/shard_map/ppermute | solution.py:302
  35.0 11.3 %collective-permute-start.13 = (bf16[400,256]{1,0:T(8,128)(2,1)}, bf16[400,256]{1,0:T(8,128)(2,1)S(1)}, u32[]{:S(2)}, u32[]{:S(2)}) collective-permute-start(bf16[400,256]{1,0:T(8,128)(2,1)} %collective-permute-done.7), channel_id=1, source_target_pairs={{0,6},{1,7},{2,4},{3,5},{4,2},{5,3},{6,0},{7,1},{8,14},{9,15},{10,... | collective-permute-start | bytes 614408 | tf_op jit(solution)/shard_map/ppermute | solution.py:302
  36.4 10.2 %collective-permute-start.11 = (bf16[400,256]{1,0:T(8,128)(2,1)}, bf16[400,256]{1,0:T(8,128)(2,1)S(1)}, u32[]{:S(2)}, u32[]{:S(2)}) collective-permute-start(bf16[400,256]{1,0:T(8,128)(2,1)} %collective-permute-done.9), channel_id=1, source_target_pairs={{0,2},{1,3},{2,0},{3,1},{4,6},{5,7},{6,4},{7,5},{8,10},{9,11},{10,... | collective-permute-start | bytes 614408 | tf_op jit(solution)/shard_map/ppermute | solution.py:302
  39.1 2.8 %copy-start = (bf16[1,4096,3,256]{3,1,2,0:T(8,128)(2,1)S(1)}, bf16[1,4096,3,256]{3,1,2,0:T(8,128)(2,1)}, u32[]{:S(2)}) copy-start(bf16[1,4096,3,256]{3,1,2,0:T(8,128)(2,1)} %param.11) | copy-start | bytes 18874372
  41.8 5.9 %copy-start.5 = (bf16[1,384,256]{2,1,0:T(8,128)(2,1)S(1)}, bf16[1,384,256]{2,1,0:T(8,128)(2,1)}, u32[]{:S(2)}) copy-start(bf16[1,384,256]{2,1,0:T(8,128)(2,1)} %param.10) | copy-start | bytes 589828
  43.8 11.4 %slice-start = ((s8[6291456]{0:T(1024)(128)(4,1)}), s8[4194304]{0:T(1024)(128)(4,1)S(1)}, s32[]{:S(2)}) async-start(s8[6291456]{0:T(1024)(128)(4,1)} %bitcast.34), calls=%async_computation | async-start | bytes 8388608
  45.1 10.1 %collective-permute-start.10 = (bf16[4,400,256]{2,1,0:T(8,128)(2,1)S(1)}, bf16[4,400,256]{2,1,0:T(8,128)(2,1)S(1)}, u32[]{:S(2)}, u32[]{:S(2)}) collective-permute-start(bf16[4,400,256]{2,1,0:T(8,128)(2,1)S(1)} %pad_maximum_fusion.mine_ref), channel_id=1, source_target_pairs={{0,1},{1,0},{2,3},{3,2},{4,5},{5,4},{6,7},{7,6},{8,9},{9,8},{10,11... | collective-permute-start | bytes 2457608 | tf_op jit(solution)/shard_map/ppermute | solution.py:306
  45.2 9.8 %collective-permute-start.12 = (bf16[400,256]{1,0:T(8,128)(2,1)S(1)}, bf16[400,256]{1,0:T(8,128)(2,1)S(1)}, u32[]{:S(2)}, u32[]{:S(2)}) collective-permute-start(bf16[400,256]{1,0:T(8,128)(2,1)S(1)} %collective-permute-done.8), channel_id=1, source_target_pairs={{0,8},{1,9},{2,10},{3,11},{4,12},{5,13},{6,14},{7,15},{8,0},{9,1},... | collective-permute-start | bytes 614408 | tf_op jit(solution)/shard_map/ppermute | solution.py:302
  46.3 6.1 %collective-permute-start.15 = (bf16[192,256]{1,0:T(8,128)(2,1)S(1)}, bf16[192,256]{1,0:T(8,128)(2,1)S(1)}, u32[]{:S(2)}, u32[]{:S(2)}) collective-permute-start(bf16[192,256]{1,0:T(8,128)(2,1)S(1)} %slice.17), channel_id=1, source_target_pairs={{0,2},{1,3},{2,0},{3,1},{4,6},{5,7},{6,4},{7,5},{8,10},{9,11},{10,... | collective-permute-start | bytes 294920 | tf_op jit(solution)/shard_map/ppermute | solution.py:302
  46.6 8.4 %collective-permute-start.14 = (bf16[208,256]{1,0:T(8,128)(2,1)S(1)}, bf16[208,256]{1,0:T(8,128)(2,1)S(1)}, u32[]{:S(2)}, u32[]{:S(2)}) collective-permute-start(bf16[208,256]{1,0:T(8,128)(2,1)S(1)} %slice.16), channel_id=1, source_target_pairs={{0,8},{1,9},{2,10},{3,11},{4,12},{5,13},{6,14},{7,15},{8,0},{9,1},... | collective-permute-start | bytes 319496 | tf_op jit(solution)/shard_map/ppermute | solution.py:302
  47.7 7.5 %slice-start.1 = ((s8[6291456]{0:T(1024)(128)(4,1)}), s8[2097152]{0:T(1024)(128)(4,1)S(1)}, s32[]{:S(2)}) async-start(s8[6291456]{0:T(1024)(128)(4,1)} %bitcast.34), calls=%async_computation.1 | async-start | bytes 4194304
  52.3 4.9 %collective-permute-start.22 = (bf16[400,768]{1,0:T(8,128)(2,1)S(1)}, bf16[400,768]{1,0:T(8,128)(2,1)S(1)}, u32[]{:S(2)}, u32[]{:S(2)}) collective-permute-start(bf16[400,768]{1,0:T(8,128)(2,1)S(1)} %get-tuple-element.33.mine_ref.g_ref), channel_id=1, source_target_pairs={{0,1},{1,0},{2,3},{3,2},{4,5},{5,4},{6,7},{7,6},{8,9},{9,8},{10,11... | collective-permute-start | bytes 1843208 | tf_op jit(solution)/shard_map/ppermute | solution.py:306
  55.1 16.7 %collective-permute-start.16 = (bf16[4,400,256]{2,1,0:T(8,128)(2,1)S(1)}, bf16[4,400,256]{2,1,0:T(8,128)(2,1)S(1)}, u32[]{:S(2)}, u32[]{:S(2)}) collective-permute-start(bf16[4,400,256]{2,1,0:T(8,128)(2,1)S(1)} %pad_maximum_fusion.1.mine_ref), channel_id=1, source_target_pairs={{0,1},{1,0},{2,3},{3,2},{4,5},{5,4},{6,7},{7,6},{8,9},{9,8},{10,11... | collective-permute-start | bytes 2457608 | tf_op jit(solution)/shard_map/ppermute | solution.py:306
  61.4 12.2 %collective-permute-start.23 = (bf16[400,256]{1,0:T(8,128)(2,1)S(1)}, bf16[400,256]{1,0:T(8,128)(2,1)S(1)}, u32[]{:S(2)}, u32[]{:S(2)}) collective-permute-start(bf16[400,256]{1,0:T(8,128)(2,1)S(1)} %get-tuple-element.35), channel_id=1, source_target_pairs={{0,12},{1,13},{2,14},{3,15},{4,8},{5,9},{6,10},{7,11},{8,4},{9,5},... | collective-permute-start | bytes 614408 | tf_op jit(solution)/shard_map/ppermute | solution.py:302
  62.6 15.6 %collective-permute-start.24 = (bf16[400,256]{1,0:T(8,128)(2,1)S(1)}, bf16[400,256]{1,0:T(8,128)(2,1)S(1)}, u32[]{:S(2)}, u32[]{:S(2)}) collective-permute-start(bf16[400,256]{1,0:T(8,128)(2,1)S(1)} %get-tuple-element.36), channel_id=1, source_target_pairs={{0,14},{1,15},{2,12},{3,13},{4,10},{5,11},{6,8},{7,9},{8,6},{9,7},... | collective-permute-start | bytes 614408 | tf_op jit(solution)/shard_map/ppermute | solution.py:302
  63.9 19.7 %collective-permute-start.25 = (bf16[400,256]{1,0:T(8,128)(2,1)S(1)}, bf16[400,256]{1,0:T(8,128)(2,1)S(1)}, u32[]{:S(2)}, u32[]{:S(2)}) collective-permute-start(bf16[400,256]{1,0:T(8,128)(2,1)S(1)} %get-tuple-element.37), channel_id=1, source_target_pairs={{0,10},{1,11},{2,8},{3,9},{4,14},{5,15},{6,12},{7,13},{8,2},{9,3},... | collective-permute-start | bytes 614408 | tf_op jit(solution)/shard_map/ppermute | solution.py:302
  67.5 11.6 %copy-start.2 = (bf16[1,384,256]{2,1,0:T(8,128)(2,1)S(1)}, bf16[1,384,256]{2,1,0:T(8,128)(2,1)}, u32[]{:S(2)}) copy-start(bf16[1,384,256]{2,1,0:T(8,128)(2,1)} %param.8) | copy-start | bytes 589828
  67.5 19.0 %collective-permute-start.26 = (bf16[400,256]{1,0:T(8,128)(2,1)S(1)}, bf16[400,256]{1,0:T(8,128)(2,1)S(1)}, u32[]{:S(2)}, u32[]{:S(2)}) collective-permute-start(bf16[400,256]{1,0:T(8,128)(2,1)S(1)} %get-tuple-element.38), channel_id=1, source_target_pairs={{0,4},{1,5},{2,6},{3,7},{4,0},{5,1},{6,2},{7,3},{8,12},{9,13},{10,... | collective-permute-start | bytes 614408 | tf_op jit(solution)/shard_map/ppermute | solution.py:302
  71.8 14.7 %collective-permute-start.27 = (bf16[400,256]{1,0:T(8,128)(2,1)S(1)}, bf16[400,256]{1,0:T(8,128)(2,1)S(1)}, u32[]{:S(2)}, u32[]{:S(2)}) collective-permute-start(bf16[400,256]{1,0:T(8,128)(2,1)S(1)} %get-tuple-element.39), channel_id=1, source_target_pairs={{0,8},{1,9},{2,10},{3,11},{4,12},{5,13},{6,14},{7,15},{8,0},{9,1},... | collective-permute-start | bytes 614408 | tf_op jit(solution)/shard_map/ppermute | solution.py:302
  73.7 14.2 %collective-permute-start.28 = (bf16[400,256]{1,0:T(8,128)(2,1)S(1)}, bf16[400,256]{1,0:T(8,128)(2,1)S(1)}, u32[]{:S(2)}, u32[]{:S(2)}) collective-permute-start(bf16[400,256]{1,0:T(8,128)(2,1)S(1)} %get-tuple-element.40), channel_id=1, source_target_pairs={{0,2},{1,3},{2,0},{3,1},{4,6},{5,7},{6,4},{7,5},{8,10},{9,11},{10,... | collective-permute-start | bytes 614408 | tf_op jit(solution)/shard_map/ppermute | solution.py:302
  78.2 9.7 %collective-permute-start.29 = (bf16[400,256]{1,0:T(8,128)(2,1)S(1)}, bf16[400,256]{1,0:T(8,128)(2,1)S(1)}, u32[]{:S(2)}, u32[]{:S(2)}) collective-permute-start(bf16[400,256]{1,0:T(8,128)(2,1)S(1)} %get-tuple-element.41), channel_id=1, source_target_pairs={{0,6},{1,7},{2,4},{3,5},{4,2},{5,3},{6,0},{7,1},{8,14},{9,15},{10,... | collective-permute-start | bytes 614408 | tf_op jit(solution)/shard_map/ppermute | solution.py:302
  79.1 8.8 %copy-start.4 = (bf16[1,384,256]{2,1,0:T(8,128)(2,1)S(1)}, bf16[1,384,256]{2,1,0:T(8,128)(2,1)}, u32[]{:S(2)}) copy-start(bf16[1,384,256]{2,1,0:T(8,128)(2,1)} %param.9) | copy-start | bytes 589828
  79.1 8.8 %copy-start.8 = (f32[1,256]{1,0:T(1,128)S(1)}, f32[1,256]{1,0:T(1,128)}, u32[]{:S(2)}) copy-start(f32[1,256]{1,0:T(1,128)} %refs_10_.1) | copy-start | bytes 3076
  83.6 20.7 %collective-permute-start.17 = (bf16[384,256]{1,0:T(8,128)(2,1)S(1)}, bf16[384,256]{1,0:T(8,128)(2,1)S(1)}, u32[]{:S(2)}, u32[]{:S(2)}) collective-permute-start(bf16[384,256]{1,0:T(8,128)(2,1)S(1)} %forward.1), channel_id=1, source_target_pairs={{240,0},{0,16},{16,32},{32,48},{48,64},{64,80},{80,96},{96,112},{1... | collective-permute-start | bytes 589832 | tf_op jit(solution)/shard_map/ppermute | solution.py:311
  88.8 15.5 %collective-permute-start.30 = (bf16[384,256]{1,0:T(8,128)(2,1)S(1)}, bf16[384,256]{1,0:T(8,128)(2,1)S(1)}, u32[]{:S(2)}, u32[]{:S(2)}) collective-permute-start(bf16[384,256]{1,0:T(8,128)(2,1)S(1)} %get-tuple-element.44), channel_id=1, source_target_pairs={{16,0},{32,16},{48,32},{64,48},{80,64},{96,80},{112,96},{128,112},... | collective-permute-start | bytes 589832 | tf_op jit(solution)/shard_map/ppermute | solution.py:311

commit v3 on v2

--- a/solution.py
+++ b/solution.py
@@ -15,7 +15,7 @@
 CHIPS = 8
 F32 = jnp.float32
 BF16 = jnp.bfloat16
-VMEM_BYTES = 40 << 20
+VMEM_BYTES = 16 << 20
 
 
 def pieces(row):
@@ -199,7 +199,7 @@
 
 def input_grad_kernel(places, ints_ref, mine_ref, other_ref, w_mine_ref, w_other_ref, *out_refs):
     tokens = mine_ref.shape[0] - STAT
-    local = out_refs[0].shape[1]
+    local = w_mine_ref.shape[2]
     grads = jnp.concatenate([mine_ref[:tokens, :], other_ref[:tokens, :]], axis=1)
     totals = stat_row(mine_ref[tokens:, :].astype(F32) + other_ref[tokens:, :].astype(F32), tokens)
     stats = stat_rows(totals, local)
@@ -208,61 +208,75 @@
         w_all = jnp.concatenate(
             [w[j, rows, :] for w in (w_mine_ref, w_other_ref) for j in range(3)], axis=1
         )
-        ref[:tokens, :] = contract(grads, w_all, 1, 1).astype(BF16)
-        ref[tokens:, :] = stats
-
-
-def weight_grad_kernel(ints_ref, mine_ref, other_ref, more_ref, rest_ref, g_ref, out_ref):
+        ref[:tokens, :] = contract(grads, w_all, 1, 1).astype(ref.dtype)
+        if ref.shape[0] > tokens:
+            ref[tokens:, :] = stats
+    if len(out_refs) > len(places):
+        out_refs[-1][...] = stats
+
+
+def add_kernel(pair_ref, *refs):
+    count = len(refs) // 3
+    pair = pair_ref[...].astype(F32)
+    for part, came, out in zip(refs[:count], refs[count : 2 * count], refs[2 * count :]):
+        tokens = part.shape[0]
+        out[:tokens, :] = (part[...] + came[:tokens, :].astype(F32)).astype(BF16)
+        total = stat_row(pair + came[tokens:, :].astype(F32), tokens)
+        out[tokens:, :] = stat_rows(total, out.shape[1])
+
+
+def weight_grad_kernel(
+    ints_ref, mine_ref, other_ref, more_ref, rest_ref, g_ref, out_ref, buf_ref, sem_ref
+):
     tokens = g_ref.shape[0] - STAT
-    local = mine_ref.shape[2]
+    half, _, local = mine_ref.shape
     side = ints_ref[66]
-    step = pl.program_id(0)
     grads = g_ref[:tokens, :]
 
-    def add(ref, at, i):
-        part = contract(ref[i, :tokens, :], grads, 0, 0)
-        for j in range(3):
-            out_ref[j, pl.ds(pl.multiple_of(at * local, local), local), :] = part[
-                :, j * local : (j + 1) * local
-            ].astype(BF16)
-
-    half = mine_ref.shape[0]
-
-    @pl.when(step < half)
-    def _():
-        add(mine_ref, side, step)
-        add(other_ref, 1 - side, step)
-
-    @pl.when(step >= half)
-    def _():
-        add(more_ref, side, step - half)
-        add(rest_ref, 1 - side, step - half)
+    def copy(piece, j, row):
+        return pltpu.make_async_copy(
+            buf_ref.at[piece, j], out_ref.at[j, pl.ds(row, local), :], sem_ref.at[piece, j]
+        )
+
+    copies = []
+    for s, pair in enumerate(((mine_ref, other_ref), (more_ref, rest_ref))):
+        for i in range(half):
+            for k, ref in enumerate(pair):
+                piece = (s * half + i) * 2 + k
+                place = ints_ref[67 + s * half + i] * 2 + (side if k == 0 else 1 - side)
+                part = contract(ref[i, :tokens, :], grads, 0, 0)
+                for j in range(3):
+                    buf_ref[piece, j] = part[:, j * local : (j + 1) * local].astype(BF16)
+                    copies.append(copy(piece, j, pl.multiple_of(place * local, local)))
+                    copies[-1].start()
+    for held in copies:
+        held.wait()
 
 
 def weight_grad(ints, blocks, grads):
     chips, rows, local = 2 * blocks[0].shape[0], *blocks[0].shape[1:]
-    whole = lambda a: pl.BlockSpec(a.shape, lambda d, ints: (0,) * a.ndim)
+    vmem = pl.BlockSpec(memory_space=pltpu.VMEM)
     return pl.pallas_call(
         weight_grad_kernel,
         out_shape=jax.ShapeDtypeStruct((3, 2 * chips * local, local), BF16),
-        grid_spec=pltpu.PrefetchScalarGridSpec(
-            num_scalar_prefetch=1,
-            grid=(chips,),
-            in_specs=[whole(a) for a in (*blocks, grads)],
-            out_specs=pl.BlockSpec((3, 2 * local, local), lambda d, ints: (0, ints[67 + d], 0)),
-        ),
+        in_specs=[pl.BlockSpec(memory_space=pltpu.SMEM), *([vmem] * 5)],
+        out_specs=pl.BlockSpec(memory_space=pltpu.HBM),
+        scratch_shapes=[
+            pltpu.VMEM((2 * chips, 3, local, local), BF16),
+            pltpu.SemaphoreType.DMA((2 * chips, 3)),
+        ],
         compiler_params=pltpu.CompilerParams(vmem_limit_bytes=VMEM_BYTES),
-        cost_estimate=cost(7.0),
+        cost_estimate=cost(5.0),
         name="weight_grad",
     )(ints, *blocks, grads)
 
 
-def finish_kernel(*refs):
-    blocks, (x_ref, c_ref, gain_ref, scale_ref, dx_ref, gg_ref) = refs[:CHIPS], refs[CHIPS:]
+def finish_kernel(own_ref, pair_ref, *refs):
+    blocks, (x_ref, c_ref, gain_ref, scale_ref, dx_ref, gg_ref) = refs[:-6], refs[-6:]
     tokens, local = x_ref.shape
-    own_in = blocks[0][:tokens, :].astype(F32)
-    stats = blocks[0][tokens:, :].astype(F32)
-    for ref in blocks[1:]:
+    own_in = own_ref[...]
+    stats = pair_ref[...].astype(F32)
+    for ref in blocks:
         own_in = own_in + ref[:tokens, :].astype(F32)
         stats = stats + ref[tokens:, :].astype(F32)
     total = as_column(stat_row(stats, tokens))
@@ -280,8 +294,8 @@
     return pl.CostEstimate(flops=int(us * 1.1e9), transcendentals=0, bytes_accessed=0)
 
 
-def plain_call(kernel, out_shape, name, us, *args, scratch=()):
-    vmem = pl.BlockSpec(memory_space=pltpu.VMEM)
+def plain_call(kernel, out_shape, name, us, *args, scratch=(), held=True):
+    vmem = pl.BlockSpec(memory_space=pltpu.VMEM) if held else pl.BlockSpec()
     specs = [
         pl.BlockSpec(memory_space=pltpu.SMEM) if a.dtype == jnp.int32 else vmem for a in args
     ]
@@ -313,7 +327,6 @@
 
 NEAR = (0, 4, 1, 3)
 FAR = (2, 5, 7, 6)
-SPLIT = 208
 tie = lax.optimization_barrier
 
 
@@ -323,12 +336,7 @@
 
 def far(blocks):
     _, by_x, by_1, by_3 = blocks
-    return to_chip(by_3, 1), to_chip(by_1, 4), to_chip(by_x, 3)
-
-
-def last(blocks):
-    at_2, _, at_7 = blocks
-    return jnp.concatenate([to_chip(at_2[:SPLIT], 4), to_chip(at_7[SPLIT:], 1)])
+    return [to_chip(by_3, 1), to_chip(by_1, 4), to_chip(by_x, 3)]
 
 
 def on_device(x_fwd, x_saved, cotangent, qkv_weight, gain, block_lists, plan):
@@ -356,21 +364,24 @@
     narrow = jax.ShapeDtypeStruct((tokens, local), BF16)
     proj = pltpu.VMEM((tokens, 3 * local), BF16)
 
-    pay_bwd = plain_call(pack_kernel, block, "pack_bwd", 1.0, saved_in, gain)
-    pay_fwd = plain_call(pack_kernel, block, "pack_fwd", 1.0, forward_in, gain)
+    pay_bwd = plain_call(pack_kernel, block, "pack_bwd", 1.0, saved_in, gain, held=False)
+    pay_fwd = plain_call(pack_kernel, block, "pack_fwd", 1.0, forward_in, gain, held=False)
     w_other = to_core(weight)
 
     near_bwd = near(pay_bwd)
+    pay_bwd, pay_fwd = tie((pay_bwd, pay_fwd))
+    last_bwd = to_chip(pay_bwd, FAR[-1])
+    near_bwd, pay_fwd = tie((near_bwd, pay_fwd))
     mine_a = jnp.stack(near_bwd)
     other_a = to_core(mine_a)
     far_bwd = far(near_bwd)
     first, first_stat = plain_call(
         first_kernel, (wide, stat), "first_bwd", 2.5, ints, mine_a, other_a, weight
     )
-    far_bwd, w_other, pay_fwd = tie((far_bwd, w_other, pay_fwd))
-    mine_b = jnp.stack([*far_bwd, last(far_bwd)])
-    near_fwd = near(pay_fwd)
+    last_bwd, first, w_other, pay_fwd = tie((last_bwd, first, w_other, pay_fwd))
+    mine_b = jnp.stack([*far_bwd, last_bwd])
     other_b = to_core(mine_b)
+    near_fwd, last_fwd = near(pay_fwd), to_chip(pay_fwd, FAR[-1])
     grads, scale = plain_call(
         backward_kernel,
         (
@@ -393,35 +404,50 @@
             pltpu.VMEM((tokens, tokens), BF16),
         ],
     )
+    near_fwd, last_fwd, grads = tie((near_fwd, last_fwd, grads))
+    grads_other = to_core(grads)
     far_fwd = far(near_fwd)
-    grads_other = to_core(grads)
-    gone = []
-    for name, places in (("input_grad_far", (7, 6, 5, 4)), ("input_grad_near", (1, 2, 3, 0))):
-        parts = plain_call(
+
+    def input_grads(places, grads, name, shapes):
+        return plain_call(
             functools.partial(input_grad_kernel, places),
-            [block] * 4,
+            shapes,
             name,
-            2.0,
+            3.5,
             ints,
             grads,
             grads_other,
             weight,
             w_other,
         )
-        for place, part in zip(places, parts):
-            gone.append(to_chip(part, (NEAR + FAR)[place]) if place else part)
-
+
+    for_2, for_5, for_7, for_6 = input_grads((4, 5, 6, 7), grads, "input_grad_far", [block] * 4)
+    alone = jax.ShapeDtypeStruct((tokens, local), F32)
+    later, for_7 = tie((grads, for_7))
+    *parts, own, pair = input_grads(
+        (1, 2, 3, 0),
+        later,
+        "input_grad_near",
+        [alone] * 4 + [jax.ShapeDtypeStruct((STAT, local), BF16)],
+    )
+    came = [to_chip(for_7, 3), to_chip(for_5, 4), to_chip(for_2, 1)]
+    direct = to_chip(for_6, 6)
+    far_fwd, near_fwd, pair = tie((far_fwd, near_fwd, pair))
     mine_fa = jnp.stack(near_fwd)
-    mine_fb = jnp.stack([*far_fwd, last(far_fwd)])
-    other_fa, other_fb = to_core(mine_fa), to_core(mine_fb)
+    other_fa = to_core(mine_fa)
+    mine_fb = jnp.stack([*far_fwd, last_fwd])
+    other_fb = to_core(mine_fb)
     first_f, stat_f = plain_call(
         first_kernel, (wide, stat), "first_fwd", 2.5, ints, mine_fa, other_fa, weight
     )
+    came, first_f = tie((came, first_f))
+    sums = plain_call(add_kernel, [block] * 3, "add", 1.0, pair, *parts, *came)
+    gone = [to_chip(part, d) for part, d in zip(sums, NEAR[1:])] + [direct]
     result = plain_call(
         forward_kernel,
         narrow,
         "forward",
-        4.0,
+        4.5,
         ints,
         first_f,
         stat_f,
@@ -432,12 +458,15 @@
         scratch=[proj],
     )
     sent_on = shifted(result, "section", 1)
+    gone, result = tie((gone, result))
     grad_w = weight_grad(ints, (mine_a, other_a, mine_b, other_b), grads)
     grad_x, grad_gain = plain_call(
         finish_kernel,
         (narrow, jax.ShapeDtypeStruct((1, local), F32)),
         "finish",
         1.0,
+        own,
+        pair,
         *gone,
         saved_in,
         upstream,

time: 106 us -> 93.1 us (0.88)
  starting transfers between devices: 46.8 us -> 41.9 us
  waiting for transfers between devices: 18.6 us -> 13.8 us
  Pallas kernels: 29.9 us -> 28.1 us
  other arithmetic: 1.64 us -> 0.43 us
    ppermute x23 -> x21, waiting for transfers between devices: 18.6 us -> 13.8 us  [to_chip(): return lax.ppermute(block, 'fsdp', route)]
    ppermute x23 -> x21, starting transfers between devices: 35.2 us -> 31.8 us  [to_chip(): return lax.ppermute(block, 'fsdp', route)]
    pallas_call x1, Pallas kernels: 7.3 us -> 5.18 us  [weight_grad(): pl.pallas_call(weight_grad_kernel, out_shape=jax.ShapeDtypeStruct((3, 2 *...]
    ppermute x2, starting transfers between devices: 11.1 us -> 9.13 us  [shifted(): lax.ppermute(block, axis, [((i - distance) % count, i) for i in range(cou...]
    another operation x1, other arithmetic: 1.28 us -> 0.11 us  [on_device(): mine_fa = jnp.stack(near_fwd)]
    pallas_call x9 -> x10, Pallas kernels: 22.6 us -> 22.9 us  [plain_call(): pl.pallas_call(kernel, out_shape=out_shape, in_specs=specs, out_specs=jax...]
    unnamed x33 -> x31, local copies, waits for them, and re-layouts: 7.48 us -> 7.48 us
  transfers between devices with their start and end apart: 31 -> 29, of which waited for: 10 -> 10; matrix products, arithmetic and copies ran while one was open for 2% -> 1% of each run, Pallas kernels for 28% -> 30%
where the time goes in v3:
time: 93.1 us; the launch traced here: 92.9 us
  starting transfers between devices  41.9 us (45%)
  Pallas kernels  28.1 us (30%)
  waiting for transfers between devices  13.8 us (15%)
  local copies, waits for them, and re-layouts  7.67 us (8%)
    ppermute x21, starting transfers between devices, to_chip(): return lax.ppermute(block, 'fsdp', route)  31.8 us
    pallas_call x10, Pallas kernels, plain_call(): pl.pallas_call(kernel, out_shape=out_shape, in_specs=specs, out_specs=jax...  22.9 us
    ppermute x21, waiting for transfers between devices, to_chip(): return lax.ppermute(block, 'fsdp', route)  13.8 us
    ppermute x2, starting transfers between devices, shifted(): lax.ppermute(block, axis, [((i - distance) % count, i) for i in range(cou...  9.13 us
    unnamed x31, local copies, waits for them, and re-layouts  7.48 us
    pallas_call x1, Pallas kernels, weight_grad(): pl.pallas_call(weight_grad_kernel, out_shape=jax.ShapeDtypeStruct((3, 2 *...  5.18 us
  transfers between devices with their start and end apart: 29, of which 10 were waited for; matrix products, arithmetic and copies ran while one was open for 1% of the time, Pallas kernels for 30%

profile of v3, /device:TPU:8, one launch (start us, length us, event | category | flops | bytes accessed | tf_op | source)
XLA Modules:
  0.0 92.9 jit_solution(5595623087399229642)
XLA Ops:
  0.7 0.1 collective-permute-start.5
  0.8 0.9 copy-done.3
  1.7 0.7 copy-done.6
  2.4 0.1 pack_bwd.1
  2.5 1.7 %collective-permute-start.3 = (bf16[400,256]{1,0:T(8,128)(2,1)S(1)}, bf16[400,256]{1,0:T(8,128)(2,1)S(1)}, u32[]{:S(2)}, u32[]{:S(2)}) collective-permute-start(bf16[400,256]{1,0:T(8,128)(2,1)S(1)} %pack_bwd.1), channel_id=1, source_target_pairs={{0,6},{1,7},{2,4},{3,5},{4,2},{5,3},{6,0},{7,1},{8,14},{9,15},{10,... | collective-permute-start | bytes 614408 | tf_op jit(solution)/shard_map/ppermute | solution.py:316
  4.2 1.9 %collective-permute-start.2 = (bf16[400,256]{1,0:T(8,128)(2,1)S(1)}, bf16[400,256]{1,0:T(8,128)(2,1)S(1)}, u32[]{:S(2)}, u32[]{:S(2)}) collective-permute-start(bf16[400,256]{1,0:T(8,128)(2,1)S(1)} %pack_bwd.1), channel_id=1, source_target_pairs={{0,2},{1,3},{2,0},{3,1},{4,6},{5,7},{6,4},{7,5},{8,10},{9,11},{10,... | collective-permute-start | bytes 614408 | tf_op jit(solution)/shard_map/ppermute | solution.py:316
  6.1 1.5 %collective-permute-start.1 = (bf16[400,256]{1,0:T(8,128)(2,1)S(1)}, bf16[400,256]{1,0:T(8,128)(2,1)S(1)}, u32[]{:S(2)}, u32[]{:S(2)}) collective-permute-start(bf16[400,256]{1,0:T(8,128)(2,1)S(1)} %pack_bwd.1), channel_id=1, source_target_pairs={{0,8},{1,9},{2,10},{3,11},{4,12},{5,13},{6,14},{7,15},{8,0},{9,1},... | collective-permute-start | bytes 614408 | tf_op jit(solution)/shard_map/ppermute | solution.py:316
  7.6 0.9 copy-done.1
  8.5 0.7 copy-done.7
  9.2 0.1 pack_fwd.1
  9.3 0.8 collective-permute-done.3
  10.1 1.4 %collective-permute-done.2 = bf16[400,256]{1,0:T(8,128)(2,1)S(1)} collective-permute-done((bf16[400,256]{1,0:T(8,128)(2,1)S(1)}, bf16[400,256]{1,0:T(8,128)(2,1)S(1)}, u32[]{:S(2)}, u32[]{:S(2)}) %collective-permute-start.2) | collective-permute-done | bytes 204832 | tf_op jit(solution)/shard_map/ppermute | solution.py:316
  11.5 1.5 %collective-permute-done.1 = bf16[400,256]{1,0:T(8,128)(2,1)S(1)} collective-permute-done((bf16[400,256]{1,0:T(8,128)(2,1)S(1)}, bf16[400,256]{1,0:T(8,128)(2,1)S(1)}, u32[]{:S(2)}, u32[]{:S(2)}) %collective-permute-start.1) | collective-permute-done | bytes 204832 | tf_op jit(solution)/shard_map/ppermute | solution.py:316
  13.0 0.1 pad_maximum_fusion.mine_ref
  13.1 0.1 collective-permute-start.4
  13.2 1.6 %collective-permute-start = (bf16[400,256]{1,0:T(8,128)(2,1)S(1)}, bf16[400,256]{1,0:T(8,128)(2,1)S(1)}, u32[]{:S(2)}, u32[]{:S(2)}) collective-permute-start(bf16[400,256]{1,0:T(8,128)(2,1)S(1)} %pack_bwd.1), channel_id=1, source_target_pairs={{0,12},{1,13},{2,14},{3,15},{4,8},{5,9},{6,10},{7,11},{8,4},{9,5},... | collective-permute-start | bytes 614408 | tf_op jit(solution)/shard_map/ppermute | solution.py:316
  14.8 0.1 copy.13
  14.9 0.1 reshape.14
  15.1 0.1 concatenate.3.ints_ref
  15.2 1.2 %collective-permute-start.12 = (bf16[400,256]{1,0:T(8,128)(2,1)S(1)}, bf16[400,256]{1,0:T(8,128)(2,1)S(1)}, u32[]{:S(2)}, u32[]{:S(2)}) collective-permute-start(bf16[400,256]{1,0:T(8,128)(2,1)S(1)} %collective-permute-done.1), channel_id=1, source_target_pairs={{0,6},{1,7},{2,4},{3,5},{4,2},{5,3},{6,0},{7,1},{8,14},{9,15},{10,... | collective-permute-start | bytes 614408 | tf_op jit(solution)/shard_map/ppermute | solution.py:316
  16.3 0.8 collective-permute-start.11
  17.1 2.7 %collective-permute-start.10 = (bf16[400,256]{1,0:T(8,128)(2,1)S(1)}, bf16[400,256]{1,0:T(8,128)(2,1)S(1)}, u32[]{:S(2)}, u32[]{:S(2)}) collective-permute-start(bf16[400,256]{1,0:T(8,128)(2,1)S(1)} %collective-permute-done.3), channel_id=1, source_target_pairs={{0,2},{1,3},{2,0},{3,1},{4,6},{5,7},{6,4},{7,5},{8,10},{9,11},{10,... | collective-permute-start | bytes 614408 | tf_op jit(solution)/shard_map/ppermute | solution.py:316
  19.8 2.8 %copy-done = bf16[1,4096,3,256]{3,1,2,0:T(8,128)(2,1)S(1)} copy-done((bf16[1,4096,3,256]{3,1,2,0:T(8,128)(2,1)S(1)}, bf16[1,4096,3,256]{3,1,2,0:T(8,128)(2,1)}, u32[]{:S(2)}) %copy-start) | copy-done | bytes 6291480
  22.6 1.9 %first_bwd.1 = (f32[384,768]{1,0:T(8,128)S(1)}, f32[16,256]{1,0:T(8,128)S(1)}) custom-call(s32[75]{0:T(128)S(1)} %concatenate.3.ints_ref, bf16[4,400,256]{2,1,0:T(8,128)(2,1)S(1)} %pad_maximum_fusion.mine_ref, bf16[4,400,256]{2,1,0:T(8,128)(2,1)S(1)} %collective-permute-done.4.other_ref, bf16[3,4096,256]{2,1,0:T(8,128)(2,1)S(1)} %bitcast.32), custom_call_target="tpu_custom_call" | custom-call | flops 2750000128 | tf_op jit(solution)/shard_map/first_bwd/pallas_call | solution.py:302
  24.6 2.2 %collective-permute-done.12 = bf16[400,256]{1,0:T(8,128)(2,1)S(1)} collective-permute-done((bf16[400,256]{1,0:T(8,128)(2,1)S(1)}, bf16[400,256]{1,0:T(8,128)(2,1)S(1)}, u32[]{:S(2)}, u32[]{:S(2)}) %collective-permute-start.12) | collective-permute-done | bytes 204832 | tf_op jit(solution)/shard_map/ppermute | solution.py:316
  26.7 0.7 collective-permute-done.10
  27.4 0.1 pad_maximum_fusion.1.mine_ref.more_ref
  27.5 0.1 collective-permute-start.13
  27.6 1.7 %collective-permute-start.9 = (bf16[400,256]{1,0:T(8,128)(2,1)S(1)}, bf16[400,256]{1,0:T(8,128)(2,1)S(1)}, u32[]{:S(2)}, u32[]{:S(2)}) collective-permute-start(bf16[400,256]{1,0:T(8,128)(2,1)S(1)} %pack_fwd.1), channel_id=1, source_target_pairs={{0,12},{1,13},{2,14},{3,15},{4,8},{5,9},{6,10},{7,11},{8,4},{9,5},... | collective-permute-start | bytes 614408 | tf_op jit(solution)/shard_map/ppermute | solution.py:316
  29.4 1.1 %collective-permute-start.8 = (bf16[400,256]{1,0:T(8,128)(2,1)S(1)}, bf16[400,256]{1,0:T(8,128)(2,1)S(1)}, u32[]{:S(2)}, u32[]{:S(2)}) collective-permute-start(bf16[400,256]{1,0:T(8,128)(2,1)S(1)} %pack_fwd.1), channel_id=1, source_target_pairs={{0,6},{1,7},{2,4},{3,5},{4,2},{5,3},{6,0},{7,1},{8,14},{9,15},{10,... | collective-permute-start | bytes 614408 | tf_op jit(solution)/shard_map/ppermute | solution.py:316
  30.5 1.7 %collective-permute-start.7 = (bf16[400,256]{1,0:T(8,128)(2,1)S(1)}, bf16[400,256]{1,0:T(8,128)(2,1)S(1)}, u32[]{:S(2)}, u32[]{:S(2)}) collective-permute-start(bf16[400,256]{1,0:T(8,128)(2,1)S(1)} %pack_fwd.1), channel_id=1, source_target_pairs={{0,2},{1,3},{2,0},{3,1},{4,6},{5,7},{6,4},{7,5},{8,10},{9,11},{10,... | collective-permute-start | bytes 614408 | tf_op jit(solution)/shard_map/ppermute | solution.py:316
  32.1 1.7 %collective-permute-start.6 = (bf16[400,256]{1,0:T(8,128)(2,1)S(1)}, bf16[400,256]{1,0:T(8,128)(2,1)S(1)}, u32[]{:S(2)}, u32[]{:S(2)}) collective-permute-start(bf16[400,256]{1,0:T(8,128)(2,1)S(1)} %pack_fwd.1), channel_id=1, source_target_pairs={{0,8},{1,9},{2,10},{3,11},{4,12},{5,13},{6,14},{7,15},{8,0},{9,1},... | collective-permute-start | bytes 614408 | tf_op jit(solution)/shard_map/ppermute | solution.py:316
  33.9 4.6 %backward.1 = (bf16[400,768]{1,0:T(8,128)(2,1)S(1)}, f32[384,128]{1,0:T(8,128)S(1)}) custom-call(s32[75]{0:T(128)S(1)} %concatenate.3.ints_ref, f32[384,768]{1,0:T(8,128)S(1)} %get-tuple-element.68.first_ref, f32[16,256]{1,0:T(8,128)S(1)} %get-tuple-element.69.stat_ref, bf16[4,400,256]{2,1,0:T(8,128)(2,1)S(1)} %pad_maximum_fusion.1.mine_ref.more_ref, ...), custom_call_target="tpu_custom_call" | custom-call | flops 6600000000 | tf_op jit(solution)/shard_map/backward/pallas_call | solution.py:302
  38.5 2.4 %collective-permute-done.8 = bf16[400,256]{1,0:T(8,128)(2,1)S(1)} collective-permute-done((bf16[400,256]{1,0:T(8,128)(2,1)S(1)}, bf16[400,256]{1,0:T(8,128)(2,1)S(1)}, u32[]{:S(2)}, u32[]{:S(2)}) %collective-permute-start.8) | collective-permute-done | bytes 204832 | tf_op jit(solution)/shard_map/ppermute | solution.py:316
  40.9 0.2 collective-permute-done.7
  41.1 0.0 collective-permute-start.14
  41.1 1.5 %collective-permute-start.18 = (bf16[400,256]{1,0:T(8,128)(2,1)S(1)}, bf16[400,256]{1,0:T(8,128)(2,1)S(1)}, u32[]{:S(2)}, u32[]{:S(2)}) collective-permute-start(bf16[400,256]{1,0:T(8,128)(2,1)S(1)} %collective-permute-done.8), channel_id=1, source_target_pairs={{0,2},{1,3},{2,0},{3,1},{4,6},{5,7},{6,4},{7,5},{8,10},{9,11},{10,... | collective-permute-start | bytes 614408 | tf_op jit(solution)/shard_map/ppermute | solution.py:316
  42.6 1.2 %collective-permute-start.19 = (bf16[400,256]{1,0:T(8,128)(2,1)S(1)}, bf16[400,256]{1,0:T(8,128)(2,1)S(1)}, u32[]{:S(2)}, u32[]{:S(2)}) collective-permute-start(bf16[400,256]{1,0:T(8,128)(2,1)S(1)} %collective-permute-done.7), channel_id=1, source_target_pairs={{0,8},{1,9},{2,10},{3,11},{4,12},{5,13},{6,14},{7,15},{8,0},{9,1},... | collective-permute-start | bytes 614408 | tf_op jit(solution)/shard_map/ppermute | solution.py:316
  43.9 0.9 collective-permute-start.20
  44.8 4.4 %input_grad_far.1 = (bf16[400,256]{1,0:T(8,128)(2,1)S(1)}, bf16[400,256]{1,0:T(8,128)(2,1)S(1)}, bf16[400,256]{1,0:T(8,128)(2,1)S(1)}, bf16[400,256]{1,0:T(8,128)(2,1)S(1)}) custom-call(s32[75]{0:T(128)S(1)} %concatenate.3.ints_ref, bf16[400,768]{1,0:T(8,128)(2,1)S(1)} %get-tuple-element.82.mine_ref.g_ref, ...), custom_call_target="tpu_custom_call" | custom-call | flops 3849999872 | tf_op jit(solution)/shard_map/input_grad_far/pallas_call | solution.py:302
  49.2 4.4 %input_grad_near.1 = (f32[384,256]{1,0:T(8,128)S(1)}, f32[384,256]{1,0:T(8,128)S(1)}, f32[384,256]{1,0:T(8,128)S(1)}, f32[384,256]{1,0:T(8,128)S(1)}, bf16[16,256]{1,0:T(8,128)(2,1)S(1)}) custom-call(s32[75]{0:T(128)S(1)} %concatenate.3.ints_ref, bf16[400,768]{1,0:T(8,128)(2,1)S(1)} %get-tuple-element.82.mine_ref.g_ref, ...), custom_call_target="tpu_custom_call" | custom-call | flops 3849999872 | tf_op jit(solution)/shard_map/input_grad_near/pallas_call | solution.py:302
  53.6 0.1 pad_maximum_fusion.2.mine_ref
  53.7 0.1 collective-permute-start.21
  53.8 0.1 pad_maximum_fusion.3.mine_ref
  53.9 0.6 collective-permute-start.22
  54.5 1.1 %collective-permute-start.15 = (bf16[400,256]{1,0:T(8,128)(2,1)S(1)}, bf16[400,256]{1,0:T(8,128)(2,1)S(1)}, u32[]{:S(2)}, u32[]{:S(2)}) collective-permute-start(bf16[400,256]{1,0:T(8,128)(2,1)S(1)} %get-tuple-element.75), channel_id=1, source_target_pairs={{0,6},{1,7},{2,4},{3,5},{4,2},{5,3},{6,0},{7,1},{8,14},{9,15},{10,... | collective-permute-start | bytes 614408 | tf_op jit(solution)/shard_map/ppermute | solution.py:316
  55.6 0.8 collective-permute-start.16
  56.4 1.8 %collective-permute-start.17 = (bf16[400,256]{1,0:T(8,128)(2,1)S(1)}, bf16[400,256]{1,0:T(8,128)(2,1)S(1)}, u32[]{:S(2)}, u32[]{:S(2)}) collective-permute-start(bf16[400,256]{1,0:T(8,128)(2,1)S(1)} %get-tuple-element.77), channel_id=1, source_target_pairs={{0,2},{1,3},{2,0},{3,1},{4,6},{5,7},{6,4},{7,5},{8,10},{9,11},{10,... | collective-permute-start | bytes 614408 | tf_op jit(solution)/shard_map/ppermute | solution.py:316
  58.1 1.3 %collective-permute-start.27 = (bf16[400,256]{1,0:T(8,128)(2,1)S(1)}, bf16[400,256]{1,0:T(8,128)(2,1)S(1)}, u32[]{:S(2)}, u32[]{:S(2)}) collective-permute-start(bf16[400,256]{1,0:T(8,128)(2,1)S(1)} %get-tuple-element.106), channel_id=1, source_target_pairs={{0,12},{1,13},{2,14},{3,15},{4,8},{5,9},{6,10},{7,11},{8,4},{9,5},... | collective-permute-start | bytes 614408 | tf_op jit(solution)/shard_map/ppermute | solution.py:316
  59.4 1.9 %first_fwd.1 = (f32[384,768]{1,0:T(8,128)S(1)}, f32[16,256]{1,0:T(8,128)S(1)}) custom-call(s32[75]{0:T(128)S(1)} %concatenate.3.ints_ref, bf16[4,400,256]{2,1,0:T(8,128)(2,1)S(1)} %pad_maximum_fusion.2.mine_ref, bf16[4,400,256]{2,1,0:T(8,128)(2,1)S(1)} %collective-permute-done.21.other_ref, bf16[3,4096,256]{2,1,0:T(8,128)(2,1)S(1)} %bitcast.38), custom_call_target="tpu_custom_call" | custom-call | flops 2750000128 | tf_op jit(solution)/shard_map/first_fwd/pallas_call | solution.py:302
  61.4 0.2 collective-permute-done.15.refs_3_
  61.6 2.0 %collective-permute-done.16.refs_4_ = bf16[400,256]{1,0:T(8,128)(2,1)S(1)} collective-permute-done((bf16[400,256]{1,0:T(8,128)(2,1)S(1)}, bf16[400,256]{1,0:T(8,128)(2,1)S(1)}, u32[]{:S(2)}, u32[]{:S(2)}) %collective-permute-start.16) | collective-permute-done | bytes 204832 | tf_op jit(solution)/shard_map/ppermute | solution.py:316
  63.5 2.5 %collective-permute-done.17.refs_5_ = bf16[400,256]{1,0:T(8,128)(2,1)S(1)} collective-permute-done((bf16[400,256]{1,0:T(8,128)(2,1)S(1)}, bf16[400,256]{1,0:T(8,128)(2,1)S(1)}, u32[]{:S(2)}, u32[]{:S(2)}) %collective-permute-start.17) | collective-permute-done | bytes 204832 | tf_op jit(solution)/shard_map/ppermute | solution.py:316
  66.0 0.1 add.23
  66.2 3.1 %collective-permute-start.24 = (bf16[400,256]{1,0:T(8,128)(2,1)S(1)}, bf16[400,256]{1,0:T(8,128)(2,1)S(1)}, u32[]{:S(2)}, u32[]{:S(2)}) collective-permute-start(bf16[400,256]{1,0:T(8,128)(2,1)S(1)} %get-tuple-element.103), channel_id=1, source_target_pairs={{0,8},{1,9},{2,10},{3,11},{4,12},{5,13},{6,14},{7,15},{8,0},{9,1},... | collective-permute-start | bytes 614408 | tf_op jit(solution)/shard_map/ppermute | solution.py:316
  69.3 2.5 %collective-permute-start.25 = (bf16[400,256]{1,0:T(8,128)(2,1)S(1)}, bf16[400,256]{1,0:T(8,128)(2,1)S(1)}, u32[]{:S(2)}, u32[]{:S(2)}) collective-permute-start(bf16[400,256]{1,0:T(8,128)(2,1)S(1)} %get-tuple-element.104), channel_id=1, source_target_pairs={{0,2},{1,3},{2,0},{3,1},{4,6},{5,7},{6,4},{7,5},{8,10},{9,11},{10,... | collective-permute-start | bytes 614408 | tf_op jit(solution)/shard_map/ppermute | solution.py:316
  71.8 0.0 collective-permute-start.26
  71.8 4.5 %forward.1 = bf16[384,256]{1,0:T(8,128)(2,1)S(1)} custom-call(s32[75]{0:T(128)S(1)} %concatenate.3.ints_ref, f32[384,768]{1,0:T(8,128)S(1)} %get-tuple-element.89.first_ref, f32[16,256]{1,0:T(8,128)S(1)} %get-tuple-element.90.stat_ref, bf16[4,400,256]{2,1,0:T(8,128)(2,1)S(1)} %pad_maximum_fusion.3.mine_ref, ...), custom_call_target="tpu_custom_call" | custom-call | flops 4950000128 | tf_op jit(solution)/shard_map/forward/pallas_call | solution.py:302
  76.3 2.7 %collective-permute-start.23 = (bf16[384,256]{1,0:T(8,128)(2,1)S(1)}, bf16[384,256]{1,0:T(8,128)(2,1)S(1)}, u32[]{:S(2)}, u32[]{:S(2)}) collective-permute-start(bf16[384,256]{1,0:T(8,128)(2,1)S(1)} %forward.1), channel_id=1, source_target_pairs={{240,0},{0,16},{16,32},{32,48},{48,64},{64,80},{80,96},{96,112},{1... | collective-permute-start | bytes 589832 | tf_op jit(solution)/shard_map/ppermute | solution.py:325
  79.1 0.8 finish.1
  79.9 6.4 %collective-permute-start.28 = (bf16[384,256]{1,0:T(8,128)(2,1)S(1)}, bf16[384,256]{1,0:T(8,128)(2,1)S(1)}, u32[]{:S(2)}, u32[]{:S(2)}) collective-permute-start(bf16[384,256]{1,0:T(8,128)(2,1)S(1)} %get-tuple-element.112), channel_id=1, source_target_pairs={{16,0},{32,16},{48,32},{64,48},{80,64},{96,80},{112,96},{128,112},... | collective-permute-start | bytes 589832 | tf_op jit(solution)/shard_map/ppermute | solution.py:325
  86.3 5.2 %weight_grad.1 = bf16[3,4096,256]{2,1,0:T(8,128)(2,1)} custom-call(s32[75]{0:T(128)S(1)} %concatenate.3.ints_ref, bf16[4,400,256]{2,1,0:T(8,128)(2,1)S(1)} %pad_maximum_fusion.mine_ref, bf16[4,400,256]{2,1,0:T(8,128)(2,1)S(1)} %collective-permute-done.4.other_ref, bf16[4,400,256]{2,1,0:T(8,128)(2,1)S(1)} %pad_maximum_fusion.1.mine_ref.more_ref, ...), custom_call_target="tpu_custom_call" | custom-call | flops 5500000256 | tf_op jit(solution)/shard_map/weight_grad/pallas_call | solution.py:259
  91.5 0.7 copy.16
  92.2 0.7 copy.17
  (44 shorter events, 0.1 us)
Async XLA Ops:
  0.6 14.2 %copy-start.9 = (s32[8,3,2]{0,2,1:T(2,128)S(1)}, s32[8,3,2]{0,2,1:T(2,128)}, u32[]{:S(2)}) copy-start(s32[8,3,2]{0,2,1:T(2,128)} %param.13) | copy-start | bytes 580
  0.6 14.4 %copy-start.10 = (s32[1,2]{1,0:T(1,128)S(1)}, s32[1,2]{1,0:T(1,128)}, u32[]{:S(2)}) copy-start(s32[1,2]{1,0:T(1,128)} %param.14) | copy-start | bytes 28
  0.7 23.9 %collective-permute-start.5 = (bf16[3,4096,256]{2,1,0:T(8,128)(2,1)}, bf16[3,4096,256]{2,1,0:T(8,128)(2,1)}, u32[]{:S(2)}, u32[]{:S(2)}) collective-permute-start(bf16[3,4096,256]{2,1,0:T(8,128)(2,1)} %bitcast.31), channel_id=1, source_target_pairs={{0,1},{1,0},{2,3},{3,2},{4,5},{5,4},{6,7},{7,6},{8,9},{9,8},{10,11... | collective-permute-start | bytes 18874376 | tf_op jit(solution)/shard_map/ppermute | solution.py:320
  0.8 0.9 %copy-start.3 = (bf16[1,384,256]{2,1,0:T(8,128)(2,1)S(1)}, bf16[1,384,256]{2,1,0:T(8,128)(2,1)}, u32[]{:S(2)}) copy-start(bf16[1,384,256]{2,1,0:T(8,128)(2,1)} %param.9) | copy-start | bytes 589828
  1.7 0.7 copy-start.6
  2.4 12.7 %copy-start.11 = (s32[8]{0:T(128)S(1)}, s32[8]{0:T(128)}, u32[]{:S(2)}) copy-start(s32[8]{0:T(128)} %constant.32.clone) | copy-start | bytes 100
  2.5 7.6 %collective-permute-start.3 = (bf16[400,256]{1,0:T(8,128)(2,1)S(1)}, bf16[400,256]{1,0:T(8,128)(2,1)S(1)}, u32[]{:S(2)}, u32[]{:S(2)}) collective-permute-start(bf16[400,256]{1,0:T(8,128)(2,1)S(1)} %pack_bwd.1), channel_id=1, source_target_pairs={{0,6},{1,7},{2,4},{3,5},{4,2},{5,3},{6,0},{7,1},{8,14},{9,15},{10,... | collective-permute-start | bytes 614408 | tf_op jit(solution)/shard_map/ppermute | solution.py:316
  4.2 7.3 %collective-permute-start.2 = (bf16[400,256]{1,0:T(8,128)(2,1)S(1)}, bf16[400,256]{1,0:T(8,128)(2,1)S(1)}, u32[]{:S(2)}, u32[]{:S(2)}) collective-permute-start(bf16[400,256]{1,0:T(8,128)(2,1)S(1)} %pack_bwd.1), channel_id=1, source_target_pairs={{0,2},{1,3},{2,0},{3,1},{4,6},{5,7},{6,4},{7,5},{8,10},{9,11},{10,... | collective-permute-start | bytes 614408 | tf_op jit(solution)/shard_map/ppermute | solution.py:316
  6.1 6.9 %collective-permute-start.1 = (bf16[400,256]{1,0:T(8,128)(2,1)S(1)}, bf16[400,256]{1,0:T(8,128)(2,1)S(1)}, u32[]{:S(2)}, u32[]{:S(2)}) collective-permute-start(bf16[400,256]{1,0:T(8,128)(2,1)S(1)} %pack_bwd.1), channel_id=1, source_target_pairs={{0,8},{1,9},{2,10},{3,11},{4,12},{5,13},{6,14},{7,15},{8,0},{9,1},... | collective-permute-start | bytes 614408 | tf_op jit(solution)/shard_map/ppermute | solution.py:316
  7.6 0.9 copy-start.1
  8.5 0.7 copy-start.7
  13.0 20.9 %copy-start.5 = (bf16[1,384,256]{2,1,0:T(8,128)(2,1)S(1)}, bf16[1,384,256]{2,1,0:T(8,128)(2,1)}, u32[]{:S(2)}) copy-start(bf16[1,384,256]{2,1,0:T(8,128)(2,1)} %param.10) | copy-start | bytes 589828
  13.1 4.0 %collective-permute-start.4 = (bf16[4,400,256]{2,1,0:T(8,128)(2,1)S(1)}, bf16[4,400,256]{2,1,0:T(8,128)(2,1)S(1)}, u32[]{:S(2)}, u32[]{:S(2)}) collective-permute-start(bf16[4,400,256]{2,1,0:T(8,128)(2,1)S(1)} %pad_maximum_fusion.mine_ref), channel_id=1, source_target_pairs={{0,1},{1,0},{2,3},{3,2},{4,5},{5,4},{6,7},{7,6},{8,9},{9,8},{10,11... | collective-permute-start | bytes 2457608 | tf_op jit(solution)/shard_map/ppermute | solution.py:320
  13.2 11.3 %collective-permute-start = (bf16[400,256]{1,0:T(8,128)(2,1)S(1)}, bf16[400,256]{1,0:T(8,128)(2,1)S(1)}, u32[]{:S(2)}, u32[]{:S(2)}) collective-permute-start(bf16[400,256]{1,0:T(8,128)(2,1)S(1)} %pack_bwd.1), channel_id=1, source_target_pairs={{0,12},{1,13},{2,14},{3,15},{4,8},{5,9},{6,10},{7,11},{8,4},{9,5},... | collective-permute-start | bytes 614408 | tf_op jit(solution)/shard_map/ppermute | solution.py:316
  15.2 11.5 %collective-permute-start.12 = (bf16[400,256]{1,0:T(8,128)(2,1)S(1)}, bf16[400,256]{1,0:T(8,128)(2,1)S(1)}, u32[]{:S(2)}, u32[]{:S(2)}) collective-permute-start(bf16[400,256]{1,0:T(8,128)(2,1)S(1)} %collective-permute-done.1), channel_id=1, source_target_pairs={{0,6},{1,7},{2,4},{3,5},{4,2},{5,3},{6,0},{7,1},{8,14},{9,15},{10,... | collective-permute-start | bytes 614408 | tf_op jit(solution)/shard_map/ppermute | solution.py:316
  16.3 10.4 %collective-permute-start.11 = (bf16[400,256]{1,0:T(8,128)(2,1)S(1)}, bf16[400,256]{1,0:T(8,128)(2,1)S(1)}, u32[]{:S(2)}, u32[]{:S(2)}) collective-permute-start(bf16[400,256]{1,0:T(8,128)(2,1)S(1)} %collective-permute-done.2), channel_id=1, source_target_pairs={{0,8},{1,9},{2,10},{3,11},{4,12},{5,13},{6,14},{7,15},{8,0},{9,1},... | collective-permute-start | bytes 614408 | tf_op jit(solution)/shard_map/ppermute | solution.py:316
  17.1 10.3 %collective-permute-start.10 = (bf16[400,256]{1,0:T(8,128)(2,1)S(1)}, bf16[400,256]{1,0:T(8,128)(2,1)S(1)}, u32[]{:S(2)}, u32[]{:S(2)}) collective-permute-start(bf16[400,256]{1,0:T(8,128)(2,1)S(1)} %collective-permute-done.3), channel_id=1, source_target_pairs={{0,2},{1,3},{2,0},{3,1},{4,6},{5,7},{6,4},{7,5},{8,10},{9,11},{10,... | collective-permute-start | bytes 614408 | tf_op jit(solution)/shard_map/ppermute | solution.py:316
  19.8 2.8 %copy-start = (bf16[1,4096,3,256]{3,1,2,0:T(8,128)(2,1)S(1)}, bf16[1,4096,3,256]{3,1,2,0:T(8,128)(2,1)}, u32[]{:S(2)}) copy-start(bf16[1,4096,3,256]{3,1,2,0:T(8,128)(2,1)} %param.11) | copy-start | bytes 18874372
  27.5 6.4 %collective-permute-start.13 = (bf16[4,400,256]{2,1,0:T(8,128)(2,1)S(1)}, bf16[4,400,256]{2,1,0:T(8,128)(2,1)S(1)}, u32[]{:S(2)}, u32[]{:S(2)}) collective-permute-start(bf16[4,400,256]{2,1,0:T(8,128)(2,1)S(1)} %pad_maximum_fusion.1.mine_ref.more_ref), channel_id=1, source_target_pairs={{0,1},{1,0},{2,3},{3,2},{4,5},{5,4},{6,7},{7,6},{8,9},{9,8},{10,11... | collective-permute-start | bytes 2457608 | tf_op jit(solution)/shard_map/ppermute | solution.py:320
  27.6 10.8 %collective-permute-start.9 = (bf16[400,256]{1,0:T(8,128)(2,1)S(1)}, bf16[400,256]{1,0:T(8,128)(2,1)S(1)}, u32[]{:S(2)}, u32[]{:S(2)}) collective-permute-start(bf16[400,256]{1,0:T(8,128)(2,1)S(1)} %pack_fwd.1), channel_id=1, source_target_pairs={{0,12},{1,13},{2,14},{3,15},{4,8},{5,9},{6,10},{7,11},{8,4},{9,5},... | collective-permute-start | bytes 614408 | tf_op jit(solution)/shard_map/ppermute | solution.py:316
  29.4 11.5 %collective-permute-start.8 = (bf16[400,256]{1,0:T(8,128)(2,1)S(1)}, bf16[400,256]{1,0:T(8,128)(2,1)S(1)}, u32[]{:S(2)}, u32[]{:S(2)}) collective-permute-start(bf16[400,256]{1,0:T(8,128)(2,1)S(1)} %pack_fwd.1), channel_id=1, source_target_pairs={{0,6},{1,7},{2,4},{3,5},{4,2},{5,3},{6,0},{7,1},{8,14},{9,15},{10,... | collective-permute-start | bytes 614408 | tf_op jit(solution)/shard_map/ppermute | solution.py:316
  30.5 10.7 %collective-permute-start.7 = (bf16[400,256]{1,0:T(8,128)(2,1)S(1)}, bf16[400,256]{1,0:T(8,128)(2,1)S(1)}, u32[]{:S(2)}, u32[]{:S(2)}) collective-permute-start(bf16[400,256]{1,0:T(8,128)(2,1)S(1)} %pack_fwd.1), channel_id=1, source_target_pairs={{0,2},{1,3},{2,0},{3,1},{4,6},{5,7},{6,4},{7,5},{8,10},{9,11},{10,... | collective-permute-start | bytes 614408 | tf_op jit(solution)/shard_map/ppermute | solution.py:316
  32.1 9.0 %collective-permute-start.6 = (bf16[400,256]{1,0:T(8,128)(2,1)S(1)}, bf16[400,256]{1,0:T(8,128)(2,1)S(1)}, u32[]{:S(2)}, u32[]{:S(2)}) collective-permute-start(bf16[400,256]{1,0:T(8,128)(2,1)S(1)} %pack_fwd.1), channel_id=1, source_target_pairs={{0,8},{1,9},{2,10},{3,11},{4,12},{5,13},{6,14},{7,15},{8,0},{9,1},... | collective-permute-start | bytes 614408 | tf_op jit(solution)/shard_map/ppermute | solution.py:316
  41.1 3.7 %collective-permute-start.14 = (bf16[400,768]{1,0:T(8,128)(2,1)S(1)}, bf16[400,768]{1,0:T(8,128)(2,1)S(1)}, u32[]{:S(2)}, u32[]{:S(2)}) collective-permute-start(bf16[400,768]{1,0:T(8,128)(2,1)S(1)} %get-tuple-element.82.mine_ref.g_ref), channel_id=1, source_target_pairs={{0,1},{1,0},{2,3},{3,2},{4,5},{5,4},{6,7},{7,6},{8,9},{9,8},{10,11... | collective-permute-start | bytes 1843208 | tf_op jit(solution)/shard_map/ppermute | solution.py:320
  41.1 12.4 %collective-permute-start.18 = (bf16[400,256]{1,0:T(8,128)(2,1)S(1)}, bf16[400,256]{1,0:T(8,128)(2,1)S(1)}, u32[]{:S(2)}, u32[]{:S(2)}) collective-permute-start(bf16[400,256]{1,0:T(8,128)(2,1)S(1)} %collective-permute-done.8), channel_id=1, source_target_pairs={{0,2},{1,3},{2,0},{3,1},{4,6},{5,7},{6,4},{7,5},{8,10},{9,11},{10,... | collective-permute-start | bytes 614408 | tf_op jit(solution)/shard_map/ppermute | solution.py:316
  42.6 10.9 %collective-permute-start.19 = (bf16[400,256]{1,0:T(8,128)(2,1)S(1)}, bf16[400,256]{1,0:T(8,128)(2,1)S(1)}, u32[]{:S(2)}, u32[]{:S(2)}) collective-permute-start(bf16[400,256]{1,0:T(8,128)(2,1)S(1)} %collective-permute-done.7), channel_id=1, source_target_pairs={{0,8},{1,9},{2,10},{3,11},{4,12},{5,13},{6,14},{7,15},{8,0},{9,1},... | collective-permute-start | bytes 614408 | tf_op jit(solution)/shard_map/ppermute | solution.py:316
  43.9 9.7 %collective-permute-start.20 = (bf16[400,256]{1,0:T(8,128)(2,1)S(1)}, bf16[400,256]{1,0:T(8,128)(2,1)S(1)}, u32[]{:S(2)}, u32[]{:S(2)}) collective-permute-start(bf16[400,256]{1,0:T(8,128)(2,1)S(1)} %collective-permute-done.6), channel_id=1, source_target_pairs={{0,6},{1,7},{2,4},{3,5},{4,2},{5,3},{6,0},{7,1},{8,14},{9,15},{10,... | collective-permute-start | bytes 614408 | tf_op jit(solution)/shard_map/ppermute | solution.py:316
  44.8 14.6 %slice-start = ((s8[6291456]{0:T(1024)(128)(4,1)}), s8[4194304]{0:T(1024)(128)(4,1)S(1)}, s32[]{:S(2)}) async-start(s8[6291456]{0:T(1024)(128)(4,1)} %bitcast.36), calls=%async_computation | async-start | bytes 8388608
  49.2 10.3 %slice-start.1 = ((s8[6291456]{0:T(1024)(128)(4,1)}), s8[2097152]{0:T(1024)(128)(4,1)S(1)}, s32[]{:S(2)}) async-start(s8[6291456]{0:T(1024)(128)(4,1)} %bitcast.36), calls=%async_computation.1 | async-start | bytes 4194304
  53.7 4.4 %collective-permute-start.21 = (bf16[4,400,256]{2,1,0:T(8,128)(2,1)S(1)}, bf16[4,400,256]{2,1,0:T(8,128)(2,1)S(1)}, u32[]{:S(2)}, u32[]{:S(2)}) collective-permute-start(bf16[4,400,256]{2,1,0:T(8,128)(2,1)S(1)} %pad_maximum_fusion.2.mine_ref), channel_id=1, source_target_pairs={{0,1},{1,0},{2,3},{3,2},{4,5},{5,4},{6,7},{7,6},{8,9},{9,8},{10,11... | collective-permute-start | bytes 2457608 | tf_op jit(solution)/shard_map/ppermute | solution.py:320
  53.9 17.9 %collective-permute-start.22 = (bf16[4,400,256]{2,1,0:T(8,128)(2,1)S(1)}, bf16[4,400,256]{2,1,0:T(8,128)(2,1)S(1)}, u32[]{:S(2)}, u32[]{:S(2)}) collective-permute-start(bf16[4,400,256]{2,1,0:T(8,128)(2,1)S(1)} %pad_maximum_fusion.3.mine_ref), channel_id=1, source_target_pairs={{0,1},{1,0},{2,3},{3,2},{4,5},{5,4},{6,7},{7,6},{8,9},{9,8},{10,11... | collective-permute-start | bytes 2457608 | tf_op jit(solution)/shard_map/ppermute | solution.py:320
  54.5 7.1 %collective-permute-start.15 = (bf16[400,256]{1,0:T(8,128)(2,1)S(1)}, bf16[400,256]{1,0:T(8,128)(2,1)S(1)}, u32[]{:S(2)}, u32[]{:S(2)}) collective-permute-start(bf16[400,256]{1,0:T(8,128)(2,1)S(1)} %get-tuple-element.75), channel_id=1, source_target_pairs={{0,6},{1,7},{2,4},{3,5},{4,2},{5,3},{6,0},{7,1},{8,14},{9,15},{10,... | collective-permute-start | bytes 614408 | tf_op jit(solution)/shard_map/ppermute | solution.py:316
  55.6 8.0 %collective-permute-start.16 = (bf16[400,256]{1,0:T(8,128)(2,1)S(1)}, bf16[400,256]{1,0:T(8,128)(2,1)S(1)}, u32[]{:S(2)}, u32[]{:S(2)}) collective-permute-start(bf16[400,256]{1,0:T(8,128)(2,1)S(1)} %get-tuple-element.76), channel_id=1, source_target_pairs={{0,8},{1,9},{2,10},{3,11},{4,12},{5,13},{6,14},{7,15},{8,0},{9,1},... | collective-permute-start | bytes 614408 | tf_op jit(solution)/shard_map/ppermute | solution.py:316
  56.4 9.6 %collective-permute-start.17 = (bf16[400,256]{1,0:T(8,128)(2,1)S(1)}, bf16[400,256]{1,0:T(8,128)(2,1)S(1)}, u32[]{:S(2)}, u32[]{:S(2)}) collective-permute-start(bf16[400,256]{1,0:T(8,128)(2,1)S(1)} %get-tuple-element.77), channel_id=1, source_target_pairs={{0,2},{1,3},{2,0},{3,1},{4,6},{5,7},{6,4},{7,5},{8,10},{9,11},{10,... | collective-permute-start | bytes 614408 | tf_op jit(solution)/shard_map/ppermute | solution.py:316
  58.1 13.7 %copy-start.2 = (bf16[1,384,256]{2,1,0:T(8,128)(2,1)S(1)}, bf16[1,384,256]{2,1,0:T(8,128)(2,1)}, u32[]{:S(2)}) copy-start(bf16[1,384,256]{2,1,0:T(8,128)(2,1)} %param.8) | copy-start | bytes 589828
  58.1 20.9 %collective-permute-start.27 = (bf16[400,256]{1,0:T(8,128)(2,1)S(1)}, bf16[400,256]{1,0:T(8,128)(2,1)S(1)}, u32[]{:S(2)}, u32[]{:S(2)}) collective-permute-start(bf16[400,256]{1,0:T(8,128)(2,1)S(1)} %get-tuple-element.106), channel_id=1, source_target_pairs={{0,12},{1,13},{2,14},{3,15},{4,8},{5,9},{6,10},{7,11},{8,4},{9,5},... | collective-permute-start | bytes 614408 | tf_op jit(solution)/shard_map/ppermute | solution.py:316
  66.2 12.9 %collective-permute-start.24 = (bf16[400,256]{1,0:T(8,128)(2,1)S(1)}, bf16[400,256]{1,0:T(8,128)(2,1)S(1)}, u32[]{:S(2)}, u32[]{:S(2)}) collective-permute-start(bf16[400,256]{1,0:T(8,128)(2,1)S(1)} %get-tuple-element.103), channel_id=1, source_target_pairs={{0,8},{1,9},{2,10},{3,11},{4,12},{5,13},{6,14},{7,15},{8,0},{9,1},... | collective-permute-start | bytes 614408 | tf_op jit(solution)/shard_map/ppermute | solution.py:316
  69.3 9.7 %collective-permute-start.25 = (bf16[400,256]{1,0:T(8,128)(2,1)S(1)}, bf16[400,256]{1,0:T(8,128)(2,1)S(1)}, u32[]{:S(2)}, u32[]{:S(2)}) collective-permute-start(bf16[400,256]{1,0:T(8,128)(2,1)S(1)} %get-tuple-element.104), channel_id=1, source_target_pairs={{0,2},{1,3},{2,0},{3,1},{4,6},{5,7},{6,4},{7,5},{8,10},{9,11},{10,... | collective-permute-start | bytes 614408 | tf_op jit(solution)/shard_map/ppermute | solution.py:316
  71.8 7.3 %collective-permute-start.26 = (bf16[400,256]{1,0:T(8,128)(2,1)S(1)}, bf16[400,256]{1,0:T(8,128)(2,1)S(1)}, u32[]{:S(2)}, u32[]{:S(2)}) collective-permute-start(bf16[400,256]{1,0:T(8,128)(2,1)S(1)} %get-tuple-element.105), channel_id=1, source_target_pairs={{0,6},{1,7},{2,4},{3,5},{4,2},{5,3},{6,0},{7,1},{8,14},{9,15},{10,... | collective-permute-start | bytes 614408 | tf_op jit(solution)/shard_map/ppermute | solution.py:316
  71.8 7.2 %copy-start.4 = (bf16[1,384,256]{2,1,0:T(8,128)(2,1)S(1)}, bf16[1,384,256]{2,1,0:T(8,128)(2,1)}, u32[]{:S(2)}) copy-start(bf16[1,384,256]{2,1,0:T(8,128)(2,1)} %param.9) | copy-start | bytes 589828
  71.8 7.2 %copy-start.8 = (f32[1,256]{1,0:T(1,128)S(1)}, f32[1,256]{1,0:T(1,128)}, u32[]{:S(2)}) copy-start(f32[1,256]{1,0:T(1,128)} %refs_6_.1) | copy-start | bytes 3076
  76.3 15.2 %collective-permute-start.23 = (bf16[384,256]{1,0:T(8,128)(2,1)S(1)}, bf16[384,256]{1,0:T(8,128)(2,1)S(1)}, u32[]{:S(2)}, u32[]{:S(2)}) collective-permute-start(bf16[384,256]{1,0:T(8,128)(2,1)S(1)} %forward.1), channel_id=1, source_target_pairs={{240,0},{0,16},{16,32},{32,48},{48,64},{64,80},{80,96},{96,112},{1... | collective-permute-start | bytes 589832 | tf_op jit(solution)/shard_map/ppermute | solution.py:325
  79.9 11.6 %collective-permute-start.28 = (bf16[384,256]{1,0:T(8,128)(2,1)S(1)}, bf16[384,256]{1,0:T(8,128)(2,1)S(1)}, u32[]{:S(2)}, u32[]{:S(2)}) collective-permute-start(bf16[384,256]{1,0:T(8,128)(2,1)S(1)} %get-tuple-element.112), channel_id=1, source_target_pairs={{16,0},{32,16},{48,32},{64,48},{80,64},{96,80},{112,96},{128,112},... | collective-permute-start | bytes 589832 | tf_op jit(solution)/shard_map/ppermute | solution.py:325

commit v4 on v3

--- a/solution.py
+++ b/solution.py
@@ -57,7 +57,15 @@
     return jnp.sum(jnp.transpose(folded), axis=0, keepdims=True)
 
 
-def pack_kernel(x_ref, gain_ref, out_ref):
+def pack_kernel(x_hbm, gain_hbm, out_ref, x_ref, gain_ref, sem_ref):
+    copies = [
+        pltpu.make_async_copy(x_hbm, x_ref, sem_ref.at[0]),
+        pltpu.make_async_copy(gain_hbm, gain_ref, sem_ref.at[1]),
+    ]
+    for held in copies:
+        held.start()
+    for held in copies:
+        held.wait()
     tokens = x_ref.shape[0]
     wide = x_ref[...].astype(F32)
     out_ref[:tokens, :] = (wide * gain_ref[...]).astype(BF16)
@@ -311,6 +319,25 @@
     )(*args)
 
 
+def pack(x, gain, name):
+    tokens, local = x.shape
+    hbm = pl.BlockSpec(memory_space=pltpu.HBM)
+    return pl.pallas_call(
+        pack_kernel,
+        out_shape=jax.ShapeDtypeStruct((tokens + STAT, local), BF16),
+        in_specs=[hbm, hbm],
+        out_specs=pl.BlockSpec(memory_space=pltpu.VMEM),
+        scratch_shapes=[
+            pltpu.VMEM((tokens, local), BF16),
+            pltpu.VMEM((1, local), F32),
+            pltpu.SemaphoreType.DMA((2,)),
+        ],
+        compiler_params=pltpu.CompilerParams(vmem_limit_bytes=VMEM_BYTES),
+        cost_estimate=cost(1.0),
+        name=name,
+    )(x, gain)
+
+
 def to_chip(block, distance):
     route = [(i, ((i >> 1) ^ distance) << 1 | (i & 1)) for i in range(2 * CHIPS)]
     return lax.ppermute(block, "fsdp", route)
@@ -364,8 +391,8 @@
     narrow = jax.ShapeDtypeStruct((tokens, local), BF16)
     proj = pltpu.VMEM((tokens, 3 * local), BF16)
 
-    pay_bwd = plain_call(pack_kernel, block, "pack_bwd", 1.0, saved_in, gain, held=False)
-    pay_fwd = plain_call(pack_kernel, block, "pack_fwd", 1.0, forward_in, gain, held=False)
+    pay_bwd = pack(saved_in, gain, "pack_bwd")
+    pay_fwd = pack(forward_in, gain, "pack_fwd")
     w_other = to_core(weight)
 
     near_bwd = near(pay_bwd)
@@ -381,7 +408,7 @@
     last_bwd, first, w_other, pay_fwd = tie((last_bwd, first, w_other, pay_fwd))
     mine_b = jnp.stack([*far_bwd, last_bwd])
     other_b = to_core(mine_b)
-    near_fwd, last_fwd = near(pay_fwd), to_chip(pay_fwd, FAR[-1])
+    near_fwd = near(pay_fwd)
     grads, scale = plain_call(
         backward_kernel,
         (
@@ -404,9 +431,10 @@
             pltpu.VMEM((tokens, tokens), BF16),
         ],
     )
-    near_fwd, last_fwd, grads = tie((near_fwd, last_fwd, grads))
+    near_fwd, grads = tie((near_fwd, grads))
     grads_other = to_core(grads)
     far_fwd = far(near_fwd)
+    last_fwd = to_chip(near_fwd[0], FAR[-1])
 
     def input_grads(places, grads, name, shapes):
         return plain_call(
@@ -423,16 +451,21 @@
 
     for_2, for_5, for_7, for_6 = input_grads((4, 5, 6, 7), grads, "input_grad_far", [block] * 4)
     alone = jax.ShapeDtypeStruct((tokens, local), F32)
-    later, for_7 = tie((grads, for_7))
+    far_fwd, near_fwd, for_2, for_5, for_7, later = tie(
+        (far_fwd, near_fwd, for_2, for_5, for_7, grads)
+    )
+    came = [to_chip(for_7, 3), to_chip(for_5, 4), to_chip(for_2, 1)]
     *parts, own, pair = input_grads(
         (1, 2, 3, 0),
         later,
         "input_grad_near",
         [alone] * 4 + [jax.ShapeDtypeStruct((STAT, local), BF16)],
     )
-    came = [to_chip(for_7, 3), to_chip(for_5, 4), to_chip(for_2, 1)]
+    last_fwd, pair = tie((last_fwd, pair))
+    came[0], for_6 = tie((came[0], for_6))
     direct = to_chip(for_6, 6)
-    far_fwd, near_fwd, pair = tie((far_fwd, near_fwd, pair))
+    sums = plain_call(add_kernel, [block] * 3, "add", 1.0, pair, *parts, *came)
+    gone = [to_chip(part, d) for part, d in zip(sums, NEAR[1:])] + [direct]
     mine_fa = jnp.stack(near_fwd)
     other_fa = to_core(mine_fa)
     mine_fb = jnp.stack([*far_fwd, last_fwd])
@@ -440,9 +473,6 @@
     first_f, stat_f = plain_call(
         first_kernel, (wide, stat), "first_fwd", 2.5, ints, mine_fa, other_fa, weight
     )
-    came, first_f = tie((came, first_f))
-    sums = plain_call(add_kernel, [block] * 3, "add", 1.0, pair, *parts, *came)
-    gone = [to_chip(part, d) for part, d in zip(sums, NEAR[1:])] + [direct]
     result = plain_call(
         forward_kernel,
         narrow,

time: 93.1 us -> 94.6 us (1.016)
  the two profiles are of different devices: /device:TPU:8 before, /device:TPU:1 now
where the time goes in v4:
time: 94.6 us; the launch traced here: 94.3 us
  starting transfers between devices  42 us (44%)
  Pallas kernels  28.3 us (30%)
  waiting for transfers between devices  15 us (16%)
  local copies, waits for them, and re-layouts  7.68 us (8%)
    pallas_call x8, Pallas kernels, plain_call(): pl.pallas_call(kernel, out_shape=out_shape, in_specs=specs, out_specs=jax...  22.3 us
    ppermute x21, starting transfers between devices, to_chip(): return lax.ppermute(block, 'fsdp', route)  20.7 us
    ppermute x21, waiting for transfers between devices, to_chip(): return lax.ppermute(block, 'fsdp', route)  15 us
    ppermute x6, starting transfers between devices, to_core(): return lax.ppermute(block, 'fsdp', [(i, i ^ 1) for i in range(2 * CHIPS)])  11.7 us
    ppermute x2, starting transfers between devices, shifted(): lax.ppermute(block, axis, [((i - distance) % count, i) for i in range(cou...  9.57 us
    unnamed x31, local copies, waits for them, and re-layouts  7.49 us
    pallas_call x1, Pallas kernels, weight_grad(): pl.pallas_call(weight_grad_kernel, out_shape=jax.ShapeDtypeStruct((3, 2 *...  5.18 us
  transfers between devices with their start and end apart: 29, of which 6 were waited for; matrix products, arithmetic and copies ran while one was open for 1% of the time, Pallas kernels for 30%

profile of v4, /device:TPU:1, one launch (start us, length us, event | category | flops | bytes accessed | tf_op | source)
XLA Modules:
  0.0 94.3 jit_solution(8858094333274487399)
XLA Ops:
  0.7 3.3 %collective-permute-start.5 = (bf16[3,4096,256]{2,1,0:T(8,128)(2,1)}, bf16[3,4096,256]{2,1,0:T(8,128)(2,1)}, u32[]{:S(2)}, u32[]{:S(2)}) collective-permute-start(bf16[3,4096,256]{2,1,0:T(8,128)(2,1)} %bitcast.31), channel_id=1, source_target_pairs={{0,1},{1,0},{2,3},{3,2},{4,5},{5,4},{6,7},{7,6},{8,9},{9,8},{10,11... | collective-permute-start | bytes 18874376 | tf_op jit(solution)/shard_map/ppermute | solution.py:347
  4.0 0.9 copy-done.3
  4.9 0.7 copy-done.6
  5.6 0.4 pack_bwd.1
  6.0 1.1 %collective-permute-start.3 = (bf16[400,256]{1,0:T(8,128)(2,1)S(1)}, bf16[400,256]{1,0:T(8,128)(2,1)S(1)}, u32[]{:S(2)}, u32[]{:S(2)}) collective-permute-start(bf16[400,256]{1,0:T(8,128)(2,1)S(1)} %pack_bwd.1), channel_id=1, source_target_pairs={{0,6},{1,7},{2,4},{3,5},{4,2},{5,3},{6,0},{7,1},{8,14},{9,15},{10,... | collective-permute-start | bytes 614408 | tf_op jit(solution)/shard_map/ppermute | solution.py:343
  7.1 0.0 collective-permute-start.2
  7.1 1.2 %collective-permute-start.1 = (bf16[400,256]{1,0:T(8,128)(2,1)S(1)}, bf16[400,256]{1,0:T(8,128)(2,1)S(1)}, u32[]{:S(2)}, u32[]{:S(2)}) collective-permute-start(bf16[400,256]{1,0:T(8,128)(2,1)S(1)} %pack_bwd.1), channel_id=1, source_target_pairs={{0,8},{1,9},{2,10},{3,11},{4,12},{5,13},{6,14},{7,15},{8,0},{9,1},... | collective-permute-start | bytes 614408 | tf_op jit(solution)/shard_map/ppermute | solution.py:343
  8.3 0.9 copy-done.1
  9.2 0.7 copy-done.7
  9.9 0.4 pack_fwd.1
  10.3 3.7 %collective-permute-done.3 = bf16[400,256]{1,0:T(8,128)(2,1)S(1)} collective-permute-done((bf16[400,256]{1,0:T(8,128)(2,1)S(1)}, bf16[400,256]{1,0:T(8,128)(2,1)S(1)}, u32[]{:S(2)}, u32[]{:S(2)}) %collective-permute-start.3) | collective-permute-done | bytes 204832 | tf_op jit(solution)/shard_map/ppermute | solution.py:343
  14.0 0.0 collective-permute-done.2
  14.0 0.0 collective-permute-done.1
  14.0 0.1 pad_maximum_fusion.mine_ref
  14.1 0.9 collective-permute-start.4
  15.0 2.4 %collective-permute-start = (bf16[400,256]{1,0:T(8,128)(2,1)S(1)}, bf16[400,256]{1,0:T(8,128)(2,1)S(1)}, u32[]{:S(2)}, u32[]{:S(2)}) collective-permute-start(bf16[400,256]{1,0:T(8,128)(2,1)S(1)} %pack_bwd.1), channel_id=1, source_target_pairs={{0,12},{1,13},{2,14},{3,15},{4,8},{5,9},{6,10},{7,11},{8,4},{9,5},... | collective-permute-start | bytes 614408 | tf_op jit(solution)/shard_map/ppermute | solution.py:343
  17.4 0.1 copy.13
  17.5 0.1 reshape.14
  17.6 0.1 concatenate.3.ints_ref
  17.7 2.2 %collective-permute-start.11 = (bf16[400,256]{1,0:T(8,128)(2,1)S(1)}, bf16[400,256]{1,0:T(8,128)(2,1)S(1)}, u32[]{:S(2)}, u32[]{:S(2)}) collective-permute-start(bf16[400,256]{1,0:T(8,128)(2,1)S(1)} %collective-permute-done.1), channel_id=1, source_target_pairs={{0,6},{1,7},{2,4},{3,5},{4,2},{5,3},{6,0},{7,1},{8,14},{9,15},{10,... | collective-permute-start | bytes 614408 | tf_op jit(solution)/shard_map/ppermute | solution.py:343
  19.9 0.3 collective-permute-start.10
  20.2 0.0 collective-permute-done.4.other_ref
  20.2 0.0 collective-permute-start.9
  20.2 2.8 %copy-done = bf16[1,4096,3,256]{3,1,2,0:T(8,128)(2,1)S(1)} copy-done((bf16[1,4096,3,256]{3,1,2,0:T(8,128)(2,1)S(1)}, bf16[1,4096,3,256]{3,1,2,0:T(8,128)(2,1)}, u32[]{:S(2)}) %copy-start) | copy-done | bytes 6291480
  23.0 1.9 %first_bwd.1 = (f32[384,768]{1,0:T(8,128)S(1)}, f32[16,256]{1,0:T(8,128)S(1)}) custom-call(s32[75]{0:T(128)S(1)} %concatenate.3.ints_ref, bf16[4,400,256]{2,1,0:T(8,128)(2,1)S(1)} %pad_maximum_fusion.mine_ref, bf16[4,400,256]{2,1,0:T(8,128)(2,1)S(1)} %collective-permute-done.4.other_ref, bf16[3,4096,256]{2,1,0:T(8,128)(2,1)S(1)} %bitcast.32), custom_call_target="tpu_custom_call" | custom-call | flops 2750000128 | tf_op jit(solution)/shard_map/first_bwd/pallas_call | solution.py:310
  25.0 3.9 %collective-permute-done.11 = bf16[400,256]{1,0:T(8,128)(2,1)S(1)} collective-permute-done((bf16[400,256]{1,0:T(8,128)(2,1)S(1)}, bf16[400,256]{1,0:T(8,128)(2,1)S(1)}, u32[]{:S(2)}, u32[]{:S(2)}) %collective-permute-start.11) | collective-permute-done | bytes 204832 | tf_op jit(solution)/shard_map/ppermute | solution.py:343
  28.8 0.1 pad_maximum_fusion.1.mine_ref.more_ref
  28.9 0.6 collective-permute-start.12
  29.5 1.4 %collective-permute-start.8 = (bf16[400,256]{1,0:T(8,128)(2,1)S(1)}, bf16[400,256]{1,0:T(8,128)(2,1)S(1)}, u32[]{:S(2)}, u32[]{:S(2)}) collective-permute-start(bf16[400,256]{1,0:T(8,128)(2,1)S(1)} %pack_fwd.1), channel_id=1, source_target_pairs={{0,6},{1,7},{2,4},{3,5},{4,2},{5,3},{6,0},{7,1},{8,14},{9,15},{10,... | collective-permute-start | bytes 614408 | tf_op jit(solution)/shard_map/ppermute | solution.py:343
  31.0 0.1 collective-permute-start.7
  31.1 1.2 %collective-permute-start.6 = (bf16[400,256]{1,0:T(8,128)(2,1)S(1)}, bf16[400,256]{1,0:T(8,128)(2,1)S(1)}, u32[]{:S(2)}, u32[]{:S(2)}) collective-permute-start(bf16[400,256]{1,0:T(8,128)(2,1)S(1)} %pack_fwd.1), channel_id=1, source_target_pairs={{0,8},{1,9},{2,10},{3,11},{4,12},{5,13},{6,14},{7,15},{8,0},{9,1},... | collective-permute-start | bytes 614408 | tf_op jit(solution)/shard_map/ppermute | solution.py:343
  32.3 4.6 %backward.1 = (bf16[400,768]{1,0:T(8,128)(2,1)S(1)}, f32[384,128]{1,0:T(8,128)S(1)}) custom-call(s32[75]{0:T(128)S(1)} %concatenate.3.ints_ref, f32[384,768]{1,0:T(8,128)S(1)} %get-tuple-element.68.first_ref, f32[16,256]{1,0:T(8,128)S(1)} %get-tuple-element.69.stat_ref, bf16[4,400,256]{2,1,0:T(8,128)(2,1)S(1)} %pad_maximum_fusion.1.mine_ref.more_ref, ...), custom_call_target="tpu_custom_call" | custom-call | flops 6600000000 | tf_op jit(solution)/shard_map/backward/pallas_call | solution.py:310
  36.9 0.5 collective-permute-done.8
  37.4 1.2 %collective-permute-start.16 = (bf16[400,768]{1,0:T(8,128)(2,1)S(1)}, bf16[400,768]{1,0:T(8,128)(2,1)S(1)}, u32[]{:S(2)}, u32[]{:S(2)}) collective-permute-start(bf16[400,768]{1,0:T(8,128)(2,1)S(1)} %get-tuple-element.90.mine_ref.g_ref), channel_id=1, source_target_pairs={{0,1},{1,0},{2,3},{3,2},{4,5},{5,4},{6,7},{7,6},{8,9},{9,8},{10,11... | collective-permute-start | bytes 1843208 | tf_op jit(solution)/shard_map/ppermute | solution.py:347
  38.6 1.4 %collective-permute-start.13 = (bf16[400,256]{1,0:T(8,128)(2,1)S(1)}, bf16[400,256]{1,0:T(8,128)(2,1)S(1)}, u32[]{:S(2)}, u32[]{:S(2)}) collective-permute-start(bf16[400,256]{1,0:T(8,128)(2,1)S(1)} %collective-permute-done.8), channel_id=1, source_target_pairs={{0,2},{1,3},{2,0},{3,1},{4,6},{5,7},{6,4},{7,5},{8,10},{9,11},{10,... | collective-permute-start | bytes 614408 | tf_op jit(solution)/shard_map/ppermute | solution.py:343
  39.9 0.8 collective-permute-start.14
  40.7 1.4 %collective-permute-start.15 = (bf16[400,256]{1,0:T(8,128)(2,1)S(1)}, bf16[400,256]{1,0:T(8,128)(2,1)S(1)}, u32[]{:S(2)}, u32[]{:S(2)}) collective-permute-start(bf16[400,256]{1,0:T(8,128)(2,1)S(1)} %collective-permute-done.6), channel_id=1, source_target_pairs={{0,6},{1,7},{2,4},{3,5},{4,2},{5,3},{6,0},{7,1},{8,14},{9,15},{10,... | collective-permute-start | bytes 614408 | tf_op jit(solution)/shard_map/ppermute | solution.py:343
  42.2 0.9 collective-permute-start.18
  43.0 4.2 %input_grad_far.1 = (bf16[400,256]{1,0:T(8,128)(2,1)S(1)}, bf16[400,256]{1,0:T(8,128)(2,1)S(1)}, bf16[400,256]{1,0:T(8,128)(2,1)S(1)}, bf16[400,256]{1,0:T(8,128)(2,1)S(1)}) custom-call(s32[75]{0:T(128)S(1)} %concatenate.3.ints_ref, bf16[400,768]{1,0:T(8,128)(2,1)S(1)} %get-tuple-element.90.mine_ref.g_ref, ...), custom_call_target="tpu_custom_call" | custom-call | flops 3849999872 | tf_op jit(solution)/shard_map/input_grad_far/pallas_call | solution.py:310
  47.3 1.2 %collective-permute-done.15 = bf16[400,256]{1,0:T(8,128)(2,1)S(1)} collective-permute-done((bf16[400,256]{1,0:T(8,128)(2,1)S(1)}, bf16[400,256]{1,0:T(8,128)(2,1)S(1)}, u32[]{:S(2)}, u32[]{:S(2)}) %collective-permute-start.15) | collective-permute-done | bytes 204832 | tf_op jit(solution)/shard_map/ppermute | solution.py:343
  48.5 0.1 pad_maximum_fusion.2.mine_ref
  48.6 0.0 slice-start.1
  48.6 5.4 %collective-permute-start.17 = (bf16[4,400,256]{2,1,0:T(8,128)(2,1)S(1)}, bf16[4,400,256]{2,1,0:T(8,128)(2,1)S(1)}, u32[]{:S(2)}, u32[]{:S(2)}) collective-permute-start(bf16[4,400,256]{2,1,0:T(8,128)(2,1)S(1)} %pad_maximum_fusion.2.mine_ref), channel_id=1, source_target_pairs={{0,1},{1,0},{2,3},{3,2},{4,5},{5,4},{6,7},{7,6},{8,9},{9,8},{10,11... | collective-permute-start | bytes 2457608 | tf_op jit(solution)/shard_map/ppermute | solution.py:347
  54.0 4.2 %input_grad_near.1 = (f32[384,256]{1,0:T(8,128)S(1)}, f32[384,256]{1,0:T(8,128)S(1)}, f32[384,256]{1,0:T(8,128)S(1)}, f32[384,256]{1,0:T(8,128)S(1)}, bf16[16,256]{1,0:T(8,128)(2,1)S(1)}) custom-call(s32[75]{0:T(128)S(1)} %concatenate.3.ints_ref, bf16[400,768]{1,0:T(8,128)(2,1)S(1)} %get-tuple-element.90.mine_ref.g_ref, ...), custom_call_target="tpu_custom_call" | custom-call | flops 3849999872 | tf_op jit(solution)/shard_map/input_grad_near/pallas_call | solution.py:310
  58.3 0.1 pad_maximum_fusion.3.mine_ref
  58.4 0.3 collective-permute-start.19
  58.6 1.6 %collective-permute-start.21 = (bf16[400,256]{1,0:T(8,128)(2,1)S(1)}, bf16[400,256]{1,0:T(8,128)(2,1)S(1)}, u32[]{:S(2)}, u32[]{:S(2)}) collective-permute-start(bf16[400,256]{1,0:T(8,128)(2,1)S(1)} %get-tuple-element.98), channel_id=1, source_target_pairs={{0,6},{1,7},{2,4},{3,5},{4,2},{5,3},{6,0},{7,1},{8,14},{9,15},{10,... | collective-permute-start | bytes 614408 | tf_op jit(solution)/shard_map/ppermute | solution.py:343
  60.2 0.3 collective-permute-start.22
  60.6 5.6 %collective-permute-done.21.refs_3_ = bf16[400,256]{1,0:T(8,128)(2,1)S(1)} collective-permute-done((bf16[400,256]{1,0:T(8,128)(2,1)S(1)}, bf16[400,256]{1,0:T(8,128)(2,1)S(1)}, u32[]{:S(2)}, u32[]{:S(2)}) %collective-permute-start.21) | collective-permute-done | bytes 204832 | tf_op jit(solution)/shard_map/ppermute | solution.py:343
  66.2 0.1 collective-permute-done.23.refs_5_
  66.2 0.2 add.23
  66.4 1.1 %collective-permute-start.24 = (bf16[400,256]{1,0:T(8,128)(2,1)S(1)}, bf16[400,256]{1,0:T(8,128)(2,1)S(1)}, u32[]{:S(2)}, u32[]{:S(2)}) collective-permute-start(bf16[400,256]{1,0:T(8,128)(2,1)S(1)} %get-tuple-element.103), channel_id=1, source_target_pairs={{0,8},{1,9},{2,10},{3,11},{4,12},{5,13},{6,14},{7,15},{8,0},{9,1},... | collective-permute-start | bytes 614408 | tf_op jit(solution)/shard_map/ppermute | solution.py:343
  67.5 2.2 %collective-permute-start.25 = (bf16[400,256]{1,0:T(8,128)(2,1)S(1)}, bf16[400,256]{1,0:T(8,128)(2,1)S(1)}, u32[]{:S(2)}, u32[]{:S(2)}) collective-permute-start(bf16[400,256]{1,0:T(8,128)(2,1)S(1)} %get-tuple-element.104), channel_id=1, source_target_pairs={{0,2},{1,3},{2,0},{3,1},{4,6},{5,7},{6,4},{7,5},{8,10},{9,11},{10,... | collective-permute-start | bytes 614408 | tf_op jit(solution)/shard_map/ppermute | solution.py:343
  69.7 1.2 %collective-permute-start.26 = (bf16[400,256]{1,0:T(8,128)(2,1)S(1)}, bf16[400,256]{1,0:T(8,128)(2,1)S(1)}, u32[]{:S(2)}, u32[]{:S(2)}) collective-permute-start(bf16[400,256]{1,0:T(8,128)(2,1)S(1)} %get-tuple-element.105), channel_id=1, source_target_pairs={{0,6},{1,7},{2,4},{3,5},{4,2},{5,3},{6,0},{7,1},{8,14},{9,15},{10,... | collective-permute-start | bytes 614408 | tf_op jit(solution)/shard_map/ppermute | solution.py:343
  70.9 1.9 %first_fwd.1 = (f32[384,768]{1,0:T(8,128)S(1)}, f32[16,256]{1,0:T(8,128)S(1)}) custom-call(s32[75]{0:T(128)S(1)} %concatenate.3.ints_ref, bf16[4,400,256]{2,1,0:T(8,128)(2,1)S(1)} %pad_maximum_fusion.2.mine_ref, bf16[4,400,256]{2,1,0:T(8,128)(2,1)S(1)} %collective-permute-done.17.other_ref, bf16[3,4096,256]{2,1,0:T(8,128)(2,1)S(1)} %bitcast.38), custom_call_target="tpu_custom_call" | custom-call | flops 2750000128 | tf_op jit(solution)/shard_map/first_fwd/pallas_call | solution.py:310
  72.8 0.0 copy-start.4
  72.8 0.0 copy-start.8
  72.8 4.5 %forward.1 = bf16[384,256]{1,0:T(8,128)(2,1)S(1)} custom-call(s32[75]{0:T(128)S(1)} %concatenate.3.ints_ref, f32[384,768]{1,0:T(8,128)S(1)} %get-tuple-element.85.first_ref, f32[16,256]{1,0:T(8,128)S(1)} %get-tuple-element.86.stat_ref, bf16[4,400,256]{2,1,0:T(8,128)(2,1)S(1)} %pad_maximum_fusion.3.mine_ref, ...), custom_call_target="tpu_custom_call" | custom-call | flops 4950000128 | tf_op jit(solution)/shard_map/forward/pallas_call | solution.py:310
  77.3 2.6 %collective-permute-start.20 = (bf16[384,256]{1,0:T(8,128)(2,1)S(1)}, bf16[384,256]{1,0:T(8,128)(2,1)S(1)}, u32[]{:S(2)}, u32[]{:S(2)}) collective-permute-start(bf16[384,256]{1,0:T(8,128)(2,1)S(1)} %forward.1), channel_id=1, source_target_pairs={{240,0},{0,16},{16,32},{32,48},{48,64},{64,80},{80,96},{96,112},{1... | collective-permute-start | bytes 589832 | tf_op jit(solution)/shard_map/ppermute | solution.py:352
  80.0 0.8 finish.1
  80.8 7.0 %collective-permute-start.28 = (bf16[384,256]{1,0:T(8,128)(2,1)S(1)}, bf16[384,256]{1,0:T(8,128)(2,1)S(1)}, u32[]{:S(2)}, u32[]{:S(2)}) collective-permute-start(bf16[384,256]{1,0:T(8,128)(2,1)S(1)} %get-tuple-element.112), channel_id=1, source_target_pairs={{16,0},{32,16},{48,32},{64,48},{80,64},{96,80},{112,96},{128,112},... | collective-permute-start | bytes 589832 | tf_op jit(solution)/shard_map/ppermute | solution.py:352
  87.8 5.2 %weight_grad.1 = bf16[3,4096,256]{2,1,0:T(8,128)(2,1)} custom-call(s32[75]{0:T(128)S(1)} %concatenate.3.ints_ref, bf16[4,400,256]{2,1,0:T(8,128)(2,1)S(1)} %pad_maximum_fusion.mine_ref, bf16[4,400,256]{2,1,0:T(8,128)(2,1)S(1)} %collective-permute-done.4.other_ref, bf16[4,400,256]{2,1,0:T(8,128)(2,1)S(1)} %pad_maximum_fusion.1.mine_ref.more_ref, ...), custom_call_target="tpu_custom_call" | custom-call | flops 5500000256 | tf_op jit(solution)/shard_map/weight_grad/pallas_call | solution.py:267
  93.0 0.7 copy.16
  93.7 0.7 copy.17
  (44 shorter events, 0.1 us)
Async XLA Ops:
  0.6 16.7 %copy-start.9 = (s32[8,3,2]{0,2,1:T(2,128)S(1)}, s32[8,3,2]{0,2,1:T(2,128)}, u32[]{:S(2)}) copy-start(s32[8,3,2]{0,2,1:T(2,128)} %param.13) | copy-start | bytes 580
  0.6 17.0 %copy-start.10 = (s32[1,2]{1,0:T(1,128)S(1)}, s32[1,2]{1,0:T(1,128)}, u32[]{:S(2)}) copy-start(s32[1,2]{1,0:T(1,128)} %param.14) | copy-start | bytes 28
  0.7 24.3 %collective-permute-start.5 = (bf16[3,4096,256]{2,1,0:T(8,128)(2,1)}, bf16[3,4096,256]{2,1,0:T(8,128)(2,1)}, u32[]{:S(2)}, u32[]{:S(2)}) collective-permute-start(bf16[3,4096,256]{2,1,0:T(8,128)(2,1)} %bitcast.31), channel_id=1, source_target_pairs={{0,1},{1,0},{2,3},{3,2},{4,5},{5,4},{6,7},{7,6},{8,9},{9,8},{10,11... | collective-permute-start | bytes 18874376 | tf_op jit(solution)/shard_map/ppermute | solution.py:347
  4.0 0.9 copy-start.3
  4.9 0.7 copy-start.6
  5.6 12.0 %copy-start.11 = (s32[8]{0:T(128)S(1)}, s32[8]{0:T(128)}, u32[]{:S(2)}) copy-start(s32[8]{0:T(128)} %constant.32.clone) | copy-start | bytes 100
  6.0 8.0 %collective-permute-start.3 = (bf16[400,256]{1,0:T(8,128)(2,1)S(1)}, bf16[400,256]{1,0:T(8,128)(2,1)S(1)}, u32[]{:S(2)}, u32[]{:S(2)}) collective-permute-start(bf16[400,256]{1,0:T(8,128)(2,1)S(1)} %pack_bwd.1), channel_id=1, source_target_pairs={{0,6},{1,7},{2,4},{3,5},{4,2},{5,3},{6,0},{7,1},{8,14},{9,15},{10,... | collective-permute-start | bytes 614408 | tf_op jit(solution)/shard_map/ppermute | solution.py:343
  7.1 6.9 %collective-permute-start.2 = (bf16[400,256]{1,0:T(8,128)(2,1)S(1)}, bf16[400,256]{1,0:T(8,128)(2,1)S(1)}, u32[]{:S(2)}, u32[]{:S(2)}) collective-permute-start(bf16[400,256]{1,0:T(8,128)(2,1)S(1)} %pack_bwd.1), channel_id=1, source_target_pairs={{0,2},{1,3},{2,0},{3,1},{4,6},{5,7},{6,4},{7,5},{8,10},{9,11},{10,... | collective-permute-start | bytes 614408 | tf_op jit(solution)/shard_map/ppermute | solution.py:343
  7.1 6.9 %collective-permute-start.1 = (bf16[400,256]{1,0:T(8,128)(2,1)S(1)}, bf16[400,256]{1,0:T(8,128)(2,1)S(1)}, u32[]{:S(2)}, u32[]{:S(2)}) collective-permute-start(bf16[400,256]{1,0:T(8,128)(2,1)S(1)} %pack_bwd.1), channel_id=1, source_target_pairs={{0,8},{1,9},{2,10},{3,11},{4,12},{5,13},{6,14},{7,15},{8,0},{9,1},... | collective-permute-start | bytes 614408 | tf_op jit(solution)/shard_map/ppermute | solution.py:343
  8.3 0.9 copy-start.1
  9.2 0.7 copy-start.7
  14.0 18.3 %copy-start.5 = (bf16[1,384,256]{2,1,0:T(8,128)(2,1)S(1)}, bf16[1,384,256]{2,1,0:T(8,128)(2,1)}, u32[]{:S(2)}) copy-start(bf16[1,384,256]{2,1,0:T(8,128)(2,1)} %param.10) | copy-start | bytes 589828
  14.1 6.1 %collective-permute-start.4 = (bf16[4,400,256]{2,1,0:T(8,128)(2,1)S(1)}, bf16[4,400,256]{2,1,0:T(8,128)(2,1)S(1)}, u32[]{:S(2)}, u32[]{:S(2)}) collective-permute-start(bf16[4,400,256]{2,1,0:T(8,128)(2,1)S(1)} %pad_maximum_fusion.mine_ref), channel_id=1, source_target_pairs={{0,1},{1,0},{2,3},{3,2},{4,5},{5,4},{6,7},{7,6},{8,9},{9,8},{10,11... | collective-permute-start | bytes 2457608 | tf_op jit(solution)/shard_map/ppermute | solution.py:347
  15.0 9.9 %collective-permute-start = (bf16[400,256]{1,0:T(8,128)(2,1)S(1)}, bf16[400,256]{1,0:T(8,128)(2,1)S(1)}, u32[]{:S(2)}, u32[]{:S(2)}) collective-permute-start(bf16[400,256]{1,0:T(8,128)(2,1)S(1)} %pack_bwd.1), channel_id=1, source_target_pairs={{0,12},{1,13},{2,14},{3,15},{4,8},{5,9},{6,10},{7,11},{8,4},{9,5},... | collective-permute-start | bytes 614408 | tf_op jit(solution)/shard_map/ppermute | solution.py:343
  17.7 11.1 %collective-permute-start.11 = (bf16[400,256]{1,0:T(8,128)(2,1)S(1)}, bf16[400,256]{1,0:T(8,128)(2,1)S(1)}, u32[]{:S(2)}, u32[]{:S(2)}) collective-permute-start(bf16[400,256]{1,0:T(8,128)(2,1)S(1)} %collective-permute-done.1), channel_id=1, source_target_pairs={{0,6},{1,7},{2,4},{3,5},{4,2},{5,3},{6,0},{7,1},{8,14},{9,15},{10,... | collective-permute-start | bytes 614408 | tf_op jit(solution)/shard_map/ppermute | solution.py:343
  19.9 8.9 %collective-permute-start.10 = (bf16[400,256]{1,0:T(8,128)(2,1)S(1)}, bf16[400,256]{1,0:T(8,128)(2,1)S(1)}, u32[]{:S(2)}, u32[]{:S(2)}) collective-permute-start(bf16[400,256]{1,0:T(8,128)(2,1)S(1)} %collective-permute-done.2), channel_id=1, source_target_pairs={{0,8},{1,9},{2,10},{3,11},{4,12},{5,13},{6,14},{7,15},{8,0},{9,1},... | collective-permute-start | bytes 614408 | tf_op jit(solution)/shard_map/ppermute | solution.py:343
  20.2 8.6 %collective-permute-start.9 = (bf16[400,256]{1,0:T(8,128)(2,1)S(1)}, bf16[400,256]{1,0:T(8,128)(2,1)S(1)}, u32[]{:S(2)}, u32[]{:S(2)}) collective-permute-start(bf16[400,256]{1,0:T(8,128)(2,1)S(1)} %collective-permute-done.3), channel_id=1, source_target_pairs={{0,2},{1,3},{2,0},{3,1},{4,6},{5,7},{6,4},{7,5},{8,10},{9,11},{10,... | collective-permute-start | bytes 614408 | tf_op jit(solution)/shard_map/ppermute | solution.py:343
  20.2 2.8 %copy-start = (bf16[1,4096,3,256]{3,1,2,0:T(8,128)(2,1)S(1)}, bf16[1,4096,3,256]{3,1,2,0:T(8,128)(2,1)}, u32[]{:S(2)}) copy-start(bf16[1,4096,3,256]{3,1,2,0:T(8,128)(2,1)} %param.11) | copy-start | bytes 18874372
  28.9 3.4 %collective-permute-start.12 = (bf16[4,400,256]{2,1,0:T(8,128)(2,1)S(1)}, bf16[4,400,256]{2,1,0:T(8,128)(2,1)S(1)}, u32[]{:S(2)}, u32[]{:S(2)}) collective-permute-start(bf16[4,400,256]{2,1,0:T(8,128)(2,1)S(1)} %pad_maximum_fusion.1.mine_ref.more_ref), channel_id=1, source_target_pairs={{0,1},{1,0},{2,3},{3,2},{4,5},{5,4},{6,7},{7,6},{8,9},{9,8},{10,11... | collective-permute-start | bytes 2457608 | tf_op jit(solution)/shard_map/ppermute | solution.py:347
  29.5 7.8 %collective-permute-start.8 = (bf16[400,256]{1,0:T(8,128)(2,1)S(1)}, bf16[400,256]{1,0:T(8,128)(2,1)S(1)}, u32[]{:S(2)}, u32[]{:S(2)}) collective-permute-start(bf16[400,256]{1,0:T(8,128)(2,1)S(1)} %pack_fwd.1), channel_id=1, source_target_pairs={{0,6},{1,7},{2,4},{3,5},{4,2},{5,3},{6,0},{7,1},{8,14},{9,15},{10,... | collective-permute-start | bytes 614408 | tf_op jit(solution)/shard_map/ppermute | solution.py:343
  31.0 6.4 %collective-permute-start.7 = (bf16[400,256]{1,0:T(8,128)(2,1)S(1)}, bf16[400,256]{1,0:T(8,128)(2,1)S(1)}, u32[]{:S(2)}, u32[]{:S(2)}) collective-permute-start(bf16[400,256]{1,0:T(8,128)(2,1)S(1)} %pack_fwd.1), channel_id=1, source_target_pairs={{0,2},{1,3},{2,0},{3,1},{4,6},{5,7},{6,4},{7,5},{8,10},{9,11},{10,... | collective-permute-start | bytes 614408 | tf_op jit(solution)/shard_map/ppermute | solution.py:343
  31.1 6.3 %collective-permute-start.6 = (bf16[400,256]{1,0:T(8,128)(2,1)S(1)}, bf16[400,256]{1,0:T(8,128)(2,1)S(1)}, u32[]{:S(2)}, u32[]{:S(2)}) collective-permute-start(bf16[400,256]{1,0:T(8,128)(2,1)S(1)} %pack_fwd.1), channel_id=1, source_target_pairs={{0,8},{1,9},{2,10},{3,11},{4,12},{5,13},{6,14},{7,15},{8,0},{9,1},... | collective-permute-start | bytes 614408 | tf_op jit(solution)/shard_map/ppermute | solution.py:343
  37.4 5.6 %collective-permute-start.16 = (bf16[400,768]{1,0:T(8,128)(2,1)S(1)}, bf16[400,768]{1,0:T(8,128)(2,1)S(1)}, u32[]{:S(2)}, u32[]{:S(2)}) collective-permute-start(bf16[400,768]{1,0:T(8,128)(2,1)S(1)} %get-tuple-element.90.mine_ref.g_ref), channel_id=1, source_target_pairs={{0,1},{1,0},{2,3},{3,2},{4,5},{5,4},{6,7},{7,6},{8,9},{9,8},{10,11... | collective-permute-start | bytes 1843208 | tf_op jit(solution)/shard_map/ppermute | solution.py:347
  38.6 8.7 %collective-permute-start.13 = (bf16[400,256]{1,0:T(8,128)(2,1)S(1)}, bf16[400,256]{1,0:T(8,128)(2,1)S(1)}, u32[]{:S(2)}, u32[]{:S(2)}) collective-permute-start(bf16[400,256]{1,0:T(8,128)(2,1)S(1)} %collective-permute-done.8), channel_id=1, source_target_pairs={{0,2},{1,3},{2,0},{3,1},{4,6},{5,7},{6,4},{7,5},{8,10},{9,11},{10,... | collective-permute-start | bytes 614408 | tf_op jit(solution)/shard_map/ppermute | solution.py:343
  39.9 7.3 %collective-permute-start.14 = (bf16[400,256]{1,0:T(8,128)(2,1)S(1)}, bf16[400,256]{1,0:T(8,128)(2,1)S(1)}, u32[]{:S(2)}, u32[]{:S(2)}) collective-permute-start(bf16[400,256]{1,0:T(8,128)(2,1)S(1)} %collective-permute-done.7), channel_id=1, source_target_pairs={{0,8},{1,9},{2,10},{3,11},{4,12},{5,13},{6,14},{7,15},{8,0},{9,1},... | collective-permute-start | bytes 614408 | tf_op jit(solution)/shard_map/ppermute | solution.py:343
  40.7 7.7 %collective-permute-start.15 = (bf16[400,256]{1,0:T(8,128)(2,1)S(1)}, bf16[400,256]{1,0:T(8,128)(2,1)S(1)}, u32[]{:S(2)}, u32[]{:S(2)}) collective-permute-start(bf16[400,256]{1,0:T(8,128)(2,1)S(1)} %collective-permute-done.6), channel_id=1, source_target_pairs={{0,6},{1,7},{2,4},{3,5},{4,2},{5,3},{6,0},{7,1},{8,14},{9,15},{10,... | collective-permute-start | bytes 614408 | tf_op jit(solution)/shard_map/ppermute | solution.py:343
  42.2 16.1 %collective-permute-start.18 = (bf16[400,256]{1,0:T(8,128)(2,1)S(1)}, bf16[400,256]{1,0:T(8,128)(2,1)S(1)}, u32[]{:S(2)}, u32[]{:S(2)}) collective-permute-start(bf16[400,256]{1,0:T(8,128)(2,1)S(1)} %pack_fwd.1), channel_id=1, source_target_pairs={{0,12},{1,13},{2,14},{3,15},{4,8},{5,9},{6,10},{7,11},{8,4},{9,5},... | collective-permute-start | bytes 614408 | tf_op jit(solution)/shard_map/ppermute | solution.py:343
  48.5 22.4 %slice-start = ((s8[6291456]{0:T(1024)(128)(4,1)}), s8[4194304]{0:T(1024)(128)(4,1)S(1)}, s32[]{:S(2)}) async-start(s8[6291456]{0:T(1024)(128)(4,1)} %bitcast.36), calls=%async_computation | async-start | bytes 8388608
  48.6 22.3 %slice-start.1 = ((s8[6291456]{0:T(1024)(128)(4,1)}), s8[2097152]{0:T(1024)(128)(4,1)S(1)}, s32[]{:S(2)}) async-start(s8[6291456]{0:T(1024)(128)(4,1)} %bitcast.36), calls=%async_computation.1 | async-start | bytes 4194304
  48.6 21.1 %collective-permute-start.17 = (bf16[4,400,256]{2,1,0:T(8,128)(2,1)S(1)}, bf16[4,400,256]{2,1,0:T(8,128)(2,1)S(1)}, u32[]{:S(2)}, u32[]{:S(2)}) collective-permute-start(bf16[4,400,256]{2,1,0:T(8,128)(2,1)S(1)} %pad_maximum_fusion.2.mine_ref), channel_id=1, source_target_pairs={{0,1},{1,0},{2,3},{3,2},{4,5},{5,4},{6,7},{7,6},{8,9},{9,8},{10,11... | collective-permute-start | bytes 2457608 | tf_op jit(solution)/shard_map/ppermute | solution.py:347
  58.4 14.4 %collective-permute-start.19 = (bf16[4,400,256]{2,1,0:T(8,128)(2,1)S(1)}, bf16[4,400,256]{2,1,0:T(8,128)(2,1)S(1)}, u32[]{:S(2)}, u32[]{:S(2)}) collective-permute-start(bf16[4,400,256]{2,1,0:T(8,128)(2,1)S(1)} %pad_maximum_fusion.3.mine_ref), channel_id=1, source_target_pairs={{0,1},{1,0},{2,3},{3,2},{4,5},{5,4},{6,7},{7,6},{8,9},{9,8},{10,11... | collective-permute-start | bytes 2457608 | tf_op jit(solution)/shard_map/ppermute | solution.py:347
  58.6 7.5 %collective-permute-start.21 = (bf16[400,256]{1,0:T(8,128)(2,1)S(1)}, bf16[400,256]{1,0:T(8,128)(2,1)S(1)}, u32[]{:S(2)}, u32[]{:S(2)}) collective-permute-start(bf16[400,256]{1,0:T(8,128)(2,1)S(1)} %get-tuple-element.98), channel_id=1, source_target_pairs={{0,6},{1,7},{2,4},{3,5},{4,2},{5,3},{6,0},{7,1},{8,14},{9,15},{10,... | collective-permute-start | bytes 614408 | tf_op jit(solution)/shard_map/ppermute | solution.py:343
  60.2 5.9 %collective-permute-start.22 = (bf16[400,256]{1,0:T(8,128)(2,1)S(1)}, bf16[400,256]{1,0:T(8,128)(2,1)S(1)}, u32[]{:S(2)}, u32[]{:S(2)}) collective-permute-start(bf16[400,256]{1,0:T(8,128)(2,1)S(1)} %get-tuple-element.101), channel_id=1, source_target_pairs={{0,8},{1,9},{2,10},{3,11},{4,12},{5,13},{6,14},{7,15},{8,0},{9,1},... | collective-permute-start | bytes 614408 | tf_op jit(solution)/shard_map/ppermute | solution.py:343
  60.6 5.7 %collective-permute-start.23 = (bf16[400,256]{1,0:T(8,128)(2,1)S(1)}, bf16[400,256]{1,0:T(8,128)(2,1)S(1)}, u32[]{:S(2)}, u32[]{:S(2)}) collective-permute-start(bf16[400,256]{1,0:T(8,128)(2,1)S(1)} %get-tuple-element.102), channel_id=1, source_target_pairs={{0,2},{1,3},{2,0},{3,1},{4,6},{5,7},{6,4},{7,5},{8,10},{9,11},{10,... | collective-permute-start | bytes 614408 | tf_op jit(solution)/shard_map/ppermute | solution.py:343
  66.2 13.8 %collective-permute-start.27 = (bf16[400,256]{1,0:T(8,128)(2,1)S(1)}, bf16[400,256]{1,0:T(8,128)(2,1)S(1)}, u32[]{:S(2)}, u32[]{:S(2)}) collective-permute-start(bf16[400,256]{1,0:T(8,128)(2,1)S(1)} %get-tuple-element.106), channel_id=1, source_target_pairs={{0,12},{1,13},{2,14},{3,15},{4,8},{5,9},{6,10},{7,11},{8,4},{9,5},... | collective-permute-start | bytes 614408 | tf_op jit(solution)/shard_map/ppermute | solution.py:343
  66.2 6.6 %copy-start.2 = (bf16[1,384,256]{2,1,0:T(8,128)(2,1)S(1)}, bf16[1,384,256]{2,1,0:T(8,128)(2,1)}, u32[]{:S(2)}) copy-start(bf16[1,384,256]{2,1,0:T(8,128)(2,1)} %param.8) | copy-start | bytes 589828
  66.4 13.5 %collective-permute-start.24 = (bf16[400,256]{1,0:T(8,128)(2,1)S(1)}, bf16[400,256]{1,0:T(8,128)(2,1)S(1)}, u32[]{:S(2)}, u32[]{:S(2)}) collective-permute-start(bf16[400,256]{1,0:T(8,128)(2,1)S(1)} %get-tuple-element.103), channel_id=1, source_target_pairs={{0,8},{1,9},{2,10},{3,11},{4,12},{5,13},{6,14},{7,15},{8,0},{9,1},... | collective-permute-start | bytes 614408 | tf_op jit(solution)/shard_map/ppermute | solution.py:343
  67.5 12.4 %collective-permute-start.25 = (bf16[400,256]{1,0:T(8,128)(2,1)S(1)}, bf16[400,256]{1,0:T(8,128)(2,1)S(1)}, u32[]{:S(2)}, u32[]{:S(2)}) collective-permute-start(bf16[400,256]{1,0:T(8,128)(2,1)S(1)} %get-tuple-element.104), channel_id=1, source_target_pairs={{0,2},{1,3},{2,0},{3,1},{4,6},{5,7},{6,4},{7,5},{8,10},{9,11},{10,... | collective-permute-start | bytes 614408 | tf_op jit(solution)/shard_map/ppermute | solution.py:343
  69.7 10.2 %collective-permute-start.26 = (bf16[400,256]{1,0:T(8,128)(2,1)S(1)}, bf16[400,256]{1,0:T(8,128)(2,1)S(1)}, u32[]{:S(2)}, u32[]{:S(2)}) collective-permute-start(bf16[400,256]{1,0:T(8,128)(2,1)S(1)} %get-tuple-element.105), channel_id=1, source_target_pairs={{0,6},{1,7},{2,4},{3,5},{4,2},{5,3},{6,0},{7,1},{8,14},{9,15},{10,... | collective-permute-start | bytes 614408 | tf_op jit(solution)/shard_map/ppermute | solution.py:343
  72.8 7.1 %copy-start.4 = (bf16[1,384,256]{2,1,0:T(8,128)(2,1)S(1)}, bf16[1,384,256]{2,1,0:T(8,128)(2,1)}, u32[]{:S(2)}) copy-start(bf16[1,384,256]{2,1,0:T(8,128)(2,1)} %param.9) | copy-start | bytes 589828
  72.8 7.1 %copy-start.8 = (f32[1,256]{1,0:T(1,128)S(1)}, f32[1,256]{1,0:T(1,128)}, u32[]{:S(2)}) copy-start(f32[1,256]{1,0:T(1,128)} %refs_6_.1) | copy-start | bytes 3076
  77.3 15.7 %collective-permute-start.20 = (bf16[384,256]{1,0:T(8,128)(2,1)S(1)}, bf16[384,256]{1,0:T(8,128)(2,1)S(1)}, u32[]{:S(2)}, u32[]{:S(2)}) collective-permute-start(bf16[384,256]{1,0:T(8,128)(2,1)S(1)} %forward.1), channel_id=1, source_target_pairs={{240,0},{0,16},{16,32},{32,48},{48,64},{64,80},{80,96},{96,112},{1... | collective-permute-start | bytes 589832 | tf_op jit(solution)/shard_map/ppermute | solution.py:352
  80.8 12.2 %collective-permute-start.28 = (bf16[384,256]{1,0:T(8,128)(2,1)S(1)}, bf16[384,256]{1,0:T(8,128)(2,1)S(1)}, u32[]{:S(2)}, u32[]{:S(2)}) collective-permute-start(bf16[384,256]{1,0:T(8,128)(2,1)S(1)} %get-tuple-element.112), channel_id=1, source_target_pairs={{16,0},{32,16},{48,32},{64,48},{80,64},{96,80},{112,96},{128,112},... | collective-permute-start | bytes 589832 | tf_op jit(solution)/shard_map/ppermute | solution.py:352

commit v5 on v4

--- a/solution.py
+++ b/solution.py
@@ -451,9 +451,7 @@
 
     for_2, for_5, for_7, for_6 = input_grads((4, 5, 6, 7), grads, "input_grad_far", [block] * 4)
     alone = jax.ShapeDtypeStruct((tokens, local), F32)
-    far_fwd, near_fwd, for_2, for_5, for_7, later = tie(
-        (far_fwd, near_fwd, for_2, for_5, for_7, grads)
-    )
+    later, for_7 = tie((grads, for_7))
     came = [to_chip(for_7, 3), to_chip(for_5, 4), to_chip(for_2, 1)]
     *parts, own, pair = input_grads(
         (1, 2, 3, 0),
@@ -461,8 +459,9 @@
         "input_grad_near",
         [alone] * 4 + [jax.ShapeDtypeStruct((STAT, local), BF16)],
     )
-    last_fwd, pair = tie((last_fwd, pair))
-    came[0], for_6 = tie((came[0], for_6))
+    far_fwd, near_fwd, last_fwd, pair = tie((far_fwd, near_fwd, last_fwd, pair))
+    grad_w = weight_grad(ints, (mine_a, other_a, mine_b, other_b), grads)
+    came, for_6, grad_w = tie((came, for_6, grad_w))
     direct = to_chip(for_6, 6)
     sums = plain_call(add_kernel, [block] * 3, "add", 1.0, pair, *parts, *came)
     gone = [to_chip(part, d) for part, d in zip(sums, NEAR[1:])] + [direct]
@@ -489,7 +488,6 @@
     )
     sent_on = shifted(result, "section", 1)
     gone, result = tie((gone, result))
-    grad_w = weight_grad(ints, (mine_a, other_a, mine_b, other_b), grads)
     grad_x, grad_gain = plain_call(
         finish_kernel,
         (narrow, jax.ShapeDtypeStruct((1, local), F32)),

time: 94.6 us -> 90.8 us (0.960)
  the two profiles are of different devices: /device:TPU:1 before, /device:TPU:8 now
where the time goes in v5:
time: 90.8 us; the launch traced here: 90 us
  starting transfers between devices  39.4 us (43%)
  Pallas kernels  28.3 us (31%)
  waiting for transfers between devices  13.2 us (15%)
  local copies, waits for them, and re-layouts  7.68 us (8%)
  between operations  1 us (1%)
    ppermute x21, starting transfers between devices, to_chip(): return lax.ppermute(block, 'fsdp', route)  30.1 us
    pallas_call x8, Pallas kernels, plain_call(): pl.pallas_call(kernel, out_shape=out_shape, in_specs=specs, out_specs=jax...  22.3 us
    ppermute x2, starting transfers between devices, shifted(): lax.ppermute(block, axis, [((i - distance) % count, i) for i in range(cou...  8.79 us
    ppermute x21, waiting for transfers between devices, to_chip(): return lax.ppermute(block, 'fsdp', route)  7.5 us
    unnamed x31, local copies, waits for them, and re-layouts  7.49 us
    ppermute x2, waiting for transfers between devices, shifted(): lax.ppermute(block, axis, [((i - distance) % count, i) for i in range(cou...  5.68 us
    pallas_call x1, Pallas kernels, weight_grad(): pl.pallas_call(weight_grad_kernel, out_shape=jax.ShapeDtypeStruct((3, 2 *...  5.18 us
  transfers between devices with their start and end apart: 29, of which 8 were waited for; matrix products, arithmetic and copies ran while one was open for 1% of the time, Pallas kernels for 31%

profile of v5, /device:TPU:8, one launch (start us, length us, event | category | flops | bytes accessed | tf_op | source)
XLA Modules:
  0.0 90.0 jit_solution(12836201924776297582)
XLA Ops:
  0.7 0.1 collective-permute-start.5
  0.8 0.9 %copy-done.3 = bf16[1,384,256]{2,1,0:T(8,128)(2,1)S(1)} copy-done((bf16[1,384,256]{2,1,0:T(8,128)(2,1)S(1)}, bf16[1,384,256]{2,1,0:T(8,128)(2,1)}, u32[]{:S(2)}) %copy-start.3) | copy-done | bytes 196632
  1.7 0.7 copy-done.6
  2.4 0.4 pack_bwd.1
  2.8 1.7 %collective-permute-start.3 = (bf16[400,256]{1,0:T(8,128)(2,1)S(1)}, bf16[400,256]{1,0:T(8,128)(2,1)S(1)}, u32[]{:S(2)}, u32[]{:S(2)}) collective-permute-start(bf16[400,256]{1,0:T(8,128)(2,1)S(1)} %pack_bwd.1), channel_id=1, source_target_pairs={{0,6},{1,7},{2,4},{3,5},{4,2},{5,3},{6,0},{7,1},{8,14},{9,15},{10,... | collective-permute-start | bytes 614408 | tf_op jit(solution)/shard_map/ppermute | solution.py:343
  4.4 1.9 %collective-permute-start.2 = (bf16[400,256]{1,0:T(8,128)(2,1)S(1)}, bf16[400,256]{1,0:T(8,128)(2,1)S(1)}, u32[]{:S(2)}, u32[]{:S(2)}) collective-permute-start(bf16[400,256]{1,0:T(8,128)(2,1)S(1)} %pack_bwd.1), channel_id=1, source_target_pairs={{0,2},{1,3},{2,0},{3,1},{4,6},{5,7},{6,4},{7,5},{8,10},{9,11},{10,... | collective-permute-start | bytes 614408 | tf_op jit(solution)/shard_map/ppermute | solution.py:343
  6.3 1.5 %collective-permute-start.1 = (bf16[400,256]{1,0:T(8,128)(2,1)S(1)}, bf16[400,256]{1,0:T(8,128)(2,1)S(1)}, u32[]{:S(2)}, u32[]{:S(2)}) collective-permute-start(bf16[400,256]{1,0:T(8,128)(2,1)S(1)} %pack_bwd.1), channel_id=1, source_target_pairs={{0,8},{1,9},{2,10},{3,11},{4,12},{5,13},{6,14},{7,15},{8,0},{9,1},... | collective-permute-start | bytes 614408 | tf_op jit(solution)/shard_map/ppermute | solution.py:343
  7.8 0.9 %copy-done.1 = bf16[1,384,256]{2,1,0:T(8,128)(2,1)S(1)} copy-done((bf16[1,384,256]{2,1,0:T(8,128)(2,1)S(1)}, bf16[1,384,256]{2,1,0:T(8,128)(2,1)}, u32[]{:S(2)}) %copy-start.1) | copy-done | bytes 196632
  8.7 0.7 copy-done.7
  9.4 0.4 pack_fwd.1
  9.8 0.5 collective-permute-done.3
  10.3 1.4 %collective-permute-done.2 = bf16[400,256]{1,0:T(8,128)(2,1)S(1)} collective-permute-done((bf16[400,256]{1,0:T(8,128)(2,1)S(1)}, bf16[400,256]{1,0:T(8,128)(2,1)S(1)}, u32[]{:S(2)}, u32[]{:S(2)}) %collective-permute-start.2) | collective-permute-done | bytes 204832 | tf_op jit(solution)/shard_map/ppermute | solution.py:343
  11.8 1.5 %collective-permute-done.1 = bf16[400,256]{1,0:T(8,128)(2,1)S(1)} collective-permute-done((bf16[400,256]{1,0:T(8,128)(2,1)S(1)}, bf16[400,256]{1,0:T(8,128)(2,1)S(1)}, u32[]{:S(2)}, u32[]{:S(2)}) %collective-permute-start.1) | collective-permute-done | bytes 204832 | tf_op jit(solution)/shard_map/ppermute | solution.py:343
  13.2 0.1 pad_maximum_fusion.mine_ref
  13.4 0.1 collective-permute-start.4
  13.5 1.6 %collective-permute-start = (bf16[400,256]{1,0:T(8,128)(2,1)S(1)}, bf16[400,256]{1,0:T(8,128)(2,1)S(1)}, u32[]{:S(2)}, u32[]{:S(2)}) collective-permute-start(bf16[400,256]{1,0:T(8,128)(2,1)S(1)} %pack_bwd.1), channel_id=1, source_target_pairs={{0,12},{1,13},{2,14},{3,15},{4,8},{5,9},{6,10},{7,11},{8,4},{9,5},... | collective-permute-start | bytes 614408 | tf_op jit(solution)/shard_map/ppermute | solution.py:343
  15.1 0.1 copy.13
  15.2 0.1 reshape.14
  15.3 0.1 concatenate.3.ints_ref
  15.4 1.2 %collective-permute-start.11 = (bf16[400,256]{1,0:T(8,128)(2,1)S(1)}, bf16[400,256]{1,0:T(8,128)(2,1)S(1)}, u32[]{:S(2)}, u32[]{:S(2)}) collective-permute-start(bf16[400,256]{1,0:T(8,128)(2,1)S(1)} %collective-permute-done.1), channel_id=1, source_target_pairs={{0,6},{1,7},{2,4},{3,5},{4,2},{5,3},{6,0},{7,1},{8,14},{9,15},{10,... | collective-permute-start | bytes 614408 | tf_op jit(solution)/shard_map/ppermute | solution.py:343
  16.6 0.8 collective-permute-start.10
  17.3 2.7 %collective-permute-start.9 = (bf16[400,256]{1,0:T(8,128)(2,1)S(1)}, bf16[400,256]{1,0:T(8,128)(2,1)S(1)}, u32[]{:S(2)}, u32[]{:S(2)}) collective-permute-start(bf16[400,256]{1,0:T(8,128)(2,1)S(1)} %collective-permute-done.3), channel_id=1, source_target_pairs={{0,2},{1,3},{2,0},{3,1},{4,6},{5,7},{6,4},{7,5},{8,10},{9,11},{10,... | collective-permute-start | bytes 614408 | tf_op jit(solution)/shard_map/ppermute | solution.py:343
  20.1 2.8 %copy-done = bf16[1,4096,3,256]{3,1,2,0:T(8,128)(2,1)S(1)} copy-done((bf16[1,4096,3,256]{3,1,2,0:T(8,128)(2,1)S(1)}, bf16[1,4096,3,256]{3,1,2,0:T(8,128)(2,1)}, u32[]{:S(2)}) %copy-start) | copy-done | bytes 6291480
  22.9 1.9 %first_bwd.1 = (f32[384,768]{1,0:T(8,128)S(1)}, f32[16,256]{1,0:T(8,128)S(1)}) custom-call(s32[75]{0:T(128)S(1)} %concatenate.3.ints_ref, bf16[4,400,256]{2,1,0:T(8,128)(2,1)S(1)} %pad_maximum_fusion.mine_ref, bf16[4,400,256]{2,1,0:T(8,128)(2,1)S(1)} %collective-permute-done.4.other_ref, bf16[3,4096,256]{2,1,0:T(8,128)(2,1)S(1)} %bitcast.32), custom_call_target="tpu_custom_call" | custom-call | flops 2750000128 | tf_op jit(solution)/shard_map/first_bwd/pallas_call | solution.py:310
  24.8 2.2 %collective-permute-done.11 = bf16[400,256]{1,0:T(8,128)(2,1)S(1)} collective-permute-done((bf16[400,256]{1,0:T(8,128)(2,1)S(1)}, bf16[400,256]{1,0:T(8,128)(2,1)S(1)}, u32[]{:S(2)}, u32[]{:S(2)}) %collective-permute-start.11) | collective-permute-done | bytes 204832 | tf_op jit(solution)/shard_map/ppermute | solution.py:343
  27.0 0.7 collective-permute-done.9
  27.7 0.1 pad_maximum_fusion.1.mine_ref.more_ref
  27.8 0.1 collective-permute-start.12
  27.9 0.8 collective-permute-start.8
  28.6 1.6 %collective-permute-start.7 = (bf16[400,256]{1,0:T(8,128)(2,1)S(1)}, bf16[400,256]{1,0:T(8,128)(2,1)S(1)}, u32[]{:S(2)}, u32[]{:S(2)}) collective-permute-start(bf16[400,256]{1,0:T(8,128)(2,1)S(1)} %pack_fwd.1), channel_id=1, source_target_pairs={{0,2},{1,3},{2,0},{3,1},{4,6},{5,7},{6,4},{7,5},{8,10},{9,11},{10,... | collective-permute-start | bytes 614408 | tf_op jit(solution)/shard_map/ppermute | solution.py:343
  30.3 1.1 %collective-permute-start.6 = (bf16[400,256]{1,0:T(8,128)(2,1)S(1)}, bf16[400,256]{1,0:T(8,128)(2,1)S(1)}, u32[]{:S(2)}, u32[]{:S(2)}) collective-permute-start(bf16[400,256]{1,0:T(8,128)(2,1)S(1)} %pack_fwd.1), channel_id=1, source_target_pairs={{0,8},{1,9},{2,10},{3,11},{4,12},{5,13},{6,14},{7,15},{8,0},{9,1},... | collective-permute-start | bytes 614408 | tf_op jit(solution)/shard_map/ppermute | solution.py:343
  31.4 4.6 %backward.1 = (bf16[400,768]{1,0:T(8,128)(2,1)S(1)}, f32[384,128]{1,0:T(8,128)S(1)}) custom-call(s32[75]{0:T(128)S(1)} %concatenate.3.ints_ref, f32[384,768]{1,0:T(8,128)S(1)} %get-tuple-element.69.first_ref, f32[16,256]{1,0:T(8,128)S(1)} %get-tuple-element.70.stat_ref, bf16[4,400,256]{2,1,0:T(8,128)(2,1)S(1)} %pad_maximum_fusion.1.mine_ref.more_ref, ...), custom_call_target="tpu_custom_call" | custom-call | flops 6600000000 | tf_op jit(solution)/shard_map/backward/pallas_call | solution.py:310
  35.9 1.2 %collective-permute-done.6 = bf16[400,256]{1,0:T(8,128)(2,1)S(1)} collective-permute-done((bf16[400,256]{1,0:T(8,128)(2,1)S(1)}, bf16[400,256]{1,0:T(8,128)(2,1)S(1)}, u32[]{:S(2)}, u32[]{:S(2)}) %collective-permute-start.6) | collective-permute-done | bytes 204832 | tf_op jit(solution)/shard_map/ppermute | solution.py:343
  37.1 0.4 collective-permute-start.13
  37.5 1.5 %collective-permute-start.14 = (bf16[400,256]{1,0:T(8,128)(2,1)S(1)}, bf16[400,256]{1,0:T(8,128)(2,1)S(1)}, u32[]{:S(2)}, u32[]{:S(2)}) collective-permute-start(bf16[400,256]{1,0:T(8,128)(2,1)S(1)} %collective-permute-done.7), channel_id=1, source_target_pairs={{0,8},{1,9},{2,10},{3,11},{4,12},{5,13},{6,14},{7,15},{8,0},{9,1},... | collective-permute-start | bytes 614408 | tf_op jit(solution)/shard_map/ppermute | solution.py:343
  39.0 0.6 collective-permute-start.15
  39.6 3.1 %collective-permute-start.16 = (bf16[400,256]{1,0:T(8,128)(2,1)S(1)}, bf16[400,256]{1,0:T(8,128)(2,1)S(1)}, u32[]{:S(2)}, u32[]{:S(2)}) collective-permute-start(bf16[400,256]{1,0:T(8,128)(2,1)S(1)} %pack_fwd.1), channel_id=1, source_target_pairs={{0,12},{1,13},{2,14},{3,15},{4,8},{5,9},{6,10},{7,11},{8,4},{9,5},... | collective-permute-start | bytes 614408 | tf_op jit(solution)/shard_map/ppermute | solution.py:343
  42.7 4.2 %input_grad_far.1 = (bf16[400,256]{1,0:T(8,128)(2,1)S(1)}, bf16[400,256]{1,0:T(8,128)(2,1)S(1)}, bf16[400,256]{1,0:T(8,128)(2,1)S(1)}, bf16[400,256]{1,0:T(8,128)(2,1)S(1)}) custom-call(s32[75]{0:T(128)S(1)} %concatenate.3.ints_ref, bf16[400,768]{1,0:T(8,128)(2,1)S(1)} %get-tuple-element.80.mine_ref.g_ref, ...), custom_call_target="tpu_custom_call" | custom-call | flops 3849999872 | tf_op jit(solution)/shard_map/input_grad_far/pallas_call | solution.py:310
  46.9 4.2 %input_grad_near.1 = (f32[384,256]{1,0:T(8,128)S(1)}, f32[384,256]{1,0:T(8,128)S(1)}, f32[384,256]{1,0:T(8,128)S(1)}, f32[384,256]{1,0:T(8,128)S(1)}, bf16[16,256]{1,0:T(8,128)(2,1)S(1)}) custom-call(s32[75]{0:T(128)S(1)} %concatenate.3.ints_ref, bf16[400,768]{1,0:T(8,128)(2,1)S(1)} %get-tuple-element.80.mine_ref.g_ref, ...), custom_call_target="tpu_custom_call" | custom-call | flops 3849999872 | tf_op jit(solution)/shard_map/input_grad_near/pallas_call | solution.py:310
  51.2 0.1 pad_maximum_fusion.2.mine_ref
  51.3 0.1 collective-permute-start.18
  51.4 1.0 %collective-permute-start.21 = (bf16[400,256]{1,0:T(8,128)(2,1)S(1)}, bf16[400,256]{1,0:T(8,128)(2,1)S(1)}, u32[]{:S(2)}, u32[]{:S(2)}) collective-permute-start(bf16[400,256]{1,0:T(8,128)(2,1)S(1)} %get-tuple-element.97), channel_id=1, source_target_pairs={{0,6},{1,7},{2,4},{3,5},{4,2},{5,3},{6,0},{7,1},{8,14},{9,15},{10,... | collective-permute-start | bytes 614408 | tf_op jit(solution)/shard_map/ppermute | solution.py:343
  52.4 1.2 %collective-permute-start.22 = (bf16[400,256]{1,0:T(8,128)(2,1)S(1)}, bf16[400,256]{1,0:T(8,128)(2,1)S(1)}, u32[]{:S(2)}, u32[]{:S(2)}) collective-permute-start(bf16[400,256]{1,0:T(8,128)(2,1)S(1)} %get-tuple-element.98), channel_id=1, source_target_pairs={{0,8},{1,9},{2,10},{3,11},{4,12},{5,13},{6,14},{7,15},{8,0},{9,1},... | collective-permute-start | bytes 614408 | tf_op jit(solution)/shard_map/ppermute | solution.py:343
  53.7 1.9 %collective-permute-start.23 = (bf16[400,256]{1,0:T(8,128)(2,1)S(1)}, bf16[400,256]{1,0:T(8,128)(2,1)S(1)}, u32[]{:S(2)}, u32[]{:S(2)}) collective-permute-start(bf16[400,256]{1,0:T(8,128)(2,1)S(1)} %get-tuple-element.99), channel_id=1, source_target_pairs={{0,2},{1,3},{2,0},{3,1},{4,6},{5,7},{6,4},{7,5},{8,10},{9,11},{10,... | collective-permute-start | bytes 614408 | tf_op jit(solution)/shard_map/ppermute | solution.py:343
  55.6 0.1 pad_maximum_fusion.3.mine_ref
  55.7 0.0 slice-start.1
  55.7 0.1 collective-permute-start.19
  55.8 5.2 %weight_grad.1 = bf16[3,4096,256]{2,1,0:T(8,128)(2,1)} custom-call(s32[75]{0:T(128)S(1)} %concatenate.3.ints_ref, bf16[4,400,256]{2,1,0:T(8,128)(2,1)S(1)} %pad_maximum_fusion.mine_ref, bf16[4,400,256]{2,1,0:T(8,128)(2,1)S(1)} %collective-permute-done.4.other_ref, bf16[4,400,256]{2,1,0:T(8,128)(2,1)S(1)} %pad_maximum_fusion.1.mine_ref.more_ref, ...), custom_call_target="tpu_custom_call" | custom-call | flops 5500000256 | tf_op jit(solution)/shard_map/weight_grad/pallas_call | solution.py:267
  61.0 0.0 copy-start.2
  61.0 0.2 add.23
  61.2 1.3 %collective-permute-start.24 = (bf16[400,256]{1,0:T(8,128)(2,1)S(1)}, bf16[400,256]{1,0:T(8,128)(2,1)S(1)}, u32[]{:S(2)}, u32[]{:S(2)}) collective-permute-start(bf16[400,256]{1,0:T(8,128)(2,1)S(1)} %get-tuple-element.104), channel_id=1, source_target_pairs={{0,8},{1,9},{2,10},{3,11},{4,12},{5,13},{6,14},{7,15},{8,0},{9,1},... | collective-permute-start | bytes 614408 | tf_op jit(solution)/shard_map/ppermute | solution.py:343
  62.5 1.4 %collective-permute-start.25 = (bf16[400,256]{1,0:T(8,128)(2,1)S(1)}, bf16[400,256]{1,0:T(8,128)(2,1)S(1)}, u32[]{:S(2)}, u32[]{:S(2)}) collective-permute-start(bf16[400,256]{1,0:T(8,128)(2,1)S(1)} %get-tuple-element.105), channel_id=1, source_target_pairs={{0,2},{1,3},{2,0},{3,1},{4,6},{5,7},{6,4},{7,5},{8,10},{9,11},{10,... | collective-permute-start | bytes 614408 | tf_op jit(solution)/shard_map/ppermute | solution.py:343
  63.9 0.9 %collective-permute-start.26 = (bf16[400,256]{1,0:T(8,128)(2,1)S(1)}, bf16[400,256]{1,0:T(8,128)(2,1)S(1)}, u32[]{:S(2)}, u32[]{:S(2)}) collective-permute-start(bf16[400,256]{1,0:T(8,128)(2,1)S(1)} %get-tuple-element.106), channel_id=1, source_target_pairs={{0,6},{1,7},{2,4},{3,5},{4,2},{5,3},{6,0},{7,1},{8,14},{9,15},{10,... | collective-permute-start | bytes 614408 | tf_op jit(solution)/shard_map/ppermute | solution.py:343
  64.8 2.0 %collective-permute-start.27 = (bf16[400,256]{1,0:T(8,128)(2,1)S(1)}, bf16[400,256]{1,0:T(8,128)(2,1)S(1)}, u32[]{:S(2)}, u32[]{:S(2)}) collective-permute-start(bf16[400,256]{1,0:T(8,128)(2,1)S(1)} %get-tuple-element.107), channel_id=1, source_target_pairs={{0,12},{1,13},{2,14},{3,15},{4,8},{5,9},{6,10},{7,11},{8,4},{9,5},... | collective-permute-start | bytes 614408 | tf_op jit(solution)/shard_map/ppermute | solution.py:343
  66.8 1.9 %first_fwd.1 = (f32[384,768]{1,0:T(8,128)S(1)}, f32[16,256]{1,0:T(8,128)S(1)}) custom-call(s32[75]{0:T(128)S(1)} %concatenate.3.ints_ref, bf16[4,400,256]{2,1,0:T(8,128)(2,1)S(1)} %pad_maximum_fusion.2.mine_ref, bf16[4,400,256]{2,1,0:T(8,128)(2,1)S(1)} %collective-permute-done.18.other_ref, bf16[3,4096,256]{2,1,0:T(8,128)(2,1)S(1)} %bitcast.38), custom_call_target="tpu_custom_call" | custom-call | flops 2750000128 | tf_op jit(solution)/shard_map/first_fwd/pallas_call | solution.py:310
  68.8 0.0 copy-start.4
  68.8 4.5 %forward.1 = bf16[384,256]{1,0:T(8,128)(2,1)S(1)} custom-call(s32[75]{0:T(128)S(1)} %concatenate.3.ints_ref, f32[384,768]{1,0:T(8,128)S(1)} %get-tuple-element.86.first_ref, f32[16,256]{1,0:T(8,128)S(1)} %get-tuple-element.87.stat_ref, bf16[4,400,256]{2,1,0:T(8,128)(2,1)S(1)} %pad_maximum_fusion.3.mine_ref, ...), custom_call_target="tpu_custom_call" | custom-call | flops 4950000128 | tf_op jit(solution)/shard_map/forward/pallas_call | solution.py:310
  73.3 2.9 %collective-permute-start.20 = (bf16[384,256]{1,0:T(8,128)(2,1)S(1)}, bf16[384,256]{1,0:T(8,128)(2,1)S(1)}, u32[]{:S(2)}, u32[]{:S(2)}) collective-permute-start(bf16[384,256]{1,0:T(8,128)(2,1)S(1)} %forward.1), channel_id=1, source_target_pairs={{240,0},{0,16},{16,32},{32,48},{48,64},{64,80},{80,96},{96,112},{1... | collective-permute-start | bytes 589832 | tf_op jit(solution)/shard_map/ppermute | solution.py:352
  76.2 0.8 finish.1
  77.0 5.9 %collective-permute-start.28 = (bf16[384,256]{1,0:T(8,128)(2,1)S(1)}, bf16[384,256]{1,0:T(8,128)(2,1)S(1)}, u32[]{:S(2)}, u32[]{:S(2)}) collective-permute-start(bf16[384,256]{1,0:T(8,128)(2,1)S(1)} %get-tuple-element.113), channel_id=1, source_target_pairs={{16,0},{32,16},{48,32},{64,48},{80,64},{96,80},{112,96},{128,112},... | collective-permute-start | bytes 589832 | tf_op jit(solution)/shard_map/ppermute | solution.py:352
  83.0 3.0 %collective-permute-done.20 = bf16[384,256]{1,0:T(8,128)(2,1)S(1)} collective-permute-done((bf16[384,256]{1,0:T(8,128)(2,1)S(1)}, bf16[384,256]{1,0:T(8,128)(2,1)S(1)}, u32[]{:S(2)}, u32[]{:S(2)}) %collective-permute-start.20) | collective-permute-done | bytes 196640 | tf_op jit(solution)/shard_map/ppermute | solution.py:352
  86.0 2.7 %collective-permute-done.28 = bf16[384,256]{1,0:T(8,128)(2,1)S(1)} collective-permute-done((bf16[384,256]{1,0:T(8,128)(2,1)S(1)}, bf16[384,256]{1,0:T(8,128)(2,1)S(1)}, u32[]{:S(2)}, u32[]{:S(2)}) %collective-permute-start.28) | collective-permute-done | bytes 196640 | tf_op jit(solution)/shard_map/ppermute | solution.py:352
  88.7 0.7 copy.16
  89.3 0.7 copy.17
  (44 shorter events, 0.1 us)
Async XLA Ops:
  0.6 14.5 %copy-start.9 = (s32[8,3,2]{0,2,1:T(2,128)S(1)}, s32[8,3,2]{0,2,1:T(2,128)}, u32[]{:S(2)}) copy-start(s32[8,3,2]{0,2,1:T(2,128)} %param.13) | copy-start | bytes 580
  0.6 14.7 %copy-start.10 = (s32[1,2]{1,0:T(1,128)S(1)}, s32[1,2]{1,0:T(1,128)}, u32[]{:S(2)}) copy-start(s32[1,2]{1,0:T(1,128)} %param.14) | copy-start | bytes 28
  0.7 24.2 %collective-permute-start.5 = (bf16[3,4096,256]{2,1,0:T(8,128)(2,1)}, bf16[3,4096,256]{2,1,0:T(8,128)(2,1)}, u32[]{:S(2)}, u32[]{:S(2)}) collective-permute-start(bf16[3,4096,256]{2,1,0:T(8,128)(2,1)} %bitcast.31), channel_id=1, source_target_pairs={{0,1},{1,0},{2,3},{3,2},{4,5},{5,4},{6,7},{7,6},{8,9},{9,8},{10,11... | collective-permute-start | bytes 18874376 | tf_op jit(solution)/shard_map/ppermute | solution.py:347
  0.8 0.9 %copy-start.3 = (bf16[1,384,256]{2,1,0:T(8,128)(2,1)S(1)}, bf16[1,384,256]{2,1,0:T(8,128)(2,1)}, u32[]{:S(2)}) copy-start(bf16[1,384,256]{2,1,0:T(8,128)(2,1)} %param.9) | copy-start | bytes 589828
  1.7 0.7 copy-start.6
  2.4 12.9 %copy-start.11 = (s32[8]{0:T(128)S(1)}, s32[8]{0:T(128)}, u32[]{:S(2)}) copy-start(s32[8]{0:T(128)} %constant.32.clone) | copy-start | bytes 100
  2.8 7.6 %collective-permute-start.3 = (bf16[400,256]{1,0:T(8,128)(2,1)S(1)}, bf16[400,256]{1,0:T(8,128)(2,1)S(1)}, u32[]{:S(2)}, u32[]{:S(2)}) collective-permute-start(bf16[400,256]{1,0:T(8,128)(2,1)S(1)} %pack_bwd.1), channel_id=1, source_target_pairs={{0,6},{1,7},{2,4},{3,5},{4,2},{5,3},{6,0},{7,1},{8,14},{9,15},{10,... | collective-permute-start | bytes 614408 | tf_op jit(solution)/shard_map/ppermute | solution.py:343
  4.4 7.3 %collective-permute-start.2 = (bf16[400,256]{1,0:T(8,128)(2,1)S(1)}, bf16[400,256]{1,0:T(8,128)(2,1)S(1)}, u32[]{:S(2)}, u32[]{:S(2)}) collective-permute-start(bf16[400,256]{1,0:T(8,128)(2,1)S(1)} %pack_bwd.1), channel_id=1, source_target_pairs={{0,2},{1,3},{2,0},{3,1},{4,6},{5,7},{6,4},{7,5},{8,10},{9,11},{10,... | collective-permute-start | bytes 614408 | tf_op jit(solution)/shard_map/ppermute | solution.py:343
  6.3 6.9 %collective-permute-start.1 = (bf16[400,256]{1,0:T(8,128)(2,1)S(1)}, bf16[400,256]{1,0:T(8,128)(2,1)S(1)}, u32[]{:S(2)}, u32[]{:S(2)}) collective-permute-start(bf16[400,256]{1,0:T(8,128)(2,1)S(1)} %pack_bwd.1), channel_id=1, source_target_pairs={{0,8},{1,9},{2,10},{3,11},{4,12},{5,13},{6,14},{7,15},{8,0},{9,1},... | collective-permute-start | bytes 614408 | tf_op jit(solution)/shard_map/ppermute | solution.py:343
  7.8 0.9 %copy-start.1 = (bf16[1,384,256]{2,1,0:T(8,128)(2,1)S(1)}, bf16[1,384,256]{2,1,0:T(8,128)(2,1)}, u32[]{:S(2)}) copy-start(bf16[1,384,256]{2,1,0:T(8,128)(2,1)} %param.8) | copy-start | bytes 589828
  8.7 0.7 copy-start.7
  13.2 18.1 %copy-start.5 = (bf16[1,384,256]{2,1,0:T(8,128)(2,1)S(1)}, bf16[1,384,256]{2,1,0:T(8,128)(2,1)}, u32[]{:S(2)}) copy-start(bf16[1,384,256]{2,1,0:T(8,128)(2,1)} %param.10) | copy-start | bytes 589828
  13.4 4.0 %collective-permute-start.4 = (bf16[4,400,256]{2,1,0:T(8,128)(2,1)S(1)}, bf16[4,400,256]{2,1,0:T(8,128)(2,1)S(1)}, u32[]{:S(2)}, u32[]{:S(2)}) collective-permute-start(bf16[4,400,256]{2,1,0:T(8,128)(2,1)S(1)} %pad_maximum_fusion.mine_ref), channel_id=1, source_target_pairs={{0,1},{1,0},{2,3},{3,2},{4,5},{5,4},{6,7},{7,6},{8,9},{9,8},{10,11... | collective-permute-start | bytes 2457608 | tf_op jit(solution)/shard_map/ppermute | solution.py:347
  13.5 11.3 %collective-permute-start = (bf16[400,256]{1,0:T(8,128)(2,1)S(1)}, bf16[400,256]{1,0:T(8,128)(2,1)S(1)}, u32[]{:S(2)}, u32[]{:S(2)}) collective-permute-start(bf16[400,256]{1,0:T(8,128)(2,1)S(1)} %pack_bwd.1), channel_id=1, source_target_pairs={{0,12},{1,13},{2,14},{3,15},{4,8},{5,9},{6,10},{7,11},{8,4},{9,5},... | collective-permute-start | bytes 614408 | tf_op jit(solution)/shard_map/ppermute | solution.py:343
  15.4 11.5 %collective-permute-start.11 = (bf16[400,256]{1,0:T(8,128)(2,1)S(1)}, bf16[400,256]{1,0:T(8,128)(2,1)S(1)}, u32[]{:S(2)}, u32[]{:S(2)}) collective-permute-start(bf16[400,256]{1,0:T(8,128)(2,1)S(1)} %collective-permute-done.1), channel_id=1, source_target_pairs={{0,6},{1,7},{2,4},{3,5},{4,2},{5,3},{6,0},{7,1},{8,14},{9,15},{10,... | collective-permute-start | bytes 614408 | tf_op jit(solution)/shard_map/ppermute | solution.py:343
  16.6 10.4 %collective-permute-start.10 = (bf16[400,256]{1,0:T(8,128)(2,1)S(1)}, bf16[400,256]{1,0:T(8,128)(2,1)S(1)}, u32[]{:S(2)}, u32[]{:S(2)}) collective-permute-start(bf16[400,256]{1,0:T(8,128)(2,1)S(1)} %collective-permute-done.2), channel_id=1, source_target_pairs={{0,8},{1,9},{2,10},{3,11},{4,12},{5,13},{6,14},{7,15},{8,0},{9,1},... | collective-permute-start | bytes 614408 | tf_op jit(solution)/shard_map/ppermute | solution.py:343
  17.3 10.3 %collective-permute-start.9 = (bf16[400,256]{1,0:T(8,128)(2,1)S(1)}, bf16[400,256]{1,0:T(8,128)(2,1)S(1)}, u32[]{:S(2)}, u32[]{:S(2)}) collective-permute-start(bf16[400,256]{1,0:T(8,128)(2,1)S(1)} %collective-permute-done.3), channel_id=1, source_target_pairs={{0,2},{1,3},{2,0},{3,1},{4,6},{5,7},{6,4},{7,5},{8,10},{9,11},{10,... | collective-permute-start | bytes 614408 | tf_op jit(solution)/shard_map/ppermute | solution.py:343
  20.1 2.8 %copy-start = (bf16[1,4096,3,256]{3,1,2,0:T(8,128)(2,1)S(1)}, bf16[1,4096,3,256]{3,1,2,0:T(8,128)(2,1)}, u32[]{:S(2)}) copy-start(bf16[1,4096,3,256]{3,1,2,0:T(8,128)(2,1)} %param.11) | copy-start | bytes 18874372
  27.8 3.6 %collective-permute-start.12 = (bf16[4,400,256]{2,1,0:T(8,128)(2,1)S(1)}, bf16[4,400,256]{2,1,0:T(8,128)(2,1)S(1)}, u32[]{:S(2)}, u32[]{:S(2)}) collective-permute-start(bf16[4,400,256]{2,1,0:T(8,128)(2,1)S(1)} %pad_maximum_fusion.1.mine_ref.more_ref), channel_id=1, source_target_pairs={{0,1},{1,0},{2,3},{3,2},{4,5},{5,4},{6,7},{7,6},{8,9},{9,8},{10,11... | collective-permute-start | bytes 2457608 | tf_op jit(solution)/shard_map/ppermute | solution.py:347
  27.9 8.0 %collective-permute-start.8 = (bf16[400,256]{1,0:T(8,128)(2,1)S(1)}, bf16[400,256]{1,0:T(8,128)(2,1)S(1)}, u32[]{:S(2)}, u32[]{:S(2)}) collective-permute-start(bf16[400,256]{1,0:T(8,128)(2,1)S(1)} %pack_fwd.1), channel_id=1, source_target_pairs={{0,6},{1,7},{2,4},{3,5},{4,2},{5,3},{6,0},{7,1},{8,14},{9,15},{10,... | collective-permute-start | bytes 614408 | tf_op jit(solution)/shard_map/ppermute | solution.py:343
  28.6 7.3 %collective-permute-start.7 = (bf16[400,256]{1,0:T(8,128)(2,1)S(1)}, bf16[400,256]{1,0:T(8,128)(2,1)S(1)}, u32[]{:S(2)}, u32[]{:S(2)}) collective-permute-start(bf16[400,256]{1,0:T(8,128)(2,1)S(1)} %pack_fwd.1), channel_id=1, source_target_pairs={{0,2},{1,3},{2,0},{3,1},{4,6},{5,7},{6,4},{7,5},{8,10},{9,11},{10,... | collective-permute-start | bytes 614408 | tf_op jit(solution)/shard_map/ppermute | solution.py:343
  30.3 6.9 %collective-permute-start.6 = (bf16[400,256]{1,0:T(8,128)(2,1)S(1)}, bf16[400,256]{1,0:T(8,128)(2,1)S(1)}, u32[]{:S(2)}, u32[]{:S(2)}) collective-permute-start(bf16[400,256]{1,0:T(8,128)(2,1)S(1)} %pack_fwd.1), channel_id=1, source_target_pairs={{0,8},{1,9},{2,10},{3,11},{4,12},{5,13},{6,14},{7,15},{8,0},{9,1},... | collective-permute-start | bytes 614408 | tf_op jit(solution)/shard_map/ppermute | solution.py:343
  37.1 5.6 %collective-permute-start.17 = (bf16[400,768]{1,0:T(8,128)(2,1)S(1)}, bf16[400,768]{1,0:T(8,128)(2,1)S(1)}, u32[]{:S(2)}, u32[]{:S(2)}) collective-permute-start(bf16[400,768]{1,0:T(8,128)(2,1)S(1)} %get-tuple-element.80.mine_ref.g_ref), channel_id=1, source_target_pairs={{0,1},{1,0},{2,3},{3,2},{4,5},{5,4},{6,7},{7,6},{8,9},{9,8},{10,11... | collective-permute-start | bytes 1843208 | tf_op jit(solution)/shard_map/ppermute | solution.py:347
  37.1 14.0 %collective-permute-start.13 = (bf16[400,256]{1,0:T(8,128)(2,1)S(1)}, bf16[400,256]{1,0:T(8,128)(2,1)S(1)}, u32[]{:S(2)}, u32[]{:S(2)}) collective-permute-start(bf16[400,256]{1,0:T(8,128)(2,1)S(1)} %collective-permute-done.8), channel_id=1, source_target_pairs={{0,2},{1,3},{2,0},{3,1},{4,6},{5,7},{6,4},{7,5},{8,10},{9,11},{10,... | collective-permute-start | bytes 614408 | tf_op jit(solution)/shard_map/ppermute | solution.py:343
  37.5 13.6 %collective-permute-start.14 = (bf16[400,256]{1,0:T(8,128)(2,1)S(1)}, bf16[400,256]{1,0:T(8,128)(2,1)S(1)}, u32[]{:S(2)}, u32[]{:S(2)}) collective-permute-start(bf16[400,256]{1,0:T(8,128)(2,1)S(1)} %collective-permute-done.7), channel_id=1, source_target_pairs={{0,8},{1,9},{2,10},{3,11},{4,12},{5,13},{6,14},{7,15},{8,0},{9,1},... | collective-permute-start | bytes 614408 | tf_op jit(solution)/shard_map/ppermute | solution.py:343
  39.0 12.1 %collective-permute-start.15 = (bf16[400,256]{1,0:T(8,128)(2,1)S(1)}, bf16[400,256]{1,0:T(8,128)(2,1)S(1)}, u32[]{:S(2)}, u32[]{:S(2)}) collective-permute-start(bf16[400,256]{1,0:T(8,128)(2,1)S(1)} %collective-permute-done.6), channel_id=1, source_target_pairs={{0,6},{1,7},{2,4},{3,5},{4,2},{5,3},{6,0},{7,1},{8,14},{9,15},{10,... | collective-permute-start | bytes 614408 | tf_op jit(solution)/shard_map/ppermute | solution.py:343
  39.6 11.6 %collective-permute-start.16 = (bf16[400,256]{1,0:T(8,128)(2,1)S(1)}, bf16[400,256]{1,0:T(8,128)(2,1)S(1)}, u32[]{:S(2)}, u32[]{:S(2)}) collective-permute-start(bf16[400,256]{1,0:T(8,128)(2,1)S(1)} %pack_fwd.1), channel_id=1, source_target_pairs={{0,12},{1,13},{2,14},{3,15},{4,8},{5,9},{6,10},{7,11},{8,4},{9,5},... | collective-permute-start | bytes 614408 | tf_op jit(solution)/shard_map/ppermute | solution.py:343
  51.3 13.5 %collective-permute-start.18 = (bf16[4,400,256]{2,1,0:T(8,128)(2,1)S(1)}, bf16[4,400,256]{2,1,0:T(8,128)(2,1)S(1)}, u32[]{:S(2)}, u32[]{:S(2)}) collective-permute-start(bf16[4,400,256]{2,1,0:T(8,128)(2,1)S(1)} %pad_maximum_fusion.2.mine_ref), channel_id=1, source_target_pairs={{0,1},{1,0},{2,3},{3,2},{4,5},{5,4},{6,7},{7,6},{8,9},{9,8},{10,11... | collective-permute-start | bytes 2457608 | tf_op jit(solution)/shard_map/ppermute | solution.py:347
  51.4 9.6 %collective-permute-start.21 = (bf16[400,256]{1,0:T(8,128)(2,1)S(1)}, bf16[400,256]{1,0:T(8,128)(2,1)S(1)}, u32[]{:S(2)}, u32[]{:S(2)}) collective-permute-start(bf16[400,256]{1,0:T(8,128)(2,1)S(1)} %get-tuple-element.97), channel_id=1, source_target_pairs={{0,6},{1,7},{2,4},{3,5},{4,2},{5,3},{6,0},{7,1},{8,14},{9,15},{10,... | collective-permute-start | bytes 614408 | tf_op jit(solution)/shard_map/ppermute | solution.py:343
  52.4 8.6 %collective-permute-start.22 = (bf16[400,256]{1,0:T(8,128)(2,1)S(1)}, bf16[400,256]{1,0:T(8,128)(2,1)S(1)}, u32[]{:S(2)}, u32[]{:S(2)}) collective-permute-start(bf16[400,256]{1,0:T(8,128)(2,1)S(1)} %get-tuple-element.98), channel_id=1, source_target_pairs={{0,8},{1,9},{2,10},{3,11},{4,12},{5,13},{6,14},{7,15},{8,0},{9,1},... | collective-permute-start | bytes 614408 | tf_op jit(solution)/shard_map/ppermute | solution.py:343
  53.7 7.3 %collective-permute-start.23 = (bf16[400,256]{1,0:T(8,128)(2,1)S(1)}, bf16[400,256]{1,0:T(8,128)(2,1)S(1)}, u32[]{:S(2)}, u32[]{:S(2)}) collective-permute-start(bf16[400,256]{1,0:T(8,128)(2,1)S(1)} %get-tuple-element.99), channel_id=1, source_target_pairs={{0,2},{1,3},{2,0},{3,1},{4,6},{5,7},{6,4},{7,5},{8,10},{9,11},{10,... | collective-permute-start | bytes 614408 | tf_op jit(solution)/shard_map/ppermute | solution.py:343
  55.6 11.3 %slice-start = ((s8[6291456]{0:T(1024)(128)(4,1)}), s8[4194304]{0:T(1024)(128)(4,1)S(1)}, s32[]{:S(2)}) async-start(s8[6291456]{0:T(1024)(128)(4,1)} %bitcast.36), calls=%async_computation | async-start | bytes 8388608
  55.7 11.2 %slice-start.1 = ((s8[6291456]{0:T(1024)(128)(4,1)}), s8[2097152]{0:T(1024)(128)(4,1)S(1)}, s32[]{:S(2)}) async-start(s8[6291456]{0:T(1024)(128)(4,1)} %bitcast.36), calls=%async_computation.1 | async-start | bytes 4194304
  55.7 13.1 %collective-permute-start.19 = (bf16[4,400,256]{2,1,0:T(8,128)(2,1)S(1)}, bf16[4,400,256]{2,1,0:T(8,128)(2,1)S(1)}, u32[]{:S(2)}, u32[]{:S(2)}) collective-permute-start(bf16[4,400,256]{2,1,0:T(8,128)(2,1)S(1)} %pad_maximum_fusion.3.mine_ref), channel_id=1, source_target_pairs={{0,1},{1,0},{2,3},{3,2},{4,5},{5,4},{6,7},{7,6},{8,9},{9,8},{10,11... | collective-permute-start | bytes 2457608 | tf_op jit(solution)/shard_map/ppermute | solution.py:347
  61.0 7.8 %copy-start.2 = (bf16[1,384,256]{2,1,0:T(8,128)(2,1)S(1)}, bf16[1,384,256]{2,1,0:T(8,128)(2,1)}, u32[]{:S(2)}) copy-start(bf16[1,384,256]{2,1,0:T(8,128)(2,1)} %param.8) | copy-start | bytes 589828
  61.2 15.0 %collective-permute-start.24 = (bf16[400,256]{1,0:T(8,128)(2,1)S(1)}, bf16[400,256]{1,0:T(8,128)(2,1)S(1)}, u32[]{:S(2)}, u32[]{:S(2)}) collective-permute-start(bf16[400,256]{1,0:T(8,128)(2,1)S(1)} %get-tuple-element.104), channel_id=1, source_target_pairs={{0,8},{1,9},{2,10},{3,11},{4,12},{5,13},{6,14},{7,15},{8,0},{9,1},... | collective-permute-start | bytes 614408 | tf_op jit(solution)/shard_map/ppermute | solution.py:343
  62.5 13.7 %collective-permute-start.25 = (bf16[400,256]{1,0:T(8,128)(2,1)S(1)}, bf16[400,256]{1,0:T(8,128)(2,1)S(1)}, u32[]{:S(2)}, u32[]{:S(2)}) collective-permute-start(bf16[400,256]{1,0:T(8,128)(2,1)S(1)} %get-tuple-element.105), channel_id=1, source_target_pairs={{0,2},{1,3},{2,0},{3,1},{4,6},{5,7},{6,4},{7,5},{8,10},{9,11},{10,... | collective-permute-start | bytes 614408 | tf_op jit(solution)/shard_map/ppermute | solution.py:343
  63.9 12.3 %collective-permute-start.26 = (bf16[400,256]{1,0:T(8,128)(2,1)S(1)}, bf16[400,256]{1,0:T(8,128)(2,1)S(1)}, u32[]{:S(2)}, u32[]{:S(2)}) collective-permute-start(bf16[400,256]{1,0:T(8,128)(2,1)S(1)} %get-tuple-element.106), channel_id=1, source_target_pairs={{0,6},{1,7},{2,4},{3,5},{4,2},{5,3},{6,0},{7,1},{8,14},{9,15},{10,... | collective-permute-start | bytes 614408 | tf_op jit(solution)/shard_map/ppermute | solution.py:343
  64.8 11.3 %collective-permute-start.27 = (bf16[400,256]{1,0:T(8,128)(2,1)S(1)}, bf16[400,256]{1,0:T(8,128)(2,1)S(1)}, u32[]{:S(2)}, u32[]{:S(2)}) collective-permute-start(bf16[400,256]{1,0:T(8,128)(2,1)S(1)} %get-tuple-element.107), channel_id=1, source_target_pairs={{0,12},{1,13},{2,14},{3,15},{4,8},{5,9},{6,10},{7,11},{8,4},{9,5},... | collective-permute-start | bytes 614408 | tf_op jit(solution)/shard_map/ppermute | solution.py:343
  68.8 7.4 %copy-start.4 = (bf16[1,384,256]{2,1,0:T(8,128)(2,1)S(1)}, bf16[1,384,256]{2,1,0:T(8,128)(2,1)}, u32[]{:S(2)}) copy-start(bf16[1,384,256]{2,1,0:T(8,128)(2,1)} %param.9) | copy-start | bytes 589828
  68.8 7.4 %copy-start.8 = (f32[1,256]{1,0:T(1,128)S(1)}, f32[1,256]{1,0:T(1,128)}, u32[]{:S(2)}) copy-start(f32[1,256]{1,0:T(1,128)} %refs_6_.1) | copy-start | bytes 3076
  73.3 12.7 %collective-permute-start.20 = (bf16[384,256]{1,0:T(8,128)(2,1)S(1)}, bf16[384,256]{1,0:T(8,128)(2,1)S(1)}, u32[]{:S(2)}, u32[]{:S(2)}) collective-permute-start(bf16[384,256]{1,0:T(8,128)(2,1)S(1)} %forward.1), channel_id=1, source_target_pairs={{240,0},{0,16},{16,32},{32,48},{48,64},{64,80},{80,96},{96,112},{1... | collective-permute-start | bytes 589832 | tf_op jit(solution)/shard_map/ppermute | solution.py:352
  77.0 11.6 %collective-permute-start.28 = (bf16[384,256]{1,0:T(8,128)(2,1)S(1)}, bf16[384,256]{1,0:T(8,128)(2,1)S(1)}, u32[]{:S(2)}, u32[]{:S(2)}) collective-permute-start(bf16[384,256]{1,0:T(8,128)(2,1)S(1)} %get-tuple-element.113), channel_id=1, source_target_pairs={{16,0},{32,16},{48,32},{64,48},{80,64},{96,80},{112,96},{128,112},... | collective-permute-start | bytes 589832 | tf_op jit(solution)/shard_map/ppermute | solution.py:352
